TPU v7x, 32 devices: a whole 2x2x4 slice. The times are simulated.
32 devices in a mesh: rows: 8 (over z, x), sub: 4 (over y, core).
Axes of the slice: x: 2, y: 2, z: 4, core: 2. Of those that a mesh axis runs over, the one named last changes fastest.
Arguments:
- queries: float32 [16384, 256], P(('rows', 'sub')), may hold values from -6 to 6
- row_scale: float32 [16384], P(('rows', 'sub')), may hold values from 0.6 to 1.6
- leaf_basis: float32 [16384, 128], P(('rows', 'sub')), may hold values from -6 to 6
- leaf_cores: float32 [8, 128, 128], P('rows'), as said below
- level_basis: float32 [3, 16384, 128], P(None, ('rows', 'sub')), may hold values from -6 to 6
- level_cores: float32 [14, 128, 128], replicated, as said below
Outputs:
- solution: float32 [16384, 256], P(('rows', 'sub'))
Inputs may be any that keep to these rules, and one draw needn't show every extreme that they name: `leaf_cores`: each core is divided by the rows of its block: every entry lies within 3 / (512 * 4) of zero. `level_cores`: each core is divided by the rows of its node: every entry of a level-l core lies within 3 * 2 ** l / 16384 of zero.
All inputs are finite; a program needn't handle non-finite values.
Results may differ from a plain program's by a relative error of at most 0.0001.
Values sent between devices are 32-bit elements; how exact they have to be, the bound alone decides.
No kernel may reach another device: no remote copies, remote signals or barrier semaphores. Data moves between devices by JAX's collectives and lax.ppermute only.
A program may use at most 64 MiB of HBM per device.

v0:
```python
import functools

import jax
import jax.numpy as jnp
from jax import lax
from jax.experimental import pallas as pl
from jax.experimental.pallas import tpu as pltpu
from jax.sharding import PartitionSpec as P


FLOAT = jnp.float32
VMEM_LIMIT = 16 << 20


def halves(value):
    high = value.astype(jnp.bfloat16)
    return high, (value - high.astype(FLOAT)).astype(jnp.bfloat16)


def dot_parts(left, right, right_dim=0):
    mult = functools.partial(
        lax.dot_general,
        dimension_numbers=(((1,), (right_dim,)), ((), ())),
        preferred_element_type=FLOAT,
    )
    return mult(left[0], right[0]) + (mult(left[0], right[1]) + mult(left[1], right[0]))


def dot(left, right, right_dim=0):
    return dot_parts(halves(left), halves(right), right_dim)


def lanes(values):
    return values[0] if len(values) == 1 else jnp.concatenate(values, axis=1)


def column_scale(scale):
    size = scale.shape[1]
    return jnp.concatenate(
        [jnp.broadcast_to(scale[i : i + 1, :], (size, size)).T for i in range(scale.shape[0])], axis=0
    )


def core_side():
    return lax.rem(lax.axis_index("sub"), 2)


def at(index, size):
    return pl.ds(pl.multiple_of(index * size, 8), size)


def call(body, outs, *operands, flops, spaces=None, out_space=pltpu.VMEM, scratch=()):
    spaces = spaces or [pltpu.VMEM] * len(operands)
    size = sum(a.dtype.itemsize * a.size for a in operands)
    outs = [out if isinstance(out, jax.ShapeDtypeStruct) else jax.ShapeDtypeStruct(out, FLOAT) for out in outs]
    return pl.pallas_call(
        body,
        out_shape=outs,
        in_specs=[pl.BlockSpec(memory_space=space) for space in spaces],
        out_specs=[pl.BlockSpec(memory_space=out_space)] * len(outs),
        scratch_shapes=list(scratch),
        compiler_params=pltpu.CompilerParams(vmem_limit_bytes=VMEM_LIMIT),
        cost_estimate=pl.CostEstimate(flops=flops, bytes_accessed=size, transcendentals=0),
    )(*operands)


def pair(*shape):
    return [jax.ShapeDtypeStruct(shape, jnp.bfloat16)] * 2


def store(refs, value):
    for ref, part in zip(refs, halves(value)):
        ref[...] = part


def swap(array, axis, bit):
    return lax.ppermute(array, axis, [(i, i ^ 1 << bit) for i in range(lax.axis_size(axis))])


def partial_sums(array, axis, bits):
    bits = list(bits)
    if not bits:
        return [array]
    for bit in bits[:-1]:
        array = array + swap(array, axis, bit)
    return [array, swap(array, axis, bits[-1])]


def add_all(parts):
    return functools.reduce(lambda a, b: a + b, parts)


def shards(queries, row_scale, leaf_basis, leaf_cores, level_basis, level_cores):
    levels = level_basis.shape[0]
    count = levels + 1
    top = levels
    rows_here, rank = leaf_basis.shape
    columns = queries.shape[1]
    groups, sub = lax.axis_size("rows"), lax.axis_size("sub")
    heights = [None] + [levels + 1 - e for e in range(1, count)]
    widths = [1] + [groups // 2 ** heights[e] for e in range(1, count)]
    head = sum(w == 1 for w in widths)
    bits = [range(0)] + [
        range(widths[e - 1].bit_length() - 1, widths[e].bit_length() - 1) for e in range(1, count)
    ]
    blocks = [list(range(e + 1, count)) for e in range(count)]
    coarse = count - head
    leaf_bits = range(1, sub.bit_length() - 1)
    mine = columns // 2
    half = rank // 2
    batches = 2
    batch = mine // batches
    small = 2 * 3 * rank**3

    scale = row_scale.reshape(-1, rank)
    starts = [sum(len(b) for b in blocks[:e]) * rank for e in range(count + 1)]

    def gram_body(*refs):
        scale_hbm, leaf_hbm, level_hbm, queries_hbm, leaf_core_hbm, core_hbm = refs[:6]
        out_ref, scale_ref, leaf_ref, level_ref, queries_ref, core_ref, sems = refs[6:]
        targets = [(scale_hbm, scale_ref), (leaf_hbm, leaf_ref)]
        targets += [(level_hbm.at[e], level_ref.at[e]) for e in reversed(range(levels))]
        place = lax.axis_index("rows")
        targets += [(queries_hbm, queries_ref), (leaf_core_hbm.at[0], core_ref.at[0])]
        for e in range(1, count):
            targets.append((core_hbm.at[2 ** heights[e] - 2 + place // widths[e]], core_ref.at[e]))
        copies = [pltpu.make_async_copy(a, b, sems.at[i]) for i, (a, b) in enumerate(targets)]
        for copy in copies:
            copy.start()
        for copy in copies[: 2 + levels]:
            copy.wait()
        vectors = [column_scale(scale_ref[...]) * leaf_ref[...]]
        vectors += [level_ref[levels - e] for e in range(1, count)]
        parts = [halves(v) for v in vectors]
        side = core_side()
        for e in range(count):
            group = ([e] if e >= head else []) + blocks[e]
            right = [lanes([parts[f][i] for f in group]) for i in range(2)]
            value = dot_parts(halves(vectors[e].T), right)
            for h in range(2):
                rows = value[h * half : (h + 1) * half]
                if e >= head:
                    place = starts[count] + (e - head) * rank
                    out_ref[at(h ^ side, half), place : place + rank] = rows[:, :rank]
                    rows = rows[:, rank:]
                if blocks[e]:
                    out_ref[at(h ^ side, half), starts[e] : starts[e + 1]] = rows
        for copy in copies[2 + levels :]:
            copy.wait()

    gram, scale, leaf_basis, level_basis, queries, cores = call(
        gram_body,
        [
            (rank, starts[count] + coarse * rank),
            *[array.shape for array in (scale, leaf_basis, level_basis, queries)],
            (count, rank, rank),
        ],
        *[
            pltpu.with_memory_space_constraint(array, pltpu.HBM)
            for array in (scale, leaf_basis, level_basis, queries, leaf_cores, level_cores)
        ],
        flops=small * (starts[count] // rank + coarse) * rows_here // rank,
        spaces=[pltpu.HBM] * 6,
        scratch=[pltpu.SemaphoreType.DMA((3 + levels + count,))],
    )
    gram_chip = gram[:half] + swap(gram[half:], "sub", 0)
    early = add_all(partial_sums(gram_chip[:, : starts[count]], "sub", leaf_bits))
    diagonal = []
    for e in reversed(range(head, count)):
        place = starts[count] + (e - head) * rank
        diagonal = lanes([gram_chip[:, place : place + rank], *diagonal])
        diagonal = [add_all(partial_sums(diagonal, "rows", bits[e]))]
    diagonal = diagonal[0]

    def moment_body(scale_ref, queries_ref, leaf_ref, level_ref, out_ref, *basis_refs):
        spread = column_scale(scale_ref[...])
        right = halves(lanes([leaf_ref[...]] + [spread * level_ref[levels - e] for e in range(1, count)]))
        for basis_ref, part in zip(basis_refs, right):
            basis_ref[...] = part
        value = dot_parts(halves(queries_ref[...].T), right)
        side = core_side()
        for h in range(2):
            out_ref[at(h ^ side, mine), :] = value[h * mine : (h + 1) * mine]

    value, *basis = call(
        moment_body,
        [(columns, count * rank), *pair(rows_here, count * rank)],
        scale,
        queries,
        leaf_basis,
        level_basis,
        flops=small * count * 2 * rows_here // rank,
    )
    moment_chip = value[:mine] + swap(value[mine:], "sub", 0)
    moment_parts = [partial_sums(moment_chip[b * batch : (b + 1) * batch], "sub", leaf_bits) for b in range(batches)]

    late_rows = columns // 2 + head * half

    def late_body(scale_ref, queries_ref, leaf_ref, level_ref, out_ref, *scaled_refs):
        spread = column_scale(scale_ref[...])
        vectors = spread * leaf_ref[...]
        side = core_side()
        scaled = halves(spread * vectors)
        for scaled_ref, part in zip(scaled_refs, scaled):
            scaled_ref[...] = part
        value = dot_parts(halves(queries_ref[...].T), scaled)
        for h in range(2):
            base = (h ^ side) * late_rows
            part = value[h * columns // 2 : (h + 1) * columns // 2]
            out_ref[pl.ds(pl.multiple_of(base, 8), columns // 2), :] = part
        for e in range(head):
            basis = vectors if e == 0 else level_ref[levels - e]
            value = dot(basis.T, basis)
            for h in range(2):
                base = (h ^ side) * late_rows + columns // 2 + e * half
                out_ref[pl.ds(pl.multiple_of(base, 8), half), :] = value[h * half : (h + 1) * half]

    late, *scaled = call(
        late_body,
        [(2 * late_rows, rank), *pair(rows_here, rank)],
        scale,
        queries,
        leaf_basis,
        level_basis,
        flops=small * (2 + head) * rows_here // rank,
    )
    late_chip = late[:late_rows] + swap(late[late_rows:], "sub", 0)

    def stacked(array, size):
        return [array[:, j : j + size] for j in range(0, array.shape[1], size)]

    late = jnp.concatenate([late_chip, *stacked(diagonal, rank)], axis=0)
    late_size = late.shape[0]
    late = add_all(partial_sums(late, "sub", leaf_bits))

    def product_body(group, own_ref, other_ref, core_ref, *refs):
        out_refs, stack_ref = refs[:-1], refs[-1]
        side = core_side()
        stack_ref[at(side, half), :] = own_ref[...]
        stack_ref[at(1 - side, half), :] = other_ref[...]
        base = starts[group[0]]
        for i, e in enumerate(group):
            block = stack_ref[:, starts[e] - base : starts[e + 1] - base]
            store(out_refs[2 * i : 2 * i + 2], dot(core_ref[e].T, block))

    def products(group, own):
        out = call(
            functools.partial(product_body, group),
            [part for e in group for part in pair(rank, starts[e + 1] - starts[e])],
            own,
            swap(own, "sub", 0),
            cores,
            flops=small * sum(len(blocks[e]) for e in group),
            scratch=[pltpu.VMEM((rank, own.shape[1]), FLOAT)],
        )
        return [out[2 * i : 2 * i + 2] for i in range(len(group))]

    factors = products(list(range(head)), early[:, : starts[head]])
    remaining = early[:, starts[head] :]
    for e in range(head, top):
        remaining = add_all(partial_sums(remaining, "rows", bits[e]))
        size = starts[e + 1] - starts[e]
        factors += products([e], remaining[:, :size])
        remaining = remaining[:, size:]

    def flat(group):
        return [part for factor in group for part in factor]

    def paired(refs):
        return [refs[i : i + 2] for i in range(0, len(refs), 2)]

    def take(factor, start, size):
        return [ref[:, start : start + size] for ref in factor]

    def head_body(number, *refs):
        part_refs, factor_refs, (own_ref, rest_ref) = refs[:number], paired(refs[number:-2]), refs[-2:]
        rest = add_all([part[...] for part in part_refs])
        for e in range(head):
            own, rest = rest[:, :rank], rest[:, rank:]
            own_ref[e * batch : (e + 1) * batch, :] = own
            rest = rest - dot_parts(halves(own), take(factor_refs[e], 0, rest.shape[1]))
        rest_ref[...] = rest

    def step_body(number, *refs):
        part_refs, factor, (own_ref, rest_ref) = refs[:number], refs[number:-2], refs[-2:]
        total = add_all([part[...] for part in part_refs])
        own, rest = total[:, :rank], total[:, rank:]
        own_ref[...] = own
        rest_ref[...] = rest - dot_parts(halves(own), take(factor, 0, rest.shape[1]))

    def scatter(parts, number, stack_ref):
        side = core_side()
        for b, part in enumerate(parts):
            for ref, place in zip(part, (side, 1 - side)):
                for e in range(number):
                    stack_ref[at(place * batches + b, batch), e * rank : (e + 1) * rank] = ref[
                        e * batch : (e + 1) * batch, :
                    ]

    head_moments, found_parts = [], []
    for b in range(batches):
        own, rest = call(
            functools.partial(head_body, len(moment_parts[b])),
            [(head * batch, rank), (batch, coarse * rank)],
            *moment_parts[b],
            *flat(factors[:head]),
            flops=small * sum(map(len, blocks[:head])) // batches,
        )
        head_moments.append(own)
        found = []
        for e in range(head, top):
            parts = partial_sums(rest, "rows", bits[e])
            own, rest = call(
                functools.partial(step_body, len(parts)),
                [(batch, rank), (batch, (top - e) * rank)],
                *parts,
                *factors[e],
                flops=small * (top - e) // batches,
            )
            found.append(own)
        found.append(add_all(partial_sums(rest, "rows", bits[top])))
        found = jnp.concatenate(found, axis=0)
        found_parts.append([found, swap(found, "sub", 0)])
    late = jnp.concatenate([late, *head_moments], axis=0)
    late_parts = [late, swap(late, "sub", 0)]

    def answer_body(*refs):
        factor_refs, basis_refs, out_refs = paired(refs[:-4]), refs[-4:-2], refs[-2:]
        rows = {}
        for f in reversed(range(count)):
            if f + 1 < count:
                stack = jnp.concatenate([rows[g] for g in range(f + 1, count)], axis=0)
                row = -dot_parts(take(factor_refs[f], 0, stack.shape[0]), halves(stack))
            else:
                row = jnp.zeros((rank, coarse * rank), FLOAT)
            if f >= head:
                line = lax.broadcasted_iota(jnp.int32, row.shape, 0) + (f - head) * rank
                row = row + jnp.where(line == lax.broadcasted_iota(jnp.int32, row.shape, 1), 1.0, 0.0)
            rows[f] = row
        gains = jnp.concatenate([rows[f] for f in range(count)], axis=0)
        store(out_refs, dot_parts([ref[...] for ref in basis_refs], halves(gains)))

    answer = call(
        answer_body,
        pair(rows_here, coarse * rank),
        *flat(factors),
        *basis,
        flops=small * coarse * count * rows_here // rank,
    )

    def base_body(scale_ref, queries_ref, own_ref, other_ref, core_ref, *refs):
        factor_refs, basis_refs, scaled_refs = paired(refs[: 2 * head]), refs[2 * head : -7], refs[-7:-5]
        out_ref, *gain_refs, stack_ref, gram_ref = refs[-5:]
        pieces = [pl.ds(late_size + b * head * batch, head * batch) for b in range(batches)]
        scatter([(own_ref.at[piece], other_ref.at[piece]) for piece in pieces], head, stack_ref)
        side = core_side()
        for late_ref, place in ((own_ref, side), (other_ref, 1 - side)):
            stack_ref[at(place, columns // 2), head * rank :] = late_ref[: columns // 2]
            for e in range(count):
                start = columns // 2 + e * half
                gram_ref[at(place, half), e * rank : (e + 1) * rank] = late_ref[start : start + half]
        products = [dot(core_ref[e].T, gram_ref[:, e * rank : (e + 1) * rank]) for e in range(count)]
        gains = [core_ref[e] + core_ref[e].T - dot(products[e], core_ref[e]) for e in range(1, count)]
        store(gain_refs, lanes(gains[head - 1 :]))
        moments = [stack_ref[:, e * rank : (e + 1) * rank] for e in range(head)]
        first = dot(moments[0], core_ref[0], 1)
        found = [dot(stack_ref[:, head * rank :], core_ref[0]) - dot(first, products[0], 1)]
        found += [dot(moments[e], gains[e - 1], 1) for e in range(1, head)]
        for e in reversed(range(head - 1)):
            size = (head - 1 - e) * rank
            found[e] = found[e] - dot_parts(halves(lanes(found[e + 1 :])), take(factor_refs[e], 0, size), 1)
        left = [lanes([a[...], b[:, : head * rank]]) for a, b in zip(scaled_refs, basis_refs)]
        square = column_scale(scale_ref[...] * scale_ref[...])
        square = lanes([square] * (columns // rank))
        out_ref[...] = square * queries_ref[...] - dot_parts(left, halves(lanes([first, *found])), 1)

    base, *gains = call(
        base_body,
        [(rows_here, columns), *pair(rank, coarse * rank)],
        scale,
        queries,
        *late_parts,
        cores,
        *flat(factors[:head]),
        *basis,
        *scaled,
        flops=small * 2 * (head + 1) * rows_here // rank,
        scratch=[pltpu.VMEM((columns, (head + 1) * rank), FLOAT), pltpu.VMEM((rank, count * rank), FLOAT)],
    )

    def last_body(base_ref, high_ref, low_ref, *refs):
        gain_refs, part_refs, (out_ref, stack_ref) = refs[:2], paired(refs[2:-2]), refs[-2:]
        scatter(part_refs, coarse, stack_ref)
        right = []
        for e in range(coarse):
            where = slice(e * rank, (e + 1) * rank)
            right.append(dot_parts(halves(stack_ref[:, where]), [ref[:, where] for ref in gain_refs], 1))
        out_ref[...] = base_ref[...] - dot_parts([high_ref[...], low_ref[...]], halves(lanes(right)), 1)

    (out,) = call(
        last_body,
        [(rows_here, columns)],
        base,
        *answer,
        *gains,
        *flat(found_parts),
        flops=small * 2 * coarse * rows_here // rank,
        scratch=[pltpu.VMEM((columns, coarse * rank), FLOAT)],
    )
    return out


def solution(mesh):
    in_specs = (
        P(("rows", "sub"), None),
        P(("rows", "sub")),
        P(("rows", "sub"), None),
        P("rows", None, None),
        P(None, ("rows", "sub"), None),
        P(),
    )
    out_specs = P(("rows", "sub"), None)

    return jax.shard_map(shards, mesh=mesh, in_specs=in_specs, out_specs=out_specs, check_vma=False)
```

profile of v0, /device:TPU:0, one launch (start us, length us, event | category | flops | bytes accessed | tf_op | source)
XLA Modules:
  0.0 40.3 jit_solution(17476112107814633357)
XLA Ops:
  0.0 2.1 %shard_map.64 = (f32[128,1024]{1,0:T(8,128)S(1)}, f32[4,128]{1,0:T(4,128)S(1)}, f32[512,128]{1,0:T(8,128)S(1)}, f32[3,512,128]{2,1,0:T(8,128)S(1)}, f32[512,256]{1,0:T(8,128)S(1)}, /*index=5*/f32[4,128,128]{2,1,0:T(8,128)S(1)}) custom-call(f32[4,128]{1,0:T(4,128)} %bitcast.1, f32[512,128]{1,0:T(8,128)} %refs_1_.1, f32[3,512,128]{2,1,0:T(8,128)} %refs_2_.1, ...), custom_call_target="tpu_custom_call" | custom-call | flops 402653184 | bytes 2557952 | tf_op jit(solution)/shard_map/pallas_call | solution.py:56
  2.1 0.8 %shard_map.65 = (f32[512,128]{1,0:T(8,128)S(1)}, bf16[512,128]{1,0:T(8,128)(2,1)S(1)}, bf16[512,128]{1,0:T(8,128)(2,1)S(1)}) custom-call(f32[4,128]{1,0:T(4,128)S(1)} %get-tuple-element.36.scale_ref, f32[512,256]{1,0:T(8,128)S(1)} %get-tuple-element.37.queries_ref, f32[512,128]{1,0:T(8,128)S(1)} %get-tuple-element.38.leaf_ref, ...), custom_call_target="tpu_custom_call" | custom-call | flops 201326592 | bytes 1574912 | tf_op jit(solution)/shard_map/pallas_call | solution.py:56
  2.9 0.6 %collective-permute-start = (f32[256,128]{1,0:T(8,128)S(1)}, f32[256,128]{1,0:T(8,128)S(1)}, u32[]{:S(2)}, u32[]{:S(2)}) collective-permute-start(f32[256,128]{1,0:T(8,128)S(1)} %slice.46), channel_id=1, source_target_pairs={{0,1},{1,0},{2,3},{3,2},{4,5},{5,4},{6,7},{7,6},{8,9},{9,8},{10,11... | collective-permute-start | bytes 393224 | tf_op jit(solution)/shard_map/ppermute | solution.py:77
  3.5 0.1 collective-permute-start.1
  3.6 0.8 %shard_map.66 = (f32[256,512]{1,0:T(8,128)S(1)}, bf16[512,512]{1,0:T(8,128)(2,1)S(1)}, bf16[512,512]{1,0:T(8,128)(2,1)S(1)}) custom-call(f32[4,128]{1,0:T(4,128)S(1)} %get-tuple-element.36.scale_ref, f32[512,256]{1,0:T(8,128)S(1)} %get-tuple-element.37.queries_ref, f32[512,128]{1,0:T(8,128)S(1)} %get-tuple-element.38.leaf_ref, ...), custom_call_target="tpu_custom_call" | custom-call | flops 402653184 | bytes 1574912 | tf_op jit(solution)/shard_map/pallas_call | solution.py:56
  4.4 0.6 %collective-permute-start.5 = (f32[128,512]{1,0:T(8,128)S(1)}, f32[128,512]{1,0:T(8,128)S(1)}, u32[]{:S(2)}, u32[]{:S(2)}) collective-permute-start(f32[128,512]{1,0:T(8,128)S(1)} %slice.54), channel_id=1, source_target_pairs={{0,1},{1,0},{2,3},{3,2},{4,5},{5,4},{6,7},{7,6},{8,9},{9,8},{10,11... | collective-permute-start | bytes 786440 | tf_op jit(solution)/shard_map/ppermute | solution.py:77
  4.9 0.0 collective-permute-done
  5.0 0.1 collective-permute-done.1
  5.2 2.8 %collective-permute-start.2 = (f32[64,128]{1,0:T(8,128)S(1)}, f32[64,128]{1,0:T(8,128)S(1)}, u32[]{:S(2)}, u32[]{:S(2)}) collective-permute-start(f32[64,128]{1,0:T(8,128)S(1)} %slice.61), channel_id=1, source_target_pairs={{0,8},{4,12},{8,0},{12,4},{16,24},{20,28},{24,16},{28,20},{1,9},{5... | collective-permute-start | bytes 98312 | tf_op jit(solution)/shard_map/ppermute | solution.py:77
  7.9 1.5 %collective-permute-start.7 = (f32[64,768]{1,0:T(8,128)S(1)}, f32[64,768]{1,0:T(8,128)S(1)}, u32[]{:S(2)}, u32[]{:S(2)}) collective-permute-start(f32[64,768]{1,0:T(8,128)S(1)} %slice.65), channel_id=1, source_target_pairs={{0,2},{1,3},{2,0},{3,1},{4,6},{5,7},{6,4},{7,5},{8,10},{9,11},{10,... | collective-permute-start | bytes 589832 | tf_op jit(solution)/shard_map/ppermute | solution.py:77
  9.4 0.0 collective-permute-done.5
  9.5 0.4 collective-permute-done.2
  9.9 2.0 %collective-permute-start.3 = (f32[64,256]{1,0:T(8,128)S(1)}, f32[64,256]{1,0:T(8,128)S(1)}, u32[]{:S(2)}, u32[]{:S(2)}) collective-permute-start(f32[64,256]{1,0:T(8,128)S(1)} %pad_maximum_fusion.2), channel_id=1, source_target_pairs={{0,4},{4,0},{8,12},{12,8},{16,20},{20,16},{24,28},{28,24},{1,5},{5... | collective-permute-start | bytes 196616 | tf_op jit(solution)/shard_map/ppermute | solution.py:77
  11.9 1.6 %collective-permute-start.6 = (f32[64,512]{1,0:T(8,128)S(1)}, f32[64,512]{1,0:T(8,128)S(1)}, u32[]{:S(2)}, u32[]{:S(2)}) collective-permute-start(f32[64,512]{1,0:T(8,128)S(1)} %get-tuple-element.69.refs_0_), channel_id=1, source_target_pairs={{0,2},{1,3},{2,0},{3,1},{4,6},{5,7},{6,4},{7,5},{8,10},{9,11},{10,... | collective-permute-start | bytes 393224 | tf_op jit(solution)/shard_map/ppermute | solution.py:77
  13.4 0.5 %collective-permute-start.9 = (f32[64,512]{1,0:T(8,128)S(1)}, f32[64,512]{1,0:T(8,128)S(1)}, u32[]{:S(2)}, u32[]{:S(2)}) collective-permute-start(f32[64,512]{1,0:T(8,128)S(1)} %get-tuple-element.70.refs_0_), channel_id=1, source_target_pairs={{0,2},{1,3},{2,0},{3,1},{4,6},{5,7},{6,4},{7,5},{8,10},{9,11},{10,... | collective-permute-start | bytes 393224 | tf_op jit(solution)/shard_map/ppermute | solution.py:77
  14.0 0.3 collective-permute-done.3
  14.2 1.5 %collective-permute-done.7 = f32[64,768]{1,0:T(8,128)S(1)} collective-permute-done((f32[64,768]{1,0:T(8,128)S(1)}, f32[64,768]{1,0:T(8,128)S(1)}, u32[]{:S(2)}, u32[]{:S(2)}) %collective-permute-start.7) | collective-permute-done | bytes 196640 | tf_op jit(solution)/shard_map/ppermute | solution.py:77
  15.7 1.6 %collective-permute-start.11 = (f32[64,128]{1,0:T(8,128)S(1)}, f32[64,128]{1,0:T(8,128)S(1)}, u32[]{:S(2)}, u32[]{:S(2)}) collective-permute-start(f32[64,128]{1,0:T(8,128)S(1)} %slice.68), channel_id=1, source_target_pairs={{0,4},{4,0},{8,12},{12,8},{16,20},{20,16},{24,28},{28,24},{1,5},{5... | collective-permute-start | bytes 98312 | tf_op jit(solution)/shard_map/ppermute | solution.py:77
  17.3 1.6 %collective-permute-start.4 = (f32[384,128]{1,0:T(8,128)S(1)}, f32[384,128]{1,0:T(8,128)S(1)}, u32[]{:S(2)}, u32[]{:S(2)}) collective-permute-start(f32[384,128]{1,0:T(8,128)S(1)} %pad_maximum_fusion.1), channel_id=1, source_target_pairs={{0,2},{1,3},{2,0},{3,1},{4,6},{5,7},{6,4},{7,5},{8,10},{9,11},{10,... | collective-permute-start | bytes 589832 | tf_op jit(solution)/shard_map/ppermute | solution.py:77
  18.9 0.1 collective-permute-start.8
  19.0 0.7 %collective-permute-done.11 = f32[64,128]{1,0:T(8,128)S(1)} collective-permute-done((f32[64,128]{1,0:T(8,128)S(1)}, f32[64,128]{1,0:T(8,128)S(1)}, u32[]{:S(2)}, u32[]{:S(2)}) %collective-permute-start.11) | collective-permute-done | bytes 32800 | tf_op jit(solution)/shard_map/ppermute | solution.py:77
  19.7 0.0 collective-permute-start.12
  19.7 4.9 %collective-permute-done.4 = f32[384,128]{1,0:T(8,128)S(1)} collective-permute-done((f32[384,128]{1,0:T(8,128)S(1)}, f32[384,128]{1,0:T(8,128)S(1)}, u32[]{:S(2)}, u32[]{:S(2)}) %collective-permute-start.4) | collective-permute-done | bytes 196640 | tf_op jit(solution)/shard_map/ppermute | solution.py:77
  24.7 0.0 collective-permute-done.8.other_ref
  24.7 0.4 shard_map.67
  25.1 0.0 collective-permute-done.6.refs_1_
  25.1 0.4 shard_map.68
  25.4 1.6 %collective-permute-start.13 = (f32[64,256]{1,0:T(8,128)S(1)}, f32[64,256]{1,0:T(8,128)S(1)}, u32[]{:S(2)}, u32[]{:S(2)}) collective-permute-start(f32[64,256]{1,0:T(8,128)S(1)} %get-tuple-element.61.refs_0_), channel_id=1, source_target_pairs={{0,4},{4,0},{8,12},{12,8},{16,20},{20,16},{24,28},{28,24},{1,5},{5... | collective-permute-start | bytes 196616 | tf_op jit(solution)/shard_map/ppermute | solution.py:77
  27.0 0.0 collective-permute-done.9.refs_1_
  27.0 0.3 shard_map.69
  27.4 0.6 %collective-permute-start.16 = (f32[64,256]{1,0:T(8,128)S(1)}, f32[64,256]{1,0:T(8,128)S(1)}, u32[]{:S(2)}, u32[]{:S(2)}) collective-permute-start(f32[64,256]{1,0:T(8,128)S(1)} %get-tuple-element.64.refs_0_), channel_id=1, source_target_pairs={{0,4},{4,0},{8,12},{12,8},{16,20},{20,16},{24,28},{28,24},{1,5},{5... | collective-permute-start | bytes 196616 | tf_op jit(solution)/shard_map/ppermute | solution.py:77
  28.0 0.1 collective-permute-start.10
  28.1 0.0 collective-permute-done.12.other_ref
  28.1 0.2 shard_map.71
  28.3 2.1 %collective-permute-done.13.refs_1_ = f32[64,256]{1,0:T(8,128)S(1)} collective-permute-done((f32[64,256]{1,0:T(8,128)S(1)}, f32[64,256]{1,0:T(8,128)S(1)}, u32[]{:S(2)}, u32[]{:S(2)}) %collective-permute-start.13) | collective-permute-done | bytes 65568 | tf_op jit(solution)/shard_map/ppermute | solution.py:77
  30.4 0.1 shard_map.73
  30.5 0.5 %collective-permute-start.14 = (f32[64,128]{1,0:T(8,128)S(1)}, f32[64,128]{1,0:T(8,128)S(1)}, u32[]{:S(2)}, u32[]{:S(2)}) collective-permute-start(f32[64,128]{1,0:T(8,128)S(1)} %get-tuple-element.63), channel_id=1, source_target_pairs={{0,8},{4,12},{8,0},{12,4},{16,24},{20,28},{24,16},{28,20},{1,9},{5... | collective-permute-start | bytes 98312 | tf_op jit(solution)/shard_map/ppermute | solution.py:77
  31.0 0.7 %collective-permute-done.16.refs_1_ = f32[64,256]{1,0:T(8,128)S(1)} collective-permute-done((f32[64,256]{1,0:T(8,128)S(1)}, f32[64,256]{1,0:T(8,128)S(1)}, u32[]{:S(2)}, u32[]{:S(2)}) %collective-permute-start.16) | collective-permute-done | bytes 65568 | tf_op jit(solution)/shard_map/ppermute | solution.py:77
  31.7 0.1 shard_map.74
  31.8 1.0 %collective-permute-start.17 = (f32[64,128]{1,0:T(8,128)S(1)}, f32[64,128]{1,0:T(8,128)S(1)}, u32[]{:S(2)}, u32[]{:S(2)}) collective-permute-start(f32[64,128]{1,0:T(8,128)S(1)} %get-tuple-element.66), channel_id=1, source_target_pairs={{0,8},{4,12},{8,0},{12,4},{16,24},{20,28},{24,16},{28,20},{1,9},{5... | collective-permute-start | bytes 98312 | tf_op jit(solution)/shard_map/ppermute | solution.py:77
  32.8 1.7 %collective-permute-done.14 = f32[64,128]{1,0:T(8,128)S(1)} collective-permute-done((f32[64,128]{1,0:T(8,128)S(1)}, f32[64,128]{1,0:T(8,128)S(1)}, u32[]{:S(2)}, u32[]{:S(2)}) %collective-permute-start.14) | collective-permute-done | bytes 32800 | tf_op jit(solution)/shard_map/ppermute | solution.py:77
  34.5 0.1 collective-permute-start.15
  34.6 1.2 %collective-permute-done.17 = f32[64,128]{1,0:T(8,128)S(1)} collective-permute-done((f32[64,128]{1,0:T(8,128)S(1)}, f32[64,128]{1,0:T(8,128)S(1)}, u32[]{:S(2)}, u32[]{:S(2)}) %collective-permute-start.17) | collective-permute-done | bytes 32800 | tf_op jit(solution)/shard_map/ppermute | solution.py:77
  35.8 0.1 collective-permute-start.18
  35.9 1.5 %shard_map.72 = (bf16[512,256]{1,0:T(8,128)(2,1)S(1)}, bf16[512,256]{1,0:T(8,128)(2,1)S(1)}) custom-call(bf16[128,384]{1,0:T(8,128)(2,1)S(1)} %get-tuple-element.44.refs_2_.refs_0_, bf16[128,384]{1,0:T(8,128)(2,1)S(1)} %get-tuple-element.45.refs_3_.refs_1_, bf16[128,256]{1,0:T(8,128)(2,1)S(1)} %get-tuple-element.46.refs_4_.refs_2_, ...), custom_call_target="tpu_custom_call" | custom-call | flops 402653184 | bytes 1441792 | tf_op jit(solution)/shard_map/pallas_call | solution.py:56
  37.4 0.0 collective-permute-done.10.other_ref
  37.4 1.5 %shard_map.70 = (f32[512,256]{1,0:T(8,128)S(1)}, bf16[128,256]{1,0:T(8,128)(2,1)S(1)}, bf16[128,256]{1,0:T(8,128)(2,1)S(1)}) custom-call(f32[4,128]{1,0:T(4,128)S(1)} %get-tuple-element.36.scale_ref, f32[512,256]{1,0:T(8,128)S(1)} %get-tuple-element.37.queries_ref, f32[640,128]{1,0:T(8,128)S(1)} %pad_maximum_fusion.own_ref, ...), custom_call_target="tpu_custom_call" | custom-call | flops 301989888 | bytes 3082240 | tf_op jit(solution)/shard_map/pallas_call | solution.py:56
  38.9 0.0 collective-permute-done.15.refs_3_
  38.9 0.0 collective-permute-done.18.refs_5_
  38.9 1.4 %shard_map.75 = f32[512,256]{1,0:T(8,128)} custom-call(f32[512,256]{1,0:T(8,128)S(1)} %get-tuple-element.54.base_ref, bf16[512,256]{1,0:T(8,128)(2,1)S(1)} %get-tuple-element.57.high_ref, bf16[512,256]{1,0:T(8,128)(2,1)S(1)} %get-tuple-element.58.low_ref, bf16[128,256]{1,0:T(8,128)(2,1)S(1)} %get-tuple-element.59.refs_0_, ...), custom_call_target="tpu_custom_call" | custom-call | flops 201326592 | bytes 1441792 | tf_op jit(solution)/shard_map/pallas_call | solution.py:56
  (24 shorter events, 0.3 us)
Async XLA Ops:
  2.9 2.0 %collective-permute-start = (f32[256,128]{1,0:T(8,128)S(1)}, f32[256,128]{1,0:T(8,128)S(1)}, u32[]{:S(2)}, u32[]{:S(2)}) collective-permute-start(f32[256,128]{1,0:T(8,128)S(1)} %slice.46), channel_id=1, source_target_pairs={{0,1},{1,0},{2,3},{3,2},{4,5},{5,4},{6,7},{7,6},{8,9},{9,8},{10,11... | collective-permute-start | bytes 393224 | tf_op jit(solution)/shard_map/ppermute | solution.py:77
  3.5 1.6 %collective-permute-start.1 = (f32[64,1024]{1,0:T(8,128)S(1)}, f32[64,1024]{1,0:T(8,128)S(1)}, u32[]{:S(2)}, u32[]{:S(2)}) collective-permute-start(f32[64,1024]{1,0:T(8,128)S(1)} %slice.48), channel_id=1, source_target_pairs={{0,1},{1,0},{2,3},{3,2},{4,5},{5,4},{6,7},{7,6},{8,9},{9,8},{10,11... | collective-permute-start | bytes 786440 | tf_op jit(solution)/shard_map/ppermute | solution.py:77
  4.4 5.1 %collective-permute-start.5 = (f32[128,512]{1,0:T(8,128)S(1)}, f32[128,512]{1,0:T(8,128)S(1)}, u32[]{:S(2)}, u32[]{:S(2)}) collective-permute-start(f32[128,512]{1,0:T(8,128)S(1)} %slice.54), channel_id=1, source_target_pairs={{0,1},{1,0},{2,3},{3,2},{4,5},{5,4},{6,7},{7,6},{8,9},{9,8},{10,11... | collective-permute-start | bytes 786440 | tf_op jit(solution)/shard_map/ppermute | solution.py:77
  5.2 4.7 %collective-permute-start.2 = (f32[64,128]{1,0:T(8,128)S(1)}, f32[64,128]{1,0:T(8,128)S(1)}, u32[]{:S(2)}, u32[]{:S(2)}) collective-permute-start(f32[64,128]{1,0:T(8,128)S(1)} %slice.61), channel_id=1, source_target_pairs={{0,8},{4,12},{8,0},{12,4},{16,24},{20,28},{24,16},{28,20},{1,9},{5... | collective-permute-start | bytes 98312 | tf_op jit(solution)/shard_map/ppermute | solution.py:77
  7.9 7.8 %collective-permute-start.7 = (f32[64,768]{1,0:T(8,128)S(1)}, f32[64,768]{1,0:T(8,128)S(1)}, u32[]{:S(2)}, u32[]{:S(2)}) collective-permute-start(f32[64,768]{1,0:T(8,128)S(1)} %slice.65), channel_id=1, source_target_pairs={{0,2},{1,3},{2,0},{3,1},{4,6},{5,7},{6,4},{7,5},{8,10},{9,11},{10,... | collective-permute-start | bytes 589832 | tf_op jit(solution)/shard_map/ppermute | solution.py:77
  9.9 4.3 %collective-permute-start.3 = (f32[64,256]{1,0:T(8,128)S(1)}, f32[64,256]{1,0:T(8,128)S(1)}, u32[]{:S(2)}, u32[]{:S(2)}) collective-permute-start(f32[64,256]{1,0:T(8,128)S(1)} %pad_maximum_fusion.2), channel_id=1, source_target_pairs={{0,4},{4,0},{8,12},{12,8},{16,20},{20,16},{24,28},{28,24},{1,5},{5... | collective-permute-start | bytes 196616 | tf_op jit(solution)/shard_map/ppermute | solution.py:77
  11.9 13.2 %collective-permute-start.6 = (f32[64,512]{1,0:T(8,128)S(1)}, f32[64,512]{1,0:T(8,128)S(1)}, u32[]{:S(2)}, u32[]{:S(2)}) collective-permute-start(f32[64,512]{1,0:T(8,128)S(1)} %get-tuple-element.69.refs_0_), channel_id=1, source_target_pairs={{0,2},{1,3},{2,0},{3,1},{4,6},{5,7},{6,4},{7,5},{8,10},{9,11},{10,... | collective-permute-start | bytes 393224 | tf_op jit(solution)/shard_map/ppermute | solution.py:77
  13.4 13.5 %collective-permute-start.9 = (f32[64,512]{1,0:T(8,128)S(1)}, f32[64,512]{1,0:T(8,128)S(1)}, u32[]{:S(2)}, u32[]{:S(2)}) collective-permute-start(f32[64,512]{1,0:T(8,128)S(1)} %get-tuple-element.70.refs_0_), channel_id=1, source_target_pairs={{0,2},{1,3},{2,0},{3,1},{4,6},{5,7},{6,4},{7,5},{8,10},{9,11},{10,... | collective-permute-start | bytes 393224 | tf_op jit(solution)/shard_map/ppermute | solution.py:77
  15.7 4.0 %collective-permute-start.11 = (f32[64,128]{1,0:T(8,128)S(1)}, f32[64,128]{1,0:T(8,128)S(1)}, u32[]{:S(2)}, u32[]{:S(2)}) collective-permute-start(f32[64,128]{1,0:T(8,128)S(1)} %slice.68), channel_id=1, source_target_pairs={{0,4},{4,0},{8,12},{12,8},{16,20},{20,16},{24,28},{28,24},{1,5},{5... | collective-permute-start | bytes 98312 | tf_op jit(solution)/shard_map/ppermute | solution.py:77
  17.3 7.3 %collective-permute-start.4 = (f32[384,128]{1,0:T(8,128)S(1)}, f32[384,128]{1,0:T(8,128)S(1)}, u32[]{:S(2)}, u32[]{:S(2)}) collective-permute-start(f32[384,128]{1,0:T(8,128)S(1)} %pad_maximum_fusion.1), channel_id=1, source_target_pairs={{0,2},{1,3},{2,0},{3,1},{4,6},{5,7},{6,4},{7,5},{8,10},{9,11},{10,... | collective-permute-start | bytes 589832 | tf_op jit(solution)/shard_map/ppermute | solution.py:77
  18.9 5.8 %collective-permute-start.8 = (f32[64,640]{1,0:T(8,128)S(1)}, f32[64,640]{1,0:T(8,128)S(1)}, u32[]{:S(2)}, u32[]{:S(2)}) collective-permute-start(f32[64,640]{1,0:T(8,128)S(1)} %slice.66.own_ref), channel_id=1, source_target_pairs={{0,1},{1,0},{2,3},{3,2},{4,5},{5,4},{6,7},{7,6},{8,9},{9,8},{10,11... | collective-permute-start | bytes 491528 | tf_op jit(solution)/shard_map/ppermute | solution.py:77
  19.7 8.3 %collective-permute-start.12 = (f32[64,128]{1,0:T(8,128)S(1)}, f32[64,128]{1,0:T(8,128)S(1)}, u32[]{:S(2)}, u32[]{:S(2)}) collective-permute-start(f32[64,128]{1,0:T(8,128)S(1)} %slice_add_fusion.3.own_ref), channel_id=1, source_target_pairs={{0,1},{1,0},{2,3},{3,2},{4,5},{5,4},{6,7},{7,6},{8,9},{9,8},{10,11... | collective-permute-start | bytes 98312 | tf_op jit(solution)/shard_map/ppermute | solution.py:77
  25.4 4.9 %collective-permute-start.13 = (f32[64,256]{1,0:T(8,128)S(1)}, f32[64,256]{1,0:T(8,128)S(1)}, u32[]{:S(2)}, u32[]{:S(2)}) collective-permute-start(f32[64,256]{1,0:T(8,128)S(1)} %get-tuple-element.61.refs_0_), channel_id=1, source_target_pairs={{0,4},{4,0},{8,12},{12,8},{16,20},{20,16},{24,28},{28,24},{1,5},{5... | collective-permute-start | bytes 196616 | tf_op jit(solution)/shard_map/ppermute | solution.py:77
  27.4 4.3 %collective-permute-start.16 = (f32[64,256]{1,0:T(8,128)S(1)}, f32[64,256]{1,0:T(8,128)S(1)}, u32[]{:S(2)}, u32[]{:S(2)}) collective-permute-start(f32[64,256]{1,0:T(8,128)S(1)} %get-tuple-element.64.refs_0_), channel_id=1, source_target_pairs={{0,4},{4,0},{8,12},{12,8},{16,20},{20,16},{24,28},{28,24},{1,5},{5... | collective-permute-start | bytes 196616 | tf_op jit(solution)/shard_map/ppermute | solution.py:77
  28.0 9.4 %collective-permute-start.10 = (f32[640,128]{1,0:T(8,128)S(1)}, f32[640,128]{1,0:T(8,128)S(1)}, u32[]{:S(2)}, u32[]{:S(2)}) collective-permute-start(f32[640,128]{1,0:T(8,128)S(1)} %pad_maximum_fusion.own_ref), channel_id=1, source_target_pairs={{0,1},{1,0},{2,3},{3,2},{4,5},{5,4},{6,7},{7,6},{8,9},{9,8},{10,11... | collective-permute-start | bytes 983048 | tf_op jit(solution)/shard_map/ppermute | solution.py:77
  30.5 4.0 %collective-permute-start.14 = (f32[64,128]{1,0:T(8,128)S(1)}, f32[64,128]{1,0:T(8,128)S(1)}, u32[]{:S(2)}, u32[]{:S(2)}) collective-permute-start(f32[64,128]{1,0:T(8,128)S(1)} %get-tuple-element.63), channel_id=1, source_target_pairs={{0,8},{4,12},{8,0},{12,4},{16,24},{20,28},{24,16},{28,20},{1,9},{5... | collective-permute-start | bytes 98312 | tf_op jit(solution)/shard_map/ppermute | solution.py:77
  31.8 4.0 %collective-permute-start.17 = (f32[64,128]{1,0:T(8,128)S(1)}, f32[64,128]{1,0:T(8,128)S(1)}, u32[]{:S(2)}, u32[]{:S(2)}) collective-permute-start(f32[64,128]{1,0:T(8,128)S(1)} %get-tuple-element.66), channel_id=1, source_target_pairs={{0,8},{4,12},{8,0},{12,4},{16,24},{20,28},{24,16},{28,20},{1,9},{5... | collective-permute-start | bytes 98312 | tf_op jit(solution)/shard_map/ppermute | solution.py:77
  34.5 4.4 %collective-permute-start.15 = (f32[128,128]{1,0:T(8,128)S(1)}, f32[128,128]{1,0:T(8,128)S(1)}, u32[]{:S(2)}, u32[]{:S(2)}) collective-permute-start(f32[128,128]{1,0:T(8,128)S(1)} %pad_maximum_fusion.3.refs_2_), channel_id=1, source_target_pairs={{0,1},{1,0},{2,3},{3,2},{4,5},{5,4},{6,7},{7,6},{8,9},{9,8},{10,11... | collective-permute-start | bytes 196616 | tf_op jit(solution)/shard_map/ppermute | solution.py:77
  35.8 3.1 %collective-permute-start.18 = (f32[128,128]{1,0:T(8,128)S(1)}, f32[128,128]{1,0:T(8,128)S(1)}, u32[]{:S(2)}, u32[]{:S(2)}) collective-permute-start(f32[128,128]{1,0:T(8,128)S(1)} %pad_maximum_fusion.4.refs_4_), channel_id=1, source_target_pairs={{0,1},{1,0},{2,3},{3,2},{4,5},{5,4},{6,7},{7,6},{8,9},{9,8},{10,11... | collective-permute-start | bytes 196616 | tf_op jit(solution)/shard_map/ppermute | solution.py:77
where the time goes:
time: 40.5 us; the launch traced here: 40.3 us
  starting transfers between devices  16.6 us (41%)
  waiting for transfers between devices  13.5 us (33%)
  Pallas kernels  9.62 us (24%)
    ppermute x19, starting transfers between devices, swap(): lax.ppermute(array, axis, [(i, i ^ 1 << bit) for i in range(lax.axis_size...  16.6 us
    ppermute x19, waiting for transfers between devices, swap(): lax.ppermute(array, axis, [(i, i ^ 1 << bit) for i in range(lax.axis_size...  13.5 us
    pallas_call x12, Pallas kernels, call(): pl.pallas_call(body, out_shape=outs, in_specs=[pl.BlockSpec(memory_space=...  9.62 us
  transfers between devices with their start and end apart: 19, of which 10 were waited for; matrix products, arithmetic and copies ran while one was open for 1% of the time, Pallas kernels for 13%

commit v1 on v0

--- a/solution.py
+++ b/solution.py
@@ -96,9 +96,9 @@
     top = levels
     rows_here, rank = leaf_basis.shape
     columns = queries.shape[1]
-    groups, sub = lax.axis_size("rows"), lax.axis_size("sub")
+    nodes, sub = lax.axis_size("rows"), lax.axis_size("sub")
     heights = [None] + [levels + 1 - e for e in range(1, count)]
-    widths = [1] + [groups // 2 ** heights[e] for e in range(1, count)]
+    widths = [1] + [nodes // 2 ** heights[e] for e in range(1, count)]
     head = sum(w == 1 for w in widths)
     bits = [range(0)] + [
         range(widths[e - 1].bit_length() - 1, widths[e].bit_length() - 1) for e in range(1, count)
@@ -113,7 +113,8 @@
     small = 2 * 3 * rank**3
 
     scale = row_scale.reshape(-1, rank)
-    starts = [sum(len(b) for b in blocks[:e]) * rank for e in range(count + 1)]
+    groups = [([e] if e >= head else []) + blocks[e] for e in range(count)]
+    starts = [sum(len(b) for b in groups[:e]) * rank for e in range(count + 1)]
 
     def gram_body(*refs):
         scale_hbm, leaf_hbm, level_hbm, queries_hbm, leaf_core_hbm, core_hbm = refs[:6]
@@ -134,24 +135,17 @@
         parts = [halves(v) for v in vectors]
         side = core_side()
         for e in range(count):
-            group = ([e] if e >= head else []) + blocks[e]
-            right = [lanes([parts[f][i] for f in group]) for i in range(2)]
+            right = [lanes([parts[f][i] for f in groups[e]]) for i in range(2)]
             value = dot_parts(halves(vectors[e].T), right)
             for h in range(2):
-                rows = value[h * half : (h + 1) * half]
-                if e >= head:
-                    place = starts[count] + (e - head) * rank
-                    out_ref[at(h ^ side, half), place : place + rank] = rows[:, :rank]
-                    rows = rows[:, rank:]
-                if blocks[e]:
-                    out_ref[at(h ^ side, half), starts[e] : starts[e + 1]] = rows
+                out_ref[at(h ^ side, half), starts[e] : starts[e + 1]] = value[h * half : (h + 1) * half]
         for copy in copies[2 + levels :]:
             copy.wait()
 
     gram, scale, leaf_basis, level_basis, queries, cores = call(
         gram_body,
         [
-            (rank, starts[count] + coarse * rank),
+            (rank, starts[count]),
             *[array.shape for array in (scale, leaf_basis, level_basis, queries)],
             (count, rank, rank),
         ],
@@ -159,18 +153,20 @@
             pltpu.with_memory_space_constraint(array, pltpu.HBM)
             for array in (scale, leaf_basis, level_basis, queries, leaf_cores, level_cores)
         ],
-        flops=small * (starts[count] // rank + coarse) * rows_here // rank,
+        flops=small * starts[count] // rank * rows_here // rank,
         spaces=[pltpu.HBM] * 6,
         scratch=[pltpu.SemaphoreType.DMA((3 + levels + count,))],
     )
     gram_chip = gram[:half] + swap(gram[half:], "sub", 0)
-    early = add_all(partial_sums(gram_chip[:, : starts[count]], "sub", leaf_bits))
-    diagonal = []
-    for e in reversed(range(head, count)):
-        place = starts[count] + (e - head) * rank
-        diagonal = lanes([gram_chip[:, place : place + rank], *diagonal])
-        diagonal = [add_all(partial_sums(diagonal, "rows", bits[e]))]
-    diagonal = diagonal[0]
+    early = add_all(partial_sums(gram_chip[:, : starts[head]], "sub", leaf_bits))
+    remaining, diagonal, coupling = gram_chip[:, starts[head] :], [], []
+    for e in range(head, count):
+        remaining = add_all(partial_sums(remaining, "rows", bits[e]))
+        size = starts[e + 1] - starts[e]
+        diagonal.append(remaining[:, :rank])
+        coupling.append(remaining[:, rank:size])
+        remaining = remaining[:, size:]
+    coupling = lanes(coupling[:-1])
 
     def moment_body(scale_ref, queries_ref, leaf_ref, level_ref, out_ref, *basis_refs):
         spread = column_scale(scale_ref[...])
@@ -192,7 +188,10 @@
         flops=small * count * 2 * rows_here // rank,
     )
     moment_chip = value[:mine] + swap(value[mine:], "sub", 0)
-    moment_parts = [partial_sums(moment_chip[b * batch : (b + 1) * batch], "sub", leaf_bits) for b in range(batches)]
+    moment_parts = [moment_chip[b * batch : (b + 1) * batch] for b in range(batches)]
+    moment_parts[-1] = lanes([moment_parts[-1], coupling])
+    moment_parts = [partial_sums(moment_parts[b], "sub", leaf_bits) for b in range(batches)]
+    coupling = add_all([part[:, count * rank :] for part in moment_parts[-1]])
 
     late_rows = columns // 2 + head * half
 
@@ -226,10 +225,7 @@
     )
     late_chip = late[:late_rows] + swap(late[late_rows:], "sub", 0)
 
-    def stacked(array, size):
-        return [array[:, j : j + size] for j in range(0, array.shape[1], size)]
-
-    late = jnp.concatenate([late_chip, *stacked(diagonal, rank)], axis=0)
+    late = jnp.concatenate([late_chip, *diagonal], axis=0)
     late_size = late.shape[0]
     late = add_all(partial_sums(late, "sub", leaf_bits))
 
@@ -238,15 +234,16 @@
         side = core_side()
         stack_ref[at(side, half), :] = own_ref[...]
         stack_ref[at(1 - side, half), :] = other_ref[...]
-        base = starts[group[0]]
+        place = 0
         for i, e in enumerate(group):
-            block = stack_ref[:, starts[e] - base : starts[e + 1] - base]
+            block = stack_ref[:, place : place + len(blocks[e]) * rank]
             store(out_refs[2 * i : 2 * i + 2], dot(core_ref[e].T, block))
+            place += len(blocks[e]) * rank
 
     def products(group, own):
         out = call(
             functools.partial(product_body, group),
-            [part for e in group for part in pair(rank, starts[e + 1] - starts[e])],
+            [part for e in group for part in pair(rank, len(blocks[e]) * rank)],
             own,
             swap(own, "sub", 0),
             cores,
@@ -255,13 +252,8 @@
         )
         return [out[2 * i : 2 * i + 2] for i in range(len(group))]
 
-    factors = products(list(range(head)), early[:, : starts[head]])
-    remaining = early[:, starts[head] :]
-    for e in range(head, top):
-        remaining = add_all(partial_sums(remaining, "rows", bits[e]))
-        size = starts[e + 1] - starts[e]
-        factors += products([e], remaining[:, :size])
-        remaining = remaining[:, size:]
+    factors = products(list(range(head)), early)
+    factors += products(list(range(head, top)), coupling)
 
     def flat(group):
         return [part for factor in group for part in factor]
@@ -274,7 +266,7 @@
 
     def head_body(number, *refs):
         part_refs, factor_refs, (own_ref, rest_ref) = refs[:number], paired(refs[number:-2]), refs[-2:]
-        rest = add_all([part[...] for part in part_refs])
+        rest = add_all([part[:, : count * rank] for part in part_refs])
         for e in range(head):
             own, rest = rest[:, :rank], rest[:, rank:]
             own_ref[e * batch : (e + 1) * batch, :] = own

time: 40.5 us -> 45 us (1.11)
  waiting for transfers between devices: 13.5 us -> 20.1 us
  starting transfers between devices: 16.6 us -> 14.5 us
    ppermute x19 -> x18, waiting for transfers between devices: 13.5 us -> 20.1 us  [swap(): lax.ppermute(array, axis, [(i, i ^ 1 << bit) for i in range(lax.axis_size...]
    ppermute x19 -> x18, starting transfers between devices: 16.6 us -> 14.5 us  [swap(): lax.ppermute(array, axis, [(i, i ^ 1 << bit) for i in range(lax.axis_size...]
  transfers between devices with their start and end apart: 19 -> 18, of which waited for: 10 -> 8; matrix products, arithmetic and copies ran while one was open for 1% -> 1% of each run, Pallas kernels for 13% -> 13%
where the time goes in v1:
time: 45 us; the launch traced here: 44.8 us
  waiting for transfers between devices  20.1 us (45%)
  starting transfers between devices  14.5 us (32%)
  Pallas kernels  9.61 us (21%)
    ppermute x18, waiting for transfers between devices, swap(): lax.ppermute(array, axis, [(i, i ^ 1 << bit) for i in range(lax.axis_size...  20.1 us
    ppermute x18, starting transfers between devices, swap(): lax.ppermute(array, axis, [(i, i ^ 1 << bit) for i in range(lax.axis_size...  14.5 us
    pallas_call x12, Pallas kernels, call(): pl.pallas_call(body, out_shape=outs, in_specs=[pl.BlockSpec(memory_space=...  9.61 us
  transfers between devices with their start and end apart: 18, of which 8 were waited for; matrix products, arithmetic and copies ran while one was open for 1% of the time, Pallas kernels for 13%

profile of v1, /device:TPU:0, one launch (start us, length us, event | category | flops | bytes accessed | tf_op | source)
XLA Modules:
  0.0 44.8 jit_solution(3836716151312939518)
XLA Ops:
  0.0 2.1 %shard_map.64 = (f32[128,1024]{1,0:T(8,128)S(1)}, f32[4,128]{1,0:T(4,128)S(1)}, f32[512,128]{1,0:T(8,128)S(1)}, f32[3,512,128]{2,1,0:T(8,128)S(1)}, f32[512,256]{1,0:T(8,128)S(1)}, /*index=5*/f32[4,128,128]{2,1,0:T(8,128)S(1)}) custom-call(f32[4,128]{1,0:T(4,128)} %bitcast.1, f32[512,128]{1,0:T(8,128)} %refs_1_.1, f32[3,512,128]{2,1,0:T(8,128)} %refs_2_.1, ...), custom_call_target="tpu_custom_call" | custom-call | flops 402653184 | bytes 2557952 | tf_op jit(solution)/shard_map/pallas_call | solution.py:56
  2.2 0.6 %collective-permute-start.1 = (f32[64,1024]{1,0:T(8,128)S(1)}, f32[64,1024]{1,0:T(8,128)S(1)}, u32[]{:S(2)}, u32[]{:S(2)}) collective-permute-start(f32[64,1024]{1,0:T(8,128)S(1)} %slice.45), channel_id=1, source_target_pairs={{0,1},{1,0},{2,3},{3,2},{4,5},{5,4},{6,7},{7,6},{8,9},{9,8},{10,11... | collective-permute-start | bytes 786440 | tf_op jit(solution)/shard_map/ppermute | solution.py:77
  2.7 0.8 %shard_map.66 = (f32[256,512]{1,0:T(8,128)S(1)}, bf16[512,512]{1,0:T(8,128)(2,1)S(1)}, bf16[512,512]{1,0:T(8,128)(2,1)S(1)}) custom-call(f32[4,128]{1,0:T(4,128)S(1)} %get-tuple-element.36.scale_ref, f32[512,256]{1,0:T(8,128)S(1)} %get-tuple-element.37.queries_ref, f32[512,128]{1,0:T(8,128)S(1)} %get-tuple-element.38.leaf_ref, ...), custom_call_target="tpu_custom_call" | custom-call | flops 402653184 | bytes 1574912 | tf_op jit(solution)/shard_map/pallas_call | solution.py:56
  3.5 0.1 collective-permute-start.5
  3.6 0.8 %shard_map.65 = (f32[512,128]{1,0:T(8,128)S(1)}, bf16[512,128]{1,0:T(8,128)(2,1)S(1)}, bf16[512,128]{1,0:T(8,128)(2,1)S(1)}) custom-call(f32[4,128]{1,0:T(4,128)S(1)} %get-tuple-element.36.scale_ref, f32[512,256]{1,0:T(8,128)S(1)} %get-tuple-element.37.queries_ref, f32[512,128]{1,0:T(8,128)S(1)} %get-tuple-element.38.leaf_ref, ...), custom_call_target="tpu_custom_call" | custom-call | flops 201326592 | bytes 1574912 | tf_op jit(solution)/shard_map/pallas_call | solution.py:56
  4.4 0.6 %collective-permute-start = (f32[256,128]{1,0:T(8,128)S(1)}, f32[256,128]{1,0:T(8,128)S(1)}, u32[]{:S(2)}, u32[]{:S(2)}) collective-permute-start(f32[256,128]{1,0:T(8,128)S(1)} %slice.43), channel_id=1, source_target_pairs={{0,1},{1,0},{2,3},{3,2},{4,5},{5,4},{6,7},{7,6},{8,9},{9,8},{10,11... | collective-permute-start | bytes 393224 | tf_op jit(solution)/shard_map/ppermute | solution.py:77
  4.9 0.0 collective-permute-done.1
  5.0 2.6 %collective-permute-start.2 = (f32[64,384]{1,0:T(8,128)S(1)}, f32[64,384]{1,0:T(8,128)S(1)}, u32[]{:S(2)}, u32[]{:S(2)}) collective-permute-start(f32[64,384]{1,0:T(8,128)S(1)} %slice.56), channel_id=1, source_target_pairs={{0,4},{4,0},{8,12},{12,8},{16,20},{20,16},{24,28},{28,24},{1,5},{5... | collective-permute-start | bytes 294920 | tf_op jit(solution)/shard_map/ppermute | solution.py:77
  7.6 0.0 collective-permute-done.5
  7.6 3.4 %collective-permute-done.2 = f32[64,384]{1,0:T(8,128)S(1)} collective-permute-done((f32[64,384]{1,0:T(8,128)S(1)}, f32[64,384]{1,0:T(8,128)S(1)}, u32[]{:S(2)}, u32[]{:S(2)}) %collective-permute-start.2) | collective-permute-done | bytes 98336 | tf_op jit(solution)/shard_map/ppermute | solution.py:77
  11.0 1.9 %collective-permute-start.3 = (f32[64,128]{1,0:T(8,128)S(1)}, f32[64,128]{1,0:T(8,128)S(1)}, u32[]{:S(2)}, u32[]{:S(2)}) collective-permute-start(f32[64,128]{1,0:T(8,128)S(1)} %get-tuple-element.72), channel_id=1, source_target_pairs={{0,8},{4,12},{8,0},{12,4},{16,24},{20,28},{24,16},{28,20},{1,9},{5... | collective-permute-start | bytes 98312 | tf_op jit(solution)/shard_map/ppermute | solution.py:77
  13.0 1.6 %collective-permute-start.9 = (f32[64,640]{1,0:T(8,128)S(1)}, f32[64,640]{1,0:T(8,128)S(1)}, u32[]{:S(2)}, u32[]{:S(2)}) collective-permute-start(f32[64,640]{1,0:T(8,128)S(1)} %pad_maximum_fusion.2.refs_0_), channel_id=1, source_target_pairs={{0,2},{1,3},{2,0},{3,1},{4,6},{5,7},{6,4},{7,5},{8,10},{9,11},{10,... | collective-permute-start | bytes 491528 | tf_op jit(solution)/shard_map/ppermute | solution.py:77
  14.5 0.0 collective-permute-done
  14.6 0.6 %collective-permute-start.7 = (f32[64,640]{1,0:T(8,128)S(1)}, f32[64,640]{1,0:T(8,128)S(1)}, u32[]{:S(2)}, u32[]{:S(2)}) collective-permute-start(f32[64,640]{1,0:T(8,128)S(1)} %slice.60), channel_id=1, source_target_pairs={{0,2},{1,3},{2,0},{3,1},{4,6},{5,7},{6,4},{7,5},{8,10},{9,11},{10,... | collective-permute-start | bytes 491528 | tf_op jit(solution)/shard_map/ppermute | solution.py:77
  15.2 0.0 collective-permute-done.3
  15.2 4.9 %collective-permute-done.9.refs_1_ = f32[64,640]{1,0:T(8,128)S(1)} collective-permute-done((f32[64,640]{1,0:T(8,128)S(1)}, f32[64,640]{1,0:T(8,128)S(1)}, u32[]{:S(2)}, u32[]{:S(2)}) %collective-permute-start.9) | collective-permute-done | bytes 163872 | tf_op jit(solution)/shard_map/ppermute | solution.py:77
  20.1 1.6 %collective-permute-start.4 = (f32[384,128]{1,0:T(8,128)S(1)}, f32[384,128]{1,0:T(8,128)S(1)}, u32[]{:S(2)}, u32[]{:S(2)}) collective-permute-start(f32[384,128]{1,0:T(8,128)S(1)} %pad_maximum_fusion.1), channel_id=1, source_target_pairs={{0,2},{1,3},{2,0},{3,1},{4,6},{5,7},{6,4},{7,5},{8,10},{9,11},{10,... | collective-permute-start | bytes 589832 | tf_op jit(solution)/shard_map/ppermute | solution.py:77
  21.7 1.9 %collective-permute-done.7 = f32[64,640]{1,0:T(8,128)S(1)} collective-permute-done((f32[64,640]{1,0:T(8,128)S(1)}, f32[64,640]{1,0:T(8,128)S(1)}, u32[]{:S(2)}, u32[]{:S(2)}) %collective-permute-start.7) | collective-permute-done | bytes 163872 | tf_op jit(solution)/shard_map/ppermute | solution.py:77
  23.6 0.1 collective-permute-start.8
  23.7 1.6 %collective-permute-start.6 = (f32[64,512]{1,0:T(8,128)S(1)}, f32[64,512]{1,0:T(8,128)S(1)}, u32[]{:S(2)}, u32[]{:S(2)}) collective-permute-start(f32[64,512]{1,0:T(8,128)S(1)} %get-tuple-element.67.refs_0_), channel_id=1, source_target_pairs={{0,2},{1,3},{2,0},{3,1},{4,6},{5,7},{6,4},{7,5},{8,10},{9,11},{10,... | collective-permute-start | bytes 393224 | tf_op jit(solution)/shard_map/ppermute | solution.py:77
  25.3 0.2 collective-permute-start.11
  25.4 0.0 collective-permute-done.8.other_ref
  25.4 0.4 shard_map.67
  25.8 3.8 %collective-permute-done.6.refs_1_ = f32[64,512]{1,0:T(8,128)S(1)} collective-permute-done((f32[64,512]{1,0:T(8,128)S(1)}, f32[64,512]{1,0:T(8,128)S(1)}, u32[]{:S(2)}, u32[]{:S(2)}) %collective-permute-start.6) | collective-permute-done | bytes 131104 | tf_op jit(solution)/shard_map/ppermute | solution.py:77
  29.6 0.4 shard_map.68
  30.0 1.6 %collective-permute-start.12 = (f32[64,256]{1,0:T(8,128)S(1)}, f32[64,256]{1,0:T(8,128)S(1)}, u32[]{:S(2)}, u32[]{:S(2)}) collective-permute-start(f32[64,256]{1,0:T(8,128)S(1)} %get-tuple-element.61.refs_0_), channel_id=1, source_target_pairs={{0,4},{4,0},{8,12},{12,8},{16,20},{20,16},{24,28},{28,24},{1,5},{5... | collective-permute-start | bytes 196616 | tf_op jit(solution)/shard_map/ppermute | solution.py:77
  31.5 0.3 shard_map.69
  31.9 0.6 %collective-permute-start.15 = (f32[64,256]{1,0:T(8,128)S(1)}, f32[64,256]{1,0:T(8,128)S(1)}, u32[]{:S(2)}, u32[]{:S(2)}) collective-permute-start(f32[64,256]{1,0:T(8,128)S(1)} %get-tuple-element.64.refs_0_), channel_id=1, source_target_pairs={{0,4},{4,0},{8,12},{12,8},{16,20},{20,16},{24,28},{28,24},{1,5},{5... | collective-permute-start | bytes 196616 | tf_op jit(solution)/shard_map/ppermute | solution.py:77
  32.5 0.0 collective-permute-done.4
  32.5 0.1 collective-permute-start.10
  32.6 0.0 collective-permute-done.11.other_ref
  32.6 0.2 shard_map.71
  32.9 1.9 %collective-permute-done.12.refs_1_ = f32[64,256]{1,0:T(8,128)S(1)} collective-permute-done((f32[64,256]{1,0:T(8,128)S(1)}, f32[64,256]{1,0:T(8,128)S(1)}, u32[]{:S(2)}, u32[]{:S(2)}) %collective-permute-start.12) | collective-permute-done | bytes 65568 | tf_op jit(solution)/shard_map/ppermute | solution.py:77
  34.8 0.1 shard_map.73
  34.9 0.1 collective-permute-start.13
  35.0 1.2 %collective-permute-done.15.refs_1_ = f32[64,256]{1,0:T(8,128)S(1)} collective-permute-done((f32[64,256]{1,0:T(8,128)S(1)}, f32[64,256]{1,0:T(8,128)S(1)}, u32[]{:S(2)}, u32[]{:S(2)}) %collective-permute-start.15) | collective-permute-done | bytes 65568 | tf_op jit(solution)/shard_map/ppermute | solution.py:77
  36.2 0.1 shard_map.74
  36.3 0.9 %collective-permute-start.16 = (f32[64,128]{1,0:T(8,128)S(1)}, f32[64,128]{1,0:T(8,128)S(1)}, u32[]{:S(2)}, u32[]{:S(2)}) collective-permute-start(f32[64,128]{1,0:T(8,128)S(1)} %get-tuple-element.66), channel_id=1, source_target_pairs={{0,8},{4,12},{8,0},{12,4},{16,24},{20,28},{24,16},{28,20},{1,9},{5... | collective-permute-start | bytes 98312 | tf_op jit(solution)/shard_map/ppermute | solution.py:77
  37.2 1.7 %collective-permute-done.13 = f32[64,128]{1,0:T(8,128)S(1)} collective-permute-done((f32[64,128]{1,0:T(8,128)S(1)}, f32[64,128]{1,0:T(8,128)S(1)}, u32[]{:S(2)}, u32[]{:S(2)}) %collective-permute-start.13) | collective-permute-done | bytes 32800 | tf_op jit(solution)/shard_map/ppermute | solution.py:77
  38.9 0.1 collective-permute-start.14
  39.0 1.4 %collective-permute-done.16 = f32[64,128]{1,0:T(8,128)S(1)} collective-permute-done((f32[64,128]{1,0:T(8,128)S(1)}, f32[64,128]{1,0:T(8,128)S(1)}, u32[]{:S(2)}, u32[]{:S(2)}) %collective-permute-start.16) | collective-permute-done | bytes 32800 | tf_op jit(solution)/shard_map/ppermute | solution.py:77
  40.3 0.1 collective-permute-start.17
  40.4 1.5 %shard_map.72 = (bf16[512,256]{1,0:T(8,128)(2,1)S(1)}, bf16[512,256]{1,0:T(8,128)(2,1)S(1)}) custom-call(bf16[128,384]{1,0:T(8,128)(2,1)S(1)} %get-tuple-element.44.refs_2_.refs_0_, bf16[128,384]{1,0:T(8,128)(2,1)S(1)} %get-tuple-element.45.refs_3_.refs_1_, bf16[128,256]{1,0:T(8,128)(2,1)S(1)} %get-tuple-element.46.refs_4_.refs_2_, ...), custom_call_target="tpu_custom_call" | custom-call | flops 402653184 | bytes 1441792 | tf_op jit(solution)/shard_map/pallas_call | solution.py:56
  41.9 0.0 collective-permute-done.10.other_ref
  41.9 1.4 %shard_map.70 = (f32[512,256]{1,0:T(8,128)S(1)}, bf16[128,256]{1,0:T(8,128)(2,1)S(1)}, bf16[128,256]{1,0:T(8,128)(2,1)S(1)}) custom-call(f32[4,128]{1,0:T(4,128)S(1)} %get-tuple-element.36.scale_ref, f32[512,256]{1,0:T(8,128)S(1)} %get-tuple-element.37.queries_ref, f32[640,128]{1,0:T(8,128)S(1)} %pad_maximum_fusion.own_ref, ...), custom_call_target="tpu_custom_call" | custom-call | flops 301989888 | bytes 3082240 | tf_op jit(solution)/shard_map/pallas_call | solution.py:56
  43.4 0.0 collective-permute-done.14.refs_3_
  43.4 0.0 collective-permute-done.17.refs_5_
  43.4 1.4 %shard_map.75 = f32[512,256]{1,0:T(8,128)} custom-call(f32[512,256]{1,0:T(8,128)S(1)} %get-tuple-element.54.base_ref, bf16[512,256]{1,0:T(8,128)(2,1)S(1)} %get-tuple-element.57.high_ref, bf16[512,256]{1,0:T(8,128)(2,1)S(1)} %get-tuple-element.58.low_ref, bf16[128,256]{1,0:T(8,128)(2,1)S(1)} %get-tuple-element.59.refs_0_, ...), custom_call_target="tpu_custom_call" | custom-call | flops 201326592 | bytes 1441792 | tf_op jit(solution)/shard_map/pallas_call | solution.py:56
  (21 shorter events, 0.3 us)
Async XLA Ops:
  2.2 2.8 %collective-permute-start.1 = (f32[64,1024]{1,0:T(8,128)S(1)}, f32[64,1024]{1,0:T(8,128)S(1)}, u32[]{:S(2)}, u32[]{:S(2)}) collective-permute-start(f32[64,1024]{1,0:T(8,128)S(1)} %slice.45), channel_id=1, source_target_pairs={{0,1},{1,0},{2,3},{3,2},{4,5},{5,4},{6,7},{7,6},{8,9},{9,8},{10,11... | collective-permute-start | bytes 786440 | tf_op jit(solution)/shard_map/ppermute | solution.py:77
  3.5 4.0 %collective-permute-start.5 = (f32[128,512]{1,0:T(8,128)S(1)}, f32[128,512]{1,0:T(8,128)S(1)}, u32[]{:S(2)}, u32[]{:S(2)}) collective-permute-start(f32[128,512]{1,0:T(8,128)S(1)} %slice.50), channel_id=1, source_target_pairs={{0,1},{1,0},{2,3},{3,2},{4,5},{5,4},{6,7},{7,6},{8,9},{9,8},{10,11... | collective-permute-start | bytes 786440 | tf_op jit(solution)/shard_map/ppermute | solution.py:77
  4.4 10.2 %collective-permute-start = (f32[256,128]{1,0:T(8,128)S(1)}, f32[256,128]{1,0:T(8,128)S(1)}, u32[]{:S(2)}, u32[]{:S(2)}) collective-permute-start(f32[256,128]{1,0:T(8,128)S(1)} %slice.43), channel_id=1, source_target_pairs={{0,1},{1,0},{2,3},{3,2},{4,5},{5,4},{6,7},{7,6},{8,9},{9,8},{10,11... | collective-permute-start | bytes 393224 | tf_op jit(solution)/shard_map/ppermute | solution.py:77
  5.0 6.0 %collective-permute-start.2 = (f32[64,384]{1,0:T(8,128)S(1)}, f32[64,384]{1,0:T(8,128)S(1)}, u32[]{:S(2)}, u32[]{:S(2)}) collective-permute-start(f32[64,384]{1,0:T(8,128)S(1)} %slice.56), channel_id=1, source_target_pairs={{0,4},{4,0},{8,12},{12,8},{16,20},{20,16},{24,28},{28,24},{1,5},{5... | collective-permute-start | bytes 294920 | tf_op jit(solution)/shard_map/ppermute | solution.py:77
  11.0 4.1 %collective-permute-start.3 = (f32[64,128]{1,0:T(8,128)S(1)}, f32[64,128]{1,0:T(8,128)S(1)}, u32[]{:S(2)}, u32[]{:S(2)}) collective-permute-start(f32[64,128]{1,0:T(8,128)S(1)} %get-tuple-element.72), channel_id=1, source_target_pairs={{0,8},{4,12},{8,0},{12,4},{16,24},{20,28},{24,16},{28,20},{1,9},{5... | collective-permute-start | bytes 98312 | tf_op jit(solution)/shard_map/ppermute | solution.py:77
  13.0 7.1 %collective-permute-start.9 = (f32[64,640]{1,0:T(8,128)S(1)}, f32[64,640]{1,0:T(8,128)S(1)}, u32[]{:S(2)}, u32[]{:S(2)}) collective-permute-start(f32[64,640]{1,0:T(8,128)S(1)} %pad_maximum_fusion.2.refs_0_), channel_id=1, source_target_pairs={{0,2},{1,3},{2,0},{3,1},{4,6},{5,7},{6,4},{7,5},{8,10},{9,11},{10,... | collective-permute-start | bytes 491528 | tf_op jit(solution)/shard_map/ppermute | solution.py:77
  14.6 9.0 %collective-permute-start.7 = (f32[64,640]{1,0:T(8,128)S(1)}, f32[64,640]{1,0:T(8,128)S(1)}, u32[]{:S(2)}, u32[]{:S(2)}) collective-permute-start(f32[64,640]{1,0:T(8,128)S(1)} %slice.60), channel_id=1, source_target_pairs={{0,2},{1,3},{2,0},{3,1},{4,6},{5,7},{6,4},{7,5},{8,10},{9,11},{10,... | collective-permute-start | bytes 491528 | tf_op jit(solution)/shard_map/ppermute | solution.py:77
  20.1 12.4 %collective-permute-start.4 = (f32[384,128]{1,0:T(8,128)S(1)}, f32[384,128]{1,0:T(8,128)S(1)}, u32[]{:S(2)}, u32[]{:S(2)}) collective-permute-start(f32[384,128]{1,0:T(8,128)S(1)} %pad_maximum_fusion.1), channel_id=1, source_target_pairs={{0,2},{1,3},{2,0},{3,1},{4,6},{5,7},{6,4},{7,5},{8,10},{9,11},{10,... | collective-permute-start | bytes 589832 | tf_op jit(solution)/shard_map/ppermute | solution.py:77
  23.6 1.8 %collective-permute-start.8 = (f32[64,640]{1,0:T(8,128)S(1)}, f32[64,640]{1,0:T(8,128)S(1)}, u32[]{:S(2)}, u32[]{:S(2)}) collective-permute-start(f32[64,640]{1,0:T(8,128)S(1)} %slice_add_fusion.6.own_ref), channel_id=1, source_target_pairs={{0,1},{1,0},{2,3},{3,2},{4,5},{5,4},{6,7},{7,6},{8,9},{9,8},{10,11... | collective-permute-start | bytes 491528 | tf_op jit(solution)/shard_map/ppermute | solution.py:77
  23.7 5.9 %collective-permute-start.6 = (f32[64,512]{1,0:T(8,128)S(1)}, f32[64,512]{1,0:T(8,128)S(1)}, u32[]{:S(2)}, u32[]{:S(2)}) collective-permute-start(f32[64,512]{1,0:T(8,128)S(1)} %get-tuple-element.67.refs_0_), channel_id=1, source_target_pairs={{0,2},{1,3},{2,0},{3,1},{4,6},{5,7},{6,4},{7,5},{8,10},{9,11},{10,... | collective-permute-start | bytes 393224 | tf_op jit(solution)/shard_map/ppermute | solution.py:77
  25.3 7.3 %collective-permute-start.11 = (f32[64,128]{1,0:T(8,128)S(1)}, f32[64,128]{1,0:T(8,128)S(1)}, u32[]{:S(2)}, u32[]{:S(2)}) collective-permute-start(f32[64,128]{1,0:T(8,128)S(1)} %get-tuple-element.69.own_ref), channel_id=1, source_target_pairs={{0,1},{1,0},{2,3},{3,2},{4,5},{5,4},{6,7},{7,6},{8,9},{9,8},{10,11... | collective-permute-start | bytes 98312 | tf_op jit(solution)/shard_map/ppermute | solution.py:77
  30.0 4.8 %collective-permute-start.12 = (f32[64,256]{1,0:T(8,128)S(1)}, f32[64,256]{1,0:T(8,128)S(1)}, u32[]{:S(2)}, u32[]{:S(2)}) collective-permute-start(f32[64,256]{1,0:T(8,128)S(1)} %get-tuple-element.61.refs_0_), channel_id=1, source_target_pairs={{0,4},{4,0},{8,12},{12,8},{16,20},{20,16},{24,28},{28,24},{1,5},{5... | collective-permute-start | bytes 196616 | tf_op jit(solution)/shard_map/ppermute | solution.py:77
  31.9 4.3 %collective-permute-start.15 = (f32[64,256]{1,0:T(8,128)S(1)}, f32[64,256]{1,0:T(8,128)S(1)}, u32[]{:S(2)}, u32[]{:S(2)}) collective-permute-start(f32[64,256]{1,0:T(8,128)S(1)} %get-tuple-element.64.refs_0_), channel_id=1, source_target_pairs={{0,4},{4,0},{8,12},{12,8},{16,20},{20,16},{24,28},{28,24},{1,5},{5... | collective-permute-start | bytes 196616 | tf_op jit(solution)/shard_map/ppermute | solution.py:77
  32.5 9.4 %collective-permute-start.10 = (f32[640,128]{1,0:T(8,128)S(1)}, f32[640,128]{1,0:T(8,128)S(1)}, u32[]{:S(2)}, u32[]{:S(2)}) collective-permute-start(f32[640,128]{1,0:T(8,128)S(1)} %pad_maximum_fusion.own_ref), channel_id=1, source_target_pairs={{0,1},{1,0},{2,3},{3,2},{4,5},{5,4},{6,7},{7,6},{8,9},{9,8},{10,11... | collective-permute-start | bytes 983048 | tf_op jit(solution)/shard_map/ppermute | solution.py:77
  34.9 4.0 %collective-permute-start.13 = (f32[64,128]{1,0:T(8,128)S(1)}, f32[64,128]{1,0:T(8,128)S(1)}, u32[]{:S(2)}, u32[]{:S(2)}) collective-permute-start(f32[64,128]{1,0:T(8,128)S(1)} %get-tuple-element.63), channel_id=1, source_target_pairs={{0,8},{4,12},{8,0},{12,4},{16,24},{20,28},{24,16},{28,20},{1,9},{5... | collective-permute-start | bytes 98312 | tf_op jit(solution)/shard_map/ppermute | solution.py:77
  36.3 4.0 %collective-permute-start.16 = (f32[64,128]{1,0:T(8,128)S(1)}, f32[64,128]{1,0:T(8,128)S(1)}, u32[]{:S(2)}, u32[]{:S(2)}) collective-permute-start(f32[64,128]{1,0:T(8,128)S(1)} %get-tuple-element.66), channel_id=1, source_target_pairs={{0,8},{4,12},{8,0},{12,4},{16,24},{20,28},{24,16},{28,20},{1,9},{5... | collective-permute-start | bytes 98312 | tf_op jit(solution)/shard_map/ppermute | solution.py:77
  38.9 4.5 %collective-permute-start.14 = (f32[128,128]{1,0:T(8,128)S(1)}, f32[128,128]{1,0:T(8,128)S(1)}, u32[]{:S(2)}, u32[]{:S(2)}) collective-permute-start(f32[128,128]{1,0:T(8,128)S(1)} %pad_maximum_fusion.3.refs_2_), channel_id=1, source_target_pairs={{0,1},{1,0},{2,3},{3,2},{4,5},{5,4},{6,7},{7,6},{8,9},{9,8},{10,11... | collective-permute-start | bytes 196616 | tf_op jit(solution)/shard_map/ppermute | solution.py:77
  40.3 3.0 %collective-permute-start.17 = (f32[128,128]{1,0:T(8,128)S(1)}, f32[128,128]{1,0:T(8,128)S(1)}, u32[]{:S(2)}, u32[]{:S(2)}) collective-permute-start(f32[128,128]{1,0:T(8,128)S(1)} %pad_maximum_fusion.4.refs_4_), channel_id=1, source_target_pairs={{0,1},{1,0},{2,3},{3,2},{4,5},{5,4},{6,7},{7,6},{8,9},{9,8},{10,11... | collective-permute-start | bytes 196616 | tf_op jit(solution)/shard_map/ppermute | solution.py:77

commit v2 on v1

--- a/solution.py
+++ b/solution.py
@@ -163,10 +163,13 @@
     for e in range(head, count):
         remaining = add_all(partial_sums(remaining, "rows", bits[e]))
         size = starts[e + 1] - starts[e]
-        diagonal.append(remaining[:, :rank])
-        coupling.append(remaining[:, rank:size])
-        remaining = remaining[:, size:]
-    coupling = lanes(coupling[:-1])
+        pieces = [remaining[:, :rank]]
+        if e < top:
+            pieces = lax.optimization_barrier([*pieces, remaining[:, rank:size], remaining[:, size:]])
+            coupling.append(pieces[1])
+            remaining = pieces[2]
+        diagonal.append(pieces[0])
+    coupling = lanes(coupling)
 
     def moment_body(scale_ref, queries_ref, leaf_ref, level_ref, out_ref, *basis_refs):
         spread = column_scale(scale_ref[...])
@@ -191,7 +194,6 @@
     moment_parts = [moment_chip[b * batch : (b + 1) * batch] for b in range(batches)]
     moment_parts[-1] = lanes([moment_parts[-1], coupling])
     moment_parts = [partial_sums(moment_parts[b], "sub", leaf_bits) for b in range(batches)]
-    coupling = add_all([part[:, count * rank :] for part in moment_parts[-1]])
 
     late_rows = columns // 2 + head * half
 
@@ -253,7 +255,6 @@
         return [out[2 * i : 2 * i + 2] for i in range(len(group))]
 
     factors = products(list(range(head)), early)
-    factors += products(list(range(head, top)), coupling)
 
     def flat(group):
         return [part for factor in group for part in factor]
@@ -265,8 +266,12 @@
         return [ref[:, start : start + size] for ref in factor]
 
     def head_body(number, *refs):
-        part_refs, factor_refs, (own_ref, rest_ref) = refs[:number], paired(refs[number:-2]), refs[-2:]
-        rest = add_all([part[:, : count * rank] for part in part_refs])
+        part_refs, factor_refs = refs[:number], paired(refs[number : number + 2 * head])
+        own_ref, rest_ref, *coupling_refs = refs[number + 2 * head :]
+        total = add_all([part[...] for part in part_refs])
+        rest = total[:, : count * rank]
+        for ref in coupling_refs:
+            ref[...] = total[:, count * rank :]
         for e in range(head):
             own, rest = rest[:, :rank], rest[:, rank:]
             own_ref[e * batch : (e + 1) * batch, :] = own
@@ -289,17 +294,21 @@
                         e * batch : (e + 1) * batch, :
                     ]
 
-    head_moments, found_parts = [], []
+    head_moments, rests, found_parts = [], [], []
     for b in range(batches):
-        own, rest = call(
+        extra = moment_parts[b][0].shape[1] - count * rank
+        own, rest, *coupling = call(
             functools.partial(head_body, len(moment_parts[b])),
-            [(head * batch, rank), (batch, coarse * rank)],
+            [(head * batch, rank), (batch, coarse * rank)] + ([(batch, extra)] if extra else []),
             *moment_parts[b],
             *flat(factors[:head]),
             flops=small * sum(map(len, blocks[:head])) // batches,
         )
         head_moments.append(own)
-        found = []
+        rests.append(rest)
+    factors += products(list(range(head, top)), coupling[0])
+    for b in range(batches):
+        rest, found = rests[b], []
         for e in range(head, top):
             parts = partial_sums(rest, "rows", bits[e])
             own, rest = call(

time: 45 us -> 43.2 us (0.960)
  waiting for transfers between devices: 20.1 us -> 15.5 us
  starting transfers between devices: 14.5 us -> 17.3 us
    ppermute x18, waiting for transfers between devices: 20.1 us -> 15.5 us  [swap(): lax.ppermute(array, axis, [(i, i ^ 1 << bit) for i in range(lax.axis_size...]
    ppermute x18, starting transfers between devices: 14.5 us -> 17.3 us  [swap(): lax.ppermute(array, axis, [(i, i ^ 1 << bit) for i in range(lax.axis_size...]
  transfers between devices with their start and end apart: 18 -> 18, of which waited for: 8 -> 8; matrix products, arithmetic and copies ran while one was open for 1% -> 1% of each run, Pallas kernels for 13% -> 12%
where the time goes in v2:
time: 43.2 us; the launch traced here: 43 us
  starting transfers between devices  17.3 us (40%)
  waiting for transfers between devices  15.5 us (36%)
  Pallas kernels  9.62 us (22%)
    ppermute x18, starting transfers between devices, swap(): lax.ppermute(array, axis, [(i, i ^ 1 << bit) for i in range(lax.axis_size...  17.3 us
    ppermute x18, waiting for transfers between devices, swap(): lax.ppermute(array, axis, [(i, i ^ 1 << bit) for i in range(lax.axis_size...  15.5 us
    pallas_call x12, Pallas kernels, call(): pl.pallas_call(body, out_shape=outs, in_specs=[pl.BlockSpec(memory_space=...  9.62 us
  transfers between devices with their start and end apart: 18, of which 8 were waited for; matrix products, arithmetic and copies ran while one was open for 1% of the time, Pallas kernels for 12%

profile of v2, /device:TPU:0, one launch (start us, length us, event | category | flops | bytes accessed | tf_op | source)
XLA Modules:
  0.0 43.0 jit_solution(12819393437224569361)
XLA Ops:
  0.0 2.1 %shard_map.64 = (f32[128,1024]{1,0:T(8,128)S(1)}, f32[4,128]{1,0:T(4,128)S(1)}, f32[512,128]{1,0:T(8,128)S(1)}, f32[3,512,128]{2,1,0:T(8,128)S(1)}, f32[512,256]{1,0:T(8,128)S(1)}, /*index=5*/f32[4,128,128]{2,1,0:T(8,128)S(1)}) custom-call(f32[4,128]{1,0:T(4,128)} %bitcast.1, f32[512,128]{1,0:T(8,128)} %refs_1_.1, f32[3,512,128]{2,1,0:T(8,128)} %refs_2_.1, ...), custom_call_target="tpu_custom_call" | custom-call | flops 402653184 | bytes 2557952 | tf_op jit(solution)/shard_map/pallas_call | solution.py:56
  2.1 0.8 %shard_map.65 = (f32[512,128]{1,0:T(8,128)S(1)}, bf16[512,128]{1,0:T(8,128)(2,1)S(1)}, bf16[512,128]{1,0:T(8,128)(2,1)S(1)}) custom-call(f32[4,128]{1,0:T(4,128)S(1)} %get-tuple-element.40.scale_ref, f32[512,256]{1,0:T(8,128)S(1)} %get-tuple-element.41.queries_ref, f32[512,128]{1,0:T(8,128)S(1)} %get-tuple-element.42.leaf_ref, ...), custom_call_target="tpu_custom_call" | custom-call | flops 201326592 | bytes 1574912 | tf_op jit(solution)/shard_map/pallas_call | solution.py:56
  2.9 0.6 %collective-permute-start = (f32[256,128]{1,0:T(8,128)S(1)}, f32[256,128]{1,0:T(8,128)S(1)}, u32[]{:S(2)}, u32[]{:S(2)}) collective-permute-start(f32[256,128]{1,0:T(8,128)S(1)} %slice.40), channel_id=1, source_target_pairs={{0,1},{1,0},{2,3},{3,2},{4,5},{5,4},{6,7},{7,6},{8,9},{9,8},{10,11... | collective-permute-start | bytes 393224 | tf_op jit(solution)/shard_map/ppermute | solution.py:77
  3.5 0.1 collective-permute-start.1
  3.6 0.8 %shard_map.66 = (f32[256,512]{1,0:T(8,128)S(1)}, bf16[512,512]{1,0:T(8,128)(2,1)S(1)}, bf16[512,512]{1,0:T(8,128)(2,1)S(1)}) custom-call(f32[4,128]{1,0:T(4,128)S(1)} %get-tuple-element.40.scale_ref, f32[512,256]{1,0:T(8,128)S(1)} %get-tuple-element.41.queries_ref, f32[512,128]{1,0:T(8,128)S(1)} %get-tuple-element.42.leaf_ref, ...), custom_call_target="tpu_custom_call" | custom-call | flops 402653184 | bytes 1574912 | tf_op jit(solution)/shard_map/pallas_call | solution.py:56
  4.4 0.6 %collective-permute-start.5 = (f32[128,512]{1,0:T(8,128)S(1)}, f32[128,512]{1,0:T(8,128)S(1)}, u32[]{:S(2)}, u32[]{:S(2)}) collective-permute-start(f32[128,512]{1,0:T(8,128)S(1)} %slice.48), channel_id=1, source_target_pairs={{0,1},{1,0},{2,3},{3,2},{4,5},{5,4},{6,7},{7,6},{8,9},{9,8},{10,11... | collective-permute-start | bytes 786440 | tf_op jit(solution)/shard_map/ppermute | solution.py:77
  4.9 0.0 collective-permute-done
  5.0 0.1 collective-permute-done.1
  5.2 2.7 %collective-permute-start.2 = (f32[64,384]{1,0:T(8,128)S(1)}, f32[64,384]{1,0:T(8,128)S(1)}, u32[]{:S(2)}, u32[]{:S(2)}) collective-permute-start(f32[64,384]{1,0:T(8,128)S(1)} %slice.52), channel_id=1, source_target_pairs={{0,4},{4,0},{8,12},{12,8},{16,20},{20,16},{24,28},{28,24},{1,5},{5... | collective-permute-start | bytes 294920 | tf_op jit(solution)/shard_map/ppermute | solution.py:77
  7.8 1.5 %collective-permute-start.7 = (f32[64,640]{1,0:T(8,128)S(1)}, f32[64,640]{1,0:T(8,128)S(1)}, u32[]{:S(2)}, u32[]{:S(2)}) collective-permute-start(f32[64,640]{1,0:T(8,128)S(1)} %slice.57), channel_id=1, source_target_pairs={{0,2},{1,3},{2,0},{3,1},{4,6},{5,7},{6,4},{7,5},{8,10},{9,11},{10,... | collective-permute-start | bytes 491528 | tf_op jit(solution)/shard_map/ppermute | solution.py:77
  9.4 0.0 collective-permute-done.5
  9.4 1.8 %collective-permute-done.2 = f32[64,384]{1,0:T(8,128)S(1)} collective-permute-done((f32[64,384]{1,0:T(8,128)S(1)}, f32[64,384]{1,0:T(8,128)S(1)}, u32[]{:S(2)}, u32[]{:S(2)}) %collective-permute-start.2) | collective-permute-done | bytes 98336 | tf_op jit(solution)/shard_map/ppermute | solution.py:77
  11.2 1.9 %collective-permute-start.3 = (f32[64,128]{1,0:T(8,128)S(1)}, f32[64,128]{1,0:T(8,128)S(1)}, u32[]{:S(2)}, u32[]{:S(2)}) collective-permute-start(f32[64,128]{1,0:T(8,128)S(1)} %get-tuple-element.47), channel_id=1, source_target_pairs={{0,8},{4,12},{8,0},{12,4},{16,24},{20,28},{24,16},{28,20},{1,9},{5... | collective-permute-start | bytes 98312 | tf_op jit(solution)/shard_map/ppermute | solution.py:77
  13.1 2.1 %collective-permute-done.3 = f32[64,128]{1,0:T(8,128)S(1)} collective-permute-done((f32[64,128]{1,0:T(8,128)S(1)}, f32[64,128]{1,0:T(8,128)S(1)}, u32[]{:S(2)}, u32[]{:S(2)}) %collective-permute-start.3) | collective-permute-done | bytes 32800 | tf_op jit(solution)/shard_map/ppermute | solution.py:77
  15.2 1.8 %collective-permute-start.4 = (f32[384,128]{1,0:T(8,128)S(1)}, f32[384,128]{1,0:T(8,128)S(1)}, u32[]{:S(2)}, u32[]{:S(2)}) collective-permute-start(f32[384,128]{1,0:T(8,128)S(1)} %pad_maximum_fusion.1), channel_id=1, source_target_pairs={{0,2},{1,3},{2,0},{3,1},{4,6},{5,7},{6,4},{7,5},{8,10},{9,11},{10,... | collective-permute-start | bytes 589832 | tf_op jit(solution)/shard_map/ppermute | solution.py:77
  17.0 0.0 collective-permute-done.7
  17.1 0.1 collective-permute-start.8
  17.2 0.3 collective-permute-start.9
  17.5 1.8 %collective-permute-start.6 = (f32[64,512]{1,0:T(8,128)S(1)}, f32[64,512]{1,0:T(8,128)S(1)}, u32[]{:S(2)}, u32[]{:S(2)}) collective-permute-start(f32[64,512]{1,0:T(8,128)S(1)} %get-tuple-element.75.refs_0_), channel_id=1, source_target_pairs={{0,2},{1,3},{2,0},{3,1},{4,6},{5,7},{6,4},{7,5},{8,10},{9,11},{10,... | collective-permute-start | bytes 393224 | tf_op jit(solution)/shard_map/ppermute | solution.py:77
  19.3 0.0 collective-permute-done.8.other_ref
  19.3 0.4 shard_map.67
  19.6 7.7 %collective-permute-done.6.refs_1_ = f32[64,512]{1,0:T(8,128)S(1)} collective-permute-done((f32[64,512]{1,0:T(8,128)S(1)}, f32[64,512]{1,0:T(8,128)S(1)}, u32[]{:S(2)}, u32[]{:S(2)}) %collective-permute-start.6) | collective-permute-done | bytes 131104 | tf_op jit(solution)/shard_map/ppermute | solution.py:77
  27.3 0.4 shard_map.68
  27.7 1.7 %collective-permute-start.12 = (f32[64,256]{1,0:T(8,128)S(1)}, f32[64,256]{1,0:T(8,128)S(1)}, u32[]{:S(2)}, u32[]{:S(2)}) collective-permute-start(f32[64,256]{1,0:T(8,128)S(1)} %get-tuple-element.69.refs_0_), channel_id=1, source_target_pairs={{0,4},{4,0},{8,12},{12,8},{16,20},{20,16},{24,28},{28,24},{1,5},{5... | collective-permute-start | bytes 196616 | tf_op jit(solution)/shard_map/ppermute | solution.py:77
  29.4 0.0 collective-permute-done.9.refs_1_
  29.4 0.4 shard_map.69
  29.8 0.1 collective-permute-start.11
  29.9 0.4 %collective-permute-start.15 = (f32[64,256]{1,0:T(8,128)S(1)}, f32[64,256]{1,0:T(8,128)S(1)}, u32[]{:S(2)}, u32[]{:S(2)}) collective-permute-start(f32[64,256]{1,0:T(8,128)S(1)} %get-tuple-element.72.refs_0_), channel_id=1, source_target_pairs={{0,4},{4,0},{8,12},{12,8},{16,20},{20,16},{24,28},{28,24},{1,5},{5... | collective-permute-start | bytes 196616 | tf_op jit(solution)/shard_map/ppermute | solution.py:77
  30.3 0.0 collective-permute-done.4
  30.4 0.2 collective-permute-start.10
  30.6 0.5 %collective-permute-done.11.other_ref = f32[64,128]{1,0:T(8,128)S(1)} collective-permute-done((f32[64,128]{1,0:T(8,128)S(1)}, f32[64,128]{1,0:T(8,128)S(1)}, u32[]{:S(2)}, u32[]{:S(2)}) %collective-permute-start.11) | collective-permute-done | bytes 32800 | tf_op jit(solution)/shard_map/ppermute | solution.py:77
  31.1 0.2 shard_map.71
  31.3 0.7 %collective-permute-done.12.refs_1_ = f32[64,256]{1,0:T(8,128)S(1)} collective-permute-done((f32[64,256]{1,0:T(8,128)S(1)}, f32[64,256]{1,0:T(8,128)S(1)}, u32[]{:S(2)}, u32[]{:S(2)}) %collective-permute-start.12) | collective-permute-done | bytes 65568 | tf_op jit(solution)/shard_map/ppermute | solution.py:77
  32.0 0.1 shard_map.73
  32.2 1.8 %collective-permute-start.13 = (f32[64,128]{1,0:T(8,128)S(1)}, f32[64,128]{1,0:T(8,128)S(1)}, u32[]{:S(2)}, u32[]{:S(2)}) collective-permute-start(f32[64,128]{1,0:T(8,128)S(1)} %get-tuple-element.71), channel_id=1, source_target_pairs={{0,8},{4,12},{8,0},{12,4},{16,24},{20,28},{24,16},{28,20},{1,9},{5... | collective-permute-start | bytes 98312 | tf_op jit(solution)/shard_map/ppermute | solution.py:77
  34.0 0.4 collective-permute-done.15.refs_1_
  34.4 0.1 shard_map.74
  34.5 1.6 %collective-permute-start.16 = (f32[64,128]{1,0:T(8,128)S(1)}, f32[64,128]{1,0:T(8,128)S(1)}, u32[]{:S(2)}, u32[]{:S(2)}) collective-permute-start(f32[64,128]{1,0:T(8,128)S(1)} %get-tuple-element.74), channel_id=1, source_target_pairs={{0,8},{4,12},{8,0},{12,4},{16,24},{20,28},{24,16},{28,20},{1,9},{5... | collective-permute-start | bytes 98312 | tf_op jit(solution)/shard_map/ppermute | solution.py:77
  36.1 0.0 collective-permute-done.13
  36.2 0.1 collective-permute-start.14
  36.3 2.2 %collective-permute-done.16 = f32[64,128]{1,0:T(8,128)S(1)} collective-permute-done((f32[64,128]{1,0:T(8,128)S(1)}, f32[64,128]{1,0:T(8,128)S(1)}, u32[]{:S(2)}, u32[]{:S(2)}) %collective-permute-start.16) | collective-permute-done | bytes 32800 | tf_op jit(solution)/shard_map/ppermute | solution.py:77
  38.5 0.1 collective-permute-start.17
  38.6 1.5 %shard_map.72 = (bf16[512,256]{1,0:T(8,128)(2,1)S(1)}, bf16[512,256]{1,0:T(8,128)(2,1)S(1)}) custom-call(bf16[128,384]{1,0:T(8,128)(2,1)S(1)} %get-tuple-element.50.refs_2_.refs_0_, bf16[128,384]{1,0:T(8,128)(2,1)S(1)} %get-tuple-element.51.refs_3_.refs_1_, bf16[128,256]{1,0:T(8,128)(2,1)S(1)} %get-tuple-element.52.refs_4_.refs_2_, ...), custom_call_target="tpu_custom_call" | custom-call | flops 402653184 | bytes 1441792 | tf_op jit(solution)/shard_map/pallas_call | solution.py:56
  40.1 0.0 collective-permute-done.10.other_ref
  40.1 1.5 %shard_map.70 = (f32[512,256]{1,0:T(8,128)S(1)}, bf16[128,256]{1,0:T(8,128)(2,1)S(1)}, bf16[128,256]{1,0:T(8,128)(2,1)S(1)}) custom-call(f32[4,128]{1,0:T(4,128)S(1)} %get-tuple-element.40.scale_ref, f32[512,256]{1,0:T(8,128)S(1)} %get-tuple-element.41.queries_ref, f32[640,128]{1,0:T(8,128)S(1)} %pad_maximum_fusion.own_ref, ...), custom_call_target="tpu_custom_call" | custom-call | flops 301989888 | bytes 3082240 | tf_op jit(solution)/shard_map/pallas_call | solution.py:56
  41.5 0.0 collective-permute-done.14.refs_3_
  41.6 0.0 collective-permute-done.17.refs_5_
  41.6 1.4 %shard_map.75 = f32[512,256]{1,0:T(8,128)} custom-call(f32[512,256]{1,0:T(8,128)S(1)} %get-tuple-element.61.base_ref, bf16[512,256]{1,0:T(8,128)(2,1)S(1)} %get-tuple-element.65.high_ref, bf16[512,256]{1,0:T(8,128)(2,1)S(1)} %get-tuple-element.66.low_ref, bf16[128,256]{1,0:T(8,128)(2,1)S(1)} %get-tuple-element.67.refs_0_, ...), custom_call_target="tpu_custom_call" | custom-call | flops 201326592 | bytes 1441792 | tf_op jit(solution)/shard_map/pallas_call | solution.py:56
  (21 shorter events, 0.3 us)
Async XLA Ops:
  2.9 2.0 %collective-permute-start = (f32[256,128]{1,0:T(8,128)S(1)}, f32[256,128]{1,0:T(8,128)S(1)}, u32[]{:S(2)}, u32[]{:S(2)}) collective-permute-start(f32[256,128]{1,0:T(8,128)S(1)} %slice.40), channel_id=1, source_target_pairs={{0,1},{1,0},{2,3},{3,2},{4,5},{5,4},{6,7},{7,6},{8,9},{9,8},{10,11... | collective-permute-start | bytes 393224 | tf_op jit(solution)/shard_map/ppermute | solution.py:77
  3.5 1.6 %collective-permute-start.1 = (f32[64,1024]{1,0:T(8,128)S(1)}, f32[64,1024]{1,0:T(8,128)S(1)}, u32[]{:S(2)}, u32[]{:S(2)}) collective-permute-start(f32[64,1024]{1,0:T(8,128)S(1)} %slice.42), channel_id=1, source_target_pairs={{0,1},{1,0},{2,3},{3,2},{4,5},{5,4},{6,7},{7,6},{8,9},{9,8},{10,11... | collective-permute-start | bytes 786440 | tf_op jit(solution)/shard_map/ppermute | solution.py:77
  4.4 5.0 %collective-permute-start.5 = (f32[128,512]{1,0:T(8,128)S(1)}, f32[128,512]{1,0:T(8,128)S(1)}, u32[]{:S(2)}, u32[]{:S(2)}) collective-permute-start(f32[128,512]{1,0:T(8,128)S(1)} %slice.48), channel_id=1, source_target_pairs={{0,1},{1,0},{2,3},{3,2},{4,5},{5,4},{6,7},{7,6},{8,9},{9,8},{10,11... | collective-permute-start | bytes 786440 | tf_op jit(solution)/shard_map/ppermute | solution.py:77
  5.2 6.0 %collective-permute-start.2 = (f32[64,384]{1,0:T(8,128)S(1)}, f32[64,384]{1,0:T(8,128)S(1)}, u32[]{:S(2)}, u32[]{:S(2)}) collective-permute-start(f32[64,384]{1,0:T(8,128)S(1)} %slice.52), channel_id=1, source_target_pairs={{0,4},{4,0},{8,12},{12,8},{16,20},{20,16},{24,28},{28,24},{1,5},{5... | collective-permute-start | bytes 294920 | tf_op jit(solution)/shard_map/ppermute | solution.py:77
  7.8 9.2 %collective-permute-start.7 = (f32[64,640]{1,0:T(8,128)S(1)}, f32[64,640]{1,0:T(8,128)S(1)}, u32[]{:S(2)}, u32[]{:S(2)}) collective-permute-start(f32[64,640]{1,0:T(8,128)S(1)} %slice.57), channel_id=1, source_target_pairs={{0,2},{1,3},{2,0},{3,1},{4,6},{5,7},{6,4},{7,5},{8,10},{9,11},{10,... | collective-permute-start | bytes 491528 | tf_op jit(solution)/shard_map/ppermute | solution.py:77
  11.2 4.0 %collective-permute-start.3 = (f32[64,128]{1,0:T(8,128)S(1)}, f32[64,128]{1,0:T(8,128)S(1)}, u32[]{:S(2)}, u32[]{:S(2)}) collective-permute-start(f32[64,128]{1,0:T(8,128)S(1)} %get-tuple-element.47), channel_id=1, source_target_pairs={{0,8},{4,12},{8,0},{12,4},{16,24},{20,28},{24,16},{28,20},{1,9},{5... | collective-permute-start | bytes 98312 | tf_op jit(solution)/shard_map/ppermute | solution.py:77
  15.2 15.1 %collective-permute-start.4 = (f32[384,128]{1,0:T(8,128)S(1)}, f32[384,128]{1,0:T(8,128)S(1)}, u32[]{:S(2)}, u32[]{:S(2)}) collective-permute-start(f32[384,128]{1,0:T(8,128)S(1)} %pad_maximum_fusion.1), channel_id=1, source_target_pairs={{0,2},{1,3},{2,0},{3,1},{4,6},{5,7},{6,4},{7,5},{8,10},{9,11},{10,... | collective-permute-start | bytes 589832 | tf_op jit(solution)/shard_map/ppermute | solution.py:77
  17.1 2.2 %collective-permute-start.8 = (f32[64,640]{1,0:T(8,128)S(1)}, f32[64,640]{1,0:T(8,128)S(1)}, u32[]{:S(2)}, u32[]{:S(2)}) collective-permute-start(f32[64,640]{1,0:T(8,128)S(1)} %slice_add_fusion.4.own_ref), channel_id=1, source_target_pairs={{0,1},{1,0},{2,3},{3,2},{4,5},{5,4},{6,7},{7,6},{8,9},{9,8},{10,11... | collective-permute-start | bytes 491528 | tf_op jit(solution)/shard_map/ppermute | solution.py:77
  17.2 12.3 %collective-permute-start.9 = (f32[64,640]{1,0:T(8,128)S(1)}, f32[64,640]{1,0:T(8,128)S(1)}, u32[]{:S(2)}, u32[]{:S(2)}) collective-permute-start(f32[64,640]{1,0:T(8,128)S(1)} %pad_maximum_fusion.2.refs_0_), channel_id=1, source_target_pairs={{0,2},{1,3},{2,0},{3,1},{4,6},{5,7},{6,4},{7,5},{8,10},{9,11},{10,... | collective-permute-start | bytes 491528 | tf_op jit(solution)/shard_map/ppermute | solution.py:77
  17.5 9.9 %collective-permute-start.6 = (f32[64,512]{1,0:T(8,128)S(1)}, f32[64,512]{1,0:T(8,128)S(1)}, u32[]{:S(2)}, u32[]{:S(2)}) collective-permute-start(f32[64,512]{1,0:T(8,128)S(1)} %get-tuple-element.75.refs_0_), channel_id=1, source_target_pairs={{0,2},{1,3},{2,0},{3,1},{4,6},{5,7},{6,4},{7,5},{8,10},{9,11},{10,... | collective-permute-start | bytes 393224 | tf_op jit(solution)/shard_map/ppermute | solution.py:77
  27.7 4.3 %collective-permute-start.12 = (f32[64,256]{1,0:T(8,128)S(1)}, f32[64,256]{1,0:T(8,128)S(1)}, u32[]{:S(2)}, u32[]{:S(2)}) collective-permute-start(f32[64,256]{1,0:T(8,128)S(1)} %get-tuple-element.69.refs_0_), channel_id=1, source_target_pairs={{0,4},{4,0},{8,12},{12,8},{16,20},{20,16},{24,28},{28,24},{1,5},{5... | collective-permute-start | bytes 196616 | tf_op jit(solution)/shard_map/ppermute | solution.py:77
  29.8 1.3 %collective-permute-start.11 = (f32[64,128]{1,0:T(8,128)S(1)}, f32[64,128]{1,0:T(8,128)S(1)}, u32[]{:S(2)}, u32[]{:S(2)}) collective-permute-start(f32[64,128]{1,0:T(8,128)S(1)} %get-tuple-element.62.own_ref), channel_id=1, source_target_pairs={{0,1},{1,0},{2,3},{3,2},{4,5},{5,4},{6,7},{7,6},{8,9},{9,8},{10,11... | collective-permute-start | bytes 98312 | tf_op jit(solution)/shard_map/ppermute | solution.py:77
  29.9 4.5 %collective-permute-start.15 = (f32[64,256]{1,0:T(8,128)S(1)}, f32[64,256]{1,0:T(8,128)S(1)}, u32[]{:S(2)}, u32[]{:S(2)}) collective-permute-start(f32[64,256]{1,0:T(8,128)S(1)} %get-tuple-element.72.refs_0_), channel_id=1, source_target_pairs={{0,4},{4,0},{8,12},{12,8},{16,20},{20,16},{24,28},{28,24},{1,5},{5... | collective-permute-start | bytes 196616 | tf_op jit(solution)/shard_map/ppermute | solution.py:77
  30.4 9.7 %collective-permute-start.10 = (f32[640,128]{1,0:T(8,128)S(1)}, f32[640,128]{1,0:T(8,128)S(1)}, u32[]{:S(2)}, u32[]{:S(2)}) collective-permute-start(f32[640,128]{1,0:T(8,128)S(1)} %pad_maximum_fusion.own_ref), channel_id=1, source_target_pairs={{0,1},{1,0},{2,3},{3,2},{4,5},{5,4},{6,7},{7,6},{8,9},{9,8},{10,11... | collective-permute-start | bytes 983048 | tf_op jit(solution)/shard_map/ppermute | solution.py:77
  32.2 4.0 %collective-permute-start.13 = (f32[64,128]{1,0:T(8,128)S(1)}, f32[64,128]{1,0:T(8,128)S(1)}, u32[]{:S(2)}, u32[]{:S(2)}) collective-permute-start(f32[64,128]{1,0:T(8,128)S(1)} %get-tuple-element.71), channel_id=1, source_target_pairs={{0,8},{4,12},{8,0},{12,4},{16,24},{20,28},{24,16},{28,20},{1,9},{5... | collective-permute-start | bytes 98312 | tf_op jit(solution)/shard_map/ppermute | solution.py:77
  34.5 4.0 %collective-permute-start.16 = (f32[64,128]{1,0:T(8,128)S(1)}, f32[64,128]{1,0:T(8,128)S(1)}, u32[]{:S(2)}, u32[]{:S(2)}) collective-permute-start(f32[64,128]{1,0:T(8,128)S(1)} %get-tuple-element.74), channel_id=1, source_target_pairs={{0,8},{4,12},{8,0},{12,4},{16,24},{20,28},{24,16},{28,20},{1,9},{5... | collective-permute-start | bytes 98312 | tf_op jit(solution)/shard_map/ppermute | solution.py:77
  36.2 5.4 %collective-permute-start.14 = (f32[128,128]{1,0:T(8,128)S(1)}, f32[128,128]{1,0:T(8,128)S(1)}, u32[]{:S(2)}, u32[]{:S(2)}) collective-permute-start(f32[128,128]{1,0:T(8,128)S(1)} %pad_maximum_fusion.3.refs_2_), channel_id=1, source_target_pairs={{0,1},{1,0},{2,3},{3,2},{4,5},{5,4},{6,7},{7,6},{8,9},{9,8},{10,11... | collective-permute-start | bytes 196616 | tf_op jit(solution)/shard_map/ppermute | solution.py:77
  38.5 3.1 %collective-permute-start.17 = (f32[128,128]{1,0:T(8,128)S(1)}, f32[128,128]{1,0:T(8,128)S(1)}, u32[]{:S(2)}, u32[]{:S(2)}) collective-permute-start(f32[128,128]{1,0:T(8,128)S(1)} %pad_maximum_fusion.4.refs_4_), channel_id=1, source_target_pairs={{0,1},{1,0},{2,3},{3,2},{4,5},{5,4},{6,7},{7,6},{8,9},{9,8},{10,11... | collective-permute-start | bytes 196616 | tf_op jit(solution)/shard_map/ppermute | solution.py:77

commit v3 on v1

--- a/solution.py
+++ b/solution.py
@@ -160,13 +160,16 @@
     gram_chip = gram[:half] + swap(gram[half:], "sub", 0)
     early = add_all(partial_sums(gram_chip[:, : starts[head]], "sub", leaf_bits))
     remaining, diagonal, coupling = gram_chip[:, starts[head] :], [], []
-    for e in range(head, count):
+    for e in range(head, top):
         remaining = add_all(partial_sums(remaining, "rows", bits[e]))
         size = starts[e + 1] - starts[e]
-        diagonal.append(remaining[:, :rank])
-        coupling.append(remaining[:, rank:size])
-        remaining = remaining[:, size:]
-    coupling = lanes(coupling[:-1])
+        pieces = [remaining[:, :rank], remaining[:, rank:size], remaining[:, size:]]
+        pieces = lax.optimization_barrier(pieces)
+        diagonal.append(pieces[0])
+        coupling.append(pieces[1])
+        remaining = pieces[2]
+    coupling = add_all(partial_sums(lanes([*coupling, remaining]), "sub", leaf_bits))
+    top_block, coupling = coupling[:, -rank:], coupling[:, :-rank]
 
     def moment_body(scale_ref, queries_ref, leaf_ref, level_ref, out_ref, *basis_refs):
         spread = column_scale(scale_ref[...])
@@ -189,9 +192,7 @@
     )
     moment_chip = value[:mine] + swap(value[mine:], "sub", 0)
     moment_parts = [moment_chip[b * batch : (b + 1) * batch] for b in range(batches)]
-    moment_parts[-1] = lanes([moment_parts[-1], coupling])
     moment_parts = [partial_sums(moment_parts[b], "sub", leaf_bits) for b in range(batches)]
-    coupling = add_all([part[:, count * rank :] for part in moment_parts[-1]])
 
     late_rows = columns // 2 + head * half
 
@@ -253,7 +254,6 @@
         return [out[2 * i : 2 * i + 2] for i in range(len(group))]
 
     factors = products(list(range(head)), early)
-    factors += products(list(range(head, top)), coupling)
 
     def flat(group):
         return [part for factor in group for part in factor]
@@ -265,8 +265,9 @@
         return [ref[:, start : start + size] for ref in factor]
 
     def head_body(number, *refs):
-        part_refs, factor_refs, (own_ref, rest_ref) = refs[:number], paired(refs[number:-2]), refs[-2:]
-        rest = add_all([part[:, : count * rank] for part in part_refs])
+        part_refs, factor_refs = refs[:number], paired(refs[number : number + 2 * head])
+        own_ref, rest_ref = refs[number + 2 * head :]
+        rest = add_all([part[...] for part in part_refs])
         for e in range(head):
             own, rest = rest[:, :rank], rest[:, rank:]
             own_ref[e * batch : (e + 1) * batch, :] = own
@@ -289,6 +290,7 @@
                         e * batch : (e + 1) * batch, :
                     ]
 
+    factors += products(list(range(head, top)), coupling)
     head_moments, found_parts = [], []
     for b in range(batches):
         own, rest = call(
@@ -310,6 +312,8 @@
                 flops=small * (top - e) // batches,
             )
             found.append(own)
+        if b == 0:
+            rest = jnp.concatenate([rest, top_block], axis=0)
         found.append(add_all(partial_sums(rest, "rows", bits[top])))
         found = jnp.concatenate(found, axis=0)
         found_parts.append([found, swap(found, "sub", 0)])
@@ -340,15 +344,17 @@
         flops=small * coarse * count * rows_here // rank,
     )
 
-    def base_body(scale_ref, queries_ref, own_ref, other_ref, core_ref, *refs):
+    def base_body(scale_ref, queries_ref, own_ref, other_ref, own_found_ref, other_found_ref, core_ref, *refs):
         factor_refs, basis_refs, scaled_refs = paired(refs[: 2 * head]), refs[2 * head : -7], refs[-7:-5]
         out_ref, *gain_refs, stack_ref, gram_ref = refs[-5:]
         pieces = [pl.ds(late_size + b * head * batch, head * batch) for b in range(batches)]
         scatter([(own_ref.at[piece], other_ref.at[piece]) for piece in pieces], head, stack_ref)
         side = core_side()
-        for late_ref, place in ((own_ref, side), (other_ref, 1 - side)):
+        sources = ((own_ref, own_found_ref, side), (other_ref, other_found_ref, 1 - side))
+        for late_ref, found_ref, place in sources:
             stack_ref[at(place, columns // 2), head * rank :] = late_ref[: columns // 2]
-            for e in range(count):
+            gram_ref[at(place, half), top * rank :] = found_ref[coarse * batch :]
+            for e in range(top):
                 start = columns // 2 + e * half
                 gram_ref[at(place, half), e * rank : (e + 1) * rank] = late_ref[start : start + half]
         products = [dot(core_ref[e].T, gram_ref[:, e * rank : (e + 1) * rank]) for e in range(count)]
@@ -372,6 +378,7 @@
         scale,
         queries,
         *late_parts,
+        *found_parts[0],
         cores,
         *flat(factors[:head]),
         *basis,

time: 45 us -> 39.2 us (0.87)
  waiting for transfers between devices: 20.1 us -> 14 us
    ppermute x18, waiting for transfers between devices: 20.1 us -> 14 us  [swap(): lax.ppermute(array, axis, [(i, i ^ 1 << bit) for i in range(lax.axis_size...]
  transfers between devices with their start and end apart: 18 -> 18, of which waited for: 8 -> 8; matrix products, arithmetic and copies ran while one was open for 1% -> 1% of each run, Pallas kernels for 13% -> 14%
where the time goes in v3:
time: 39.2 us; the launch traced here: 39 us
  starting transfers between devices  14.7 us (38%)
  waiting for transfers between devices  14 us (36%)
  Pallas kernels  9.62 us (25%)
    ppermute x18, starting transfers between devices, swap(): lax.ppermute(array, axis, [(i, i ^ 1 << bit) for i in range(lax.axis_size...  14.7 us
    ppermute x18, waiting for transfers between devices, swap(): lax.ppermute(array, axis, [(i, i ^ 1 << bit) for i in range(lax.axis_size...  14 us
    pallas_call x12, Pallas kernels, call(): pl.pallas_call(body, out_shape=outs, in_specs=[pl.BlockSpec(memory_space=...  9.62 us
  transfers between devices with their start and end apart: 18, of which 8 were waited for; matrix products, arithmetic and copies ran while one was open for 1% of the time, Pallas kernels for 14%

profile of v3, /device:TPU:0, one launch (start us, length us, event | category | flops | bytes accessed | tf_op | source)
XLA Modules:
  0.0 39.0 jit_solution(14098467273719421903)
XLA Ops:
  0.0 2.1 %shard_map.64 = (f32[128,1024]{1,0:T(8,128)S(1)}, f32[4,128]{1,0:T(4,128)S(1)}, f32[512,128]{1,0:T(8,128)S(1)}, f32[3,512,128]{2,1,0:T(8,128)S(1)}, f32[512,256]{1,0:T(8,128)S(1)}, /*index=5*/f32[4,128,128]{2,1,0:T(8,128)S(1)}) custom-call(f32[4,128]{1,0:T(4,128)} %bitcast.1, f32[512,128]{1,0:T(8,128)} %refs_1_.1, f32[3,512,128]{2,1,0:T(8,128)} %refs_2_.1, ...), custom_call_target="tpu_custom_call" | custom-call | flops 402653184 | bytes 2557952 | tf_op jit(solution)/shard_map/pallas_call | solution.py:56
  2.1 0.8 %shard_map.65 = (f32[512,128]{1,0:T(8,128)S(1)}, bf16[512,128]{1,0:T(8,128)(2,1)S(1)}, bf16[512,128]{1,0:T(8,128)(2,1)S(1)}) custom-call(f32[4,128]{1,0:T(4,128)S(1)} %get-tuple-element.39.scale_ref, f32[512,256]{1,0:T(8,128)S(1)} %get-tuple-element.40.queries_ref, f32[512,128]{1,0:T(8,128)S(1)} %get-tuple-element.41.leaf_ref, ...), custom_call_target="tpu_custom_call" | custom-call | flops 201326592 | bytes 1574912 | tf_op jit(solution)/shard_map/pallas_call | solution.py:56
  2.9 0.6 %collective-permute-start = (f32[256,128]{1,0:T(8,128)S(1)}, f32[256,128]{1,0:T(8,128)S(1)}, u32[]{:S(2)}, u32[]{:S(2)}) collective-permute-start(f32[256,128]{1,0:T(8,128)S(1)} %slice.46), channel_id=1, source_target_pairs={{0,1},{1,0},{2,3},{3,2},{4,5},{5,4},{6,7},{7,6},{8,9},{9,8},{10,11... | collective-permute-start | bytes 393224 | tf_op jit(solution)/shard_map/ppermute | solution.py:77
  3.5 0.1 collective-permute-start.1
  3.6 0.8 %shard_map.66 = (f32[256,512]{1,0:T(8,128)S(1)}, bf16[512,512]{1,0:T(8,128)(2,1)S(1)}, bf16[512,512]{1,0:T(8,128)(2,1)S(1)}) custom-call(f32[4,128]{1,0:T(4,128)S(1)} %get-tuple-element.39.scale_ref, f32[512,256]{1,0:T(8,128)S(1)} %get-tuple-element.40.queries_ref, f32[512,128]{1,0:T(8,128)S(1)} %get-tuple-element.41.leaf_ref, ...), custom_call_target="tpu_custom_call" | custom-call | flops 402653184 | bytes 1574912 | tf_op jit(solution)/shard_map/pallas_call | solution.py:56
  4.4 0.6 %collective-permute-start.4 = (f32[128,512]{1,0:T(8,128)S(1)}, f32[128,512]{1,0:T(8,128)S(1)}, u32[]{:S(2)}, u32[]{:S(2)}) collective-permute-start(f32[128,512]{1,0:T(8,128)S(1)} %slice.54), channel_id=1, source_target_pairs={{0,1},{1,0},{2,3},{3,2},{4,5},{5,4},{6,7},{7,6},{8,9},{9,8},{10,11... | collective-permute-start | bytes 786440 | tf_op jit(solution)/shard_map/ppermute | solution.py:77
  4.9 0.0 collective-permute-done
  5.0 0.1 collective-permute-done.1
  5.2 2.7 %collective-permute-start.2 = (f32[64,384]{1,0:T(8,128)S(1)}, f32[64,384]{1,0:T(8,128)S(1)}, u32[]{:S(2)}, u32[]{:S(2)}) collective-permute-start(f32[64,384]{1,0:T(8,128)S(1)} %slice.60), channel_id=1, source_target_pairs={{0,4},{4,0},{8,12},{12,8},{16,20},{20,16},{24,28},{28,24},{1,5},{5... | collective-permute-start | bytes 294920 | tf_op jit(solution)/shard_map/ppermute | solution.py:77
  7.8 1.5 %collective-permute-start.6 = (f32[64,640]{1,0:T(8,128)S(1)}, f32[64,640]{1,0:T(8,128)S(1)}, u32[]{:S(2)}, u32[]{:S(2)}) collective-permute-start(f32[64,640]{1,0:T(8,128)S(1)} %slice.65), channel_id=1, source_target_pairs={{0,2},{1,3},{2,0},{3,1},{4,6},{5,7},{6,4},{7,5},{8,10},{9,11},{10,... | collective-permute-start | bytes 491528 | tf_op jit(solution)/shard_map/ppermute | solution.py:77
  9.4 0.0 collective-permute-done.4
  9.4 0.6 %collective-permute-start.5 = (f32[64,512]{1,0:T(8,128)S(1)}, f32[64,512]{1,0:T(8,128)S(1)}, u32[]{:S(2)}, u32[]{:S(2)}) collective-permute-start(f32[64,512]{1,0:T(8,128)S(1)} %get-tuple-element.73.refs_0_), channel_id=1, source_target_pairs={{0,2},{1,3},{2,0},{3,1},{4,6},{5,7},{6,4},{7,5},{8,10},{9,11},{10,... | collective-permute-start | bytes 393224 | tf_op jit(solution)/shard_map/ppermute | solution.py:77
  10.0 1.2 %collective-permute-done.2 = f32[64,384]{1,0:T(8,128)S(1)} collective-permute-done((f32[64,384]{1,0:T(8,128)S(1)}, f32[64,384]{1,0:T(8,128)S(1)}, u32[]{:S(2)}, u32[]{:S(2)}) %collective-permute-start.2) | collective-permute-done | bytes 98336 | tf_op jit(solution)/shard_map/ppermute | solution.py:77
  11.2 1.8 %collective-permute-start.11 = (f32[64,256]{1,0:T(8,128)S(1)}, f32[64,256]{1,0:T(8,128)S(1)}, u32[]{:S(2)}, u32[]{:S(2)}) collective-permute-start(f32[64,256]{1,0:T(8,128)S(1)} %constant_dynamic-update-slice_fusion), channel_id=1, source_target_pairs={{0,2},{1,3},{2,0},{3,1},{4,6},{5,7},{6,4},{7,5},{8,10},{9,11},{10,... | collective-permute-start | bytes 196616 | tf_op jit(solution)/shard_map/ppermute | solution.py:77
  13.1 0.3 collective-permute-start.3
  13.4 1.5 %collective-permute-done.6 = f32[64,640]{1,0:T(8,128)S(1)} collective-permute-done((f32[64,640]{1,0:T(8,128)S(1)}, f32[64,640]{1,0:T(8,128)S(1)}, u32[]{:S(2)}, u32[]{:S(2)}) %collective-permute-start.6) | collective-permute-done | bytes 163872 | tf_op jit(solution)/shard_map/ppermute | solution.py:77
  14.9 0.1 collective-permute-start.7
  15.0 4.1 %collective-permute-done.11 = f32[64,256]{1,0:T(8,128)S(1)} collective-permute-done((f32[64,256]{1,0:T(8,128)S(1)}, f32[64,256]{1,0:T(8,128)S(1)}, u32[]{:S(2)}, u32[]{:S(2)}) %collective-permute-start.11) | collective-permute-done | bytes 65568 | tf_op jit(solution)/shard_map/ppermute | solution.py:77
  19.1 0.1 collective-permute-start.12
  19.2 1.6 %collective-permute-start.8 = (f32[64,512]{1,0:T(8,128)S(1)}, f32[64,512]{1,0:T(8,128)S(1)}, u32[]{:S(2)}, u32[]{:S(2)}) collective-permute-start(f32[64,512]{1,0:T(8,128)S(1)} %get-tuple-element.74.refs_0_), channel_id=1, source_target_pairs={{0,2},{1,3},{2,0},{3,1},{4,6},{5,7},{6,4},{7,5},{8,10},{9,11},{10,... | collective-permute-start | bytes 393224 | tf_op jit(solution)/shard_map/ppermute | solution.py:77
  20.8 0.0 collective-permute-done.12.other_ref
  20.8 0.2 shard_map.70
  21.1 0.0 collective-permute-done.7.other_ref
  21.1 0.4 shard_map.67
  21.4 0.0 collective-permute-done.5.refs_1_
  21.4 0.4 shard_map.68
  21.8 0.6 %collective-permute-start.10 = (f32[64,256]{1,0:T(8,128)S(1)}, f32[64,256]{1,0:T(8,128)S(1)}, u32[]{:S(2)}, u32[]{:S(2)}) collective-permute-start(f32[64,256]{1,0:T(8,128)S(1)} %get-tuple-element.54.refs_0_), channel_id=1, source_target_pairs={{0,4},{4,0},{8,12},{12,8},{16,20},{20,16},{24,28},{28,24},{1,5},{5... | collective-permute-start | bytes 196616 | tf_op jit(solution)/shard_map/ppermute | solution.py:77
  22.4 0.0 collective-permute-done.3
  22.4 2.7 %collective-permute-done.8.refs_1_ = f32[64,512]{1,0:T(8,128)S(1)} collective-permute-done((f32[64,512]{1,0:T(8,128)S(1)}, f32[64,512]{1,0:T(8,128)S(1)}, u32[]{:S(2)}, u32[]{:S(2)}) %collective-permute-start.8) | collective-permute-done | bytes 131104 | tf_op jit(solution)/shard_map/ppermute | solution.py:77
  25.1 0.3 shard_map.69
  25.5 0.4 collective-permute-start.15
  25.9 0.3 collective-permute-done.10.refs_1_
  26.1 0.1 shard_map.71
  26.3 1.6 %collective-permute-start.13 = (f32[128,128]{1,0:T(8,128)S(1)}, f32[128,128]{1,0:T(8,128)S(1)}, u32[]{:S(2)}, u32[]{:S(2)}) collective-permute-start(f32[128,128]{1,0:T(8,128)S(1)} %pad_maximum_fusion.3), channel_id=1, source_target_pairs={{0,8},{4,12},{8,0},{12,4},{16,24},{20,28},{24,16},{28,20},{1,9},{5... | collective-permute-start | bytes 196616 | tf_op jit(solution)/shard_map/ppermute | solution.py:77
  28.0 1.9 %collective-permute-done.15.refs_1_ = f32[64,256]{1,0:T(8,128)S(1)} collective-permute-done((f32[64,256]{1,0:T(8,128)S(1)}, f32[64,256]{1,0:T(8,128)S(1)}, u32[]{:S(2)}, u32[]{:S(2)}) %collective-permute-start.15) | collective-permute-done | bytes 65568 | tf_op jit(solution)/shard_map/ppermute | solution.py:77
  29.8 0.1 shard_map.74
  30.0 1.6 %collective-permute-start.16 = (f32[64,128]{1,0:T(8,128)S(1)}, f32[64,128]{1,0:T(8,128)S(1)}, u32[]{:S(2)}, u32[]{:S(2)}) collective-permute-start(f32[64,128]{1,0:T(8,128)S(1)} %get-tuple-element.72), channel_id=1, source_target_pairs={{0,8},{4,12},{8,0},{12,4},{16,24},{20,28},{24,16},{28,20},{1,9},{5... | collective-permute-start | bytes 98312 | tf_op jit(solution)/shard_map/ppermute | solution.py:77
  31.6 0.1 collective-permute-start.9
  31.7 2.2 %collective-permute-done.16 = f32[64,128]{1,0:T(8,128)S(1)} collective-permute-done((f32[64,128]{1,0:T(8,128)S(1)}, f32[64,128]{1,0:T(8,128)S(1)}, u32[]{:S(2)}, u32[]{:S(2)}) %collective-permute-start.16) | collective-permute-done | bytes 32800 | tf_op jit(solution)/shard_map/ppermute | solution.py:77
  33.9 0.0 collective-permute-done.13
  34.0 0.1 collective-permute-start.14
  34.1 0.5 %collective-permute-start.17 = (f32[128,128]{1,0:T(8,128)S(1)}, f32[128,128]{1,0:T(8,128)S(1)}, u32[]{:S(2)}, u32[]{:S(2)}) collective-permute-start(f32[128,128]{1,0:T(8,128)S(1)} %pad_maximum_fusion.4.refs_4_), channel_id=1, source_target_pairs={{0,1},{1,0},{2,3},{3,2},{4,5},{5,4},{6,7},{7,6},{8,9},{9,8},{10,11... | collective-permute-start | bytes 196616 | tf_op jit(solution)/shard_map/ppermute | solution.py:77
  34.6 1.5 %shard_map.73 = (bf16[512,256]{1,0:T(8,128)(2,1)S(1)}, bf16[512,256]{1,0:T(8,128)(2,1)S(1)}) custom-call(bf16[128,384]{1,0:T(8,128)(2,1)S(1)} %get-tuple-element.48.refs_2_.refs_0_, bf16[128,384]{1,0:T(8,128)(2,1)S(1)} %get-tuple-element.49.refs_3_.refs_1_, bf16[128,256]{1,0:T(8,128)(2,1)S(1)} %get-tuple-element.50.refs_4_.refs_2_, ...), custom_call_target="tpu_custom_call" | custom-call | flops 402653184 | bytes 1441792 | tf_op jit(solution)/shard_map/pallas_call | solution.py:56
  36.1 0.0 collective-permute-done.14.other_found_ref.refs_3_
  36.1 0.0 collective-permute-done.9.other_ref
  36.1 1.5 %shard_map.72 = (f32[512,256]{1,0:T(8,128)S(1)}, bf16[128,256]{1,0:T(8,128)(2,1)S(1)}, bf16[128,256]{1,0:T(8,128)(2,1)S(1)}) custom-call(f32[4,128]{1,0:T(4,128)S(1)} %get-tuple-element.39.scale_ref, f32[512,256]{1,0:T(8,128)S(1)} %get-tuple-element.40.queries_ref, f32[576,128]{1,0:T(8,128)S(1)} %pad_maximum_fusion.own_ref, ...), custom_call_target="tpu_custom_call" | custom-call | flops 301989888 | bytes 3213312 | tf_op jit(solution)/shard_map/pallas_call | solution.py:56
  37.6 0.0 collective-permute-done.17.refs_5_
  37.6 1.4 %shard_map.75 = f32[512,256]{1,0:T(8,128)} custom-call(f32[512,256]{1,0:T(8,128)S(1)} %get-tuple-element.65.base_ref, bf16[512,256]{1,0:T(8,128)(2,1)S(1)} %get-tuple-element.66.high_ref, bf16[512,256]{1,0:T(8,128)(2,1)S(1)} %get-tuple-element.67.low_ref, bf16[128,256]{1,0:T(8,128)(2,1)S(1)} %get-tuple-element.68.refs_0_, ...), custom_call_target="tpu_custom_call" | custom-call | flops 201326592 | bytes 1507328 | tf_op jit(solution)/shard_map/pallas_call | solution.py:56
  (24 shorter events, 0.4 us)
Async XLA Ops:
  2.9 2.0 %collective-permute-start = (f32[256,128]{1,0:T(8,128)S(1)}, f32[256,128]{1,0:T(8,128)S(1)}, u32[]{:S(2)}, u32[]{:S(2)}) collective-permute-start(f32[256,128]{1,0:T(8,128)S(1)} %slice.46), channel_id=1, source_target_pairs={{0,1},{1,0},{2,3},{3,2},{4,5},{5,4},{6,7},{7,6},{8,9},{9,8},{10,11... | collective-permute-start | bytes 393224 | tf_op jit(solution)/shard_map/ppermute | solution.py:77
  3.5 1.6 %collective-permute-start.1 = (f32[64,1024]{1,0:T(8,128)S(1)}, f32[64,1024]{1,0:T(8,128)S(1)}, u32[]{:S(2)}, u32[]{:S(2)}) collective-permute-start(f32[64,1024]{1,0:T(8,128)S(1)} %slice.48), channel_id=1, source_target_pairs={{0,1},{1,0},{2,3},{3,2},{4,5},{5,4},{6,7},{7,6},{8,9},{9,8},{10,11... | collective-permute-start | bytes 786440 | tf_op jit(solution)/shard_map/ppermute | solution.py:77
  4.4 5.0 %collective-permute-start.4 = (f32[128,512]{1,0:T(8,128)S(1)}, f32[128,512]{1,0:T(8,128)S(1)}, u32[]{:S(2)}, u32[]{:S(2)}) collective-permute-start(f32[128,512]{1,0:T(8,128)S(1)} %slice.54), channel_id=1, source_target_pairs={{0,1},{1,0},{2,3},{3,2},{4,5},{5,4},{6,7},{7,6},{8,9},{9,8},{10,11... | collective-permute-start | bytes 786440 | tf_op jit(solution)/shard_map/ppermute | solution.py:77
  5.2 6.0 %collective-permute-start.2 = (f32[64,384]{1,0:T(8,128)S(1)}, f32[64,384]{1,0:T(8,128)S(1)}, u32[]{:S(2)}, u32[]{:S(2)}) collective-permute-start(f32[64,384]{1,0:T(8,128)S(1)} %slice.60), channel_id=1, source_target_pairs={{0,4},{4,0},{8,12},{12,8},{16,20},{20,16},{24,28},{28,24},{1,5},{5... | collective-permute-start | bytes 294920 | tf_op jit(solution)/shard_map/ppermute | solution.py:77
  7.8 7.1 %collective-permute-start.6 = (f32[64,640]{1,0:T(8,128)S(1)}, f32[64,640]{1,0:T(8,128)S(1)}, u32[]{:S(2)}, u32[]{:S(2)}) collective-permute-start(f32[64,640]{1,0:T(8,128)S(1)} %slice.65), channel_id=1, source_target_pairs={{0,2},{1,3},{2,0},{3,1},{4,6},{5,7},{6,4},{7,5},{8,10},{9,11},{10,... | collective-permute-start | bytes 491528 | tf_op jit(solution)/shard_map/ppermute | solution.py:77
  9.4 12.0 %collective-permute-start.5 = (f32[64,512]{1,0:T(8,128)S(1)}, f32[64,512]{1,0:T(8,128)S(1)}, u32[]{:S(2)}, u32[]{:S(2)}) collective-permute-start(f32[64,512]{1,0:T(8,128)S(1)} %get-tuple-element.73.refs_0_), channel_id=1, source_target_pairs={{0,2},{1,3},{2,0},{3,1},{4,6},{5,7},{6,4},{7,5},{8,10},{9,11},{10,... | collective-permute-start | bytes 393224 | tf_op jit(solution)/shard_map/ppermute | solution.py:77
  11.2 7.9 %collective-permute-start.11 = (f32[64,256]{1,0:T(8,128)S(1)}, f32[64,256]{1,0:T(8,128)S(1)}, u32[]{:S(2)}, u32[]{:S(2)}) collective-permute-start(f32[64,256]{1,0:T(8,128)S(1)} %constant_dynamic-update-slice_fusion), channel_id=1, source_target_pairs={{0,2},{1,3},{2,0},{3,1},{4,6},{5,7},{6,4},{7,5},{8,10},{9,11},{10,... | collective-permute-start | bytes 196616 | tf_op jit(solution)/shard_map/ppermute | solution.py:77
  13.1 9.3 %collective-permute-start.3 = (f32[320,128]{1,0:T(8,128)S(1)}, f32[320,128]{1,0:T(8,128)S(1)}, u32[]{:S(2)}, u32[]{:S(2)}) collective-permute-start(f32[320,128]{1,0:T(8,128)S(1)} %pad_maximum_fusion.1), channel_id=1, source_target_pairs={{0,2},{1,3},{2,0},{3,1},{4,6},{5,7},{6,4},{7,5},{8,10},{9,11},{10,... | collective-permute-start | bytes 491528 | tf_op jit(solution)/shard_map/ppermute | solution.py:77
  14.9 6.1 %collective-permute-start.7 = (f32[64,640]{1,0:T(8,128)S(1)}, f32[64,640]{1,0:T(8,128)S(1)}, u32[]{:S(2)}, u32[]{:S(2)}) collective-permute-start(f32[64,640]{1,0:T(8,128)S(1)} %slice_add_fusion.4.own_ref), channel_id=1, source_target_pairs={{0,1},{1,0},{2,3},{3,2},{4,5},{5,4},{6,7},{7,6},{8,9},{9,8},{10,11... | collective-permute-start | bytes 491528 | tf_op jit(solution)/shard_map/ppermute | solution.py:77
  19.1 1.7 %collective-permute-start.12 = (f32[64,128]{1,0:T(8,128)S(1)}, f32[64,128]{1,0:T(8,128)S(1)}, u32[]{:S(2)}, u32[]{:S(2)}) collective-permute-start(f32[64,128]{1,0:T(8,128)S(1)} %get-tuple-element.78.own_ref), channel_id=1, source_target_pairs={{0,1},{1,0},{2,3},{3,2},{4,5},{5,4},{6,7},{7,6},{8,9},{9,8},{10,11... | collective-permute-start | bytes 98312 | tf_op jit(solution)/shard_map/ppermute | solution.py:77
  19.2 5.9 %collective-permute-start.8 = (f32[64,512]{1,0:T(8,128)S(1)}, f32[64,512]{1,0:T(8,128)S(1)}, u32[]{:S(2)}, u32[]{:S(2)}) collective-permute-start(f32[64,512]{1,0:T(8,128)S(1)} %get-tuple-element.74.refs_0_), channel_id=1, source_target_pairs={{0,2},{1,3},{2,0},{3,1},{4,6},{5,7},{6,4},{7,5},{8,10},{9,11},{10,... | collective-permute-start | bytes 393224 | tf_op jit(solution)/shard_map/ppermute | solution.py:77
  21.8 4.3 %collective-permute-start.10 = (f32[64,256]{1,0:T(8,128)S(1)}, f32[64,256]{1,0:T(8,128)S(1)}, u32[]{:S(2)}, u32[]{:S(2)}) collective-permute-start(f32[64,256]{1,0:T(8,128)S(1)} %get-tuple-element.54.refs_0_), channel_id=1, source_target_pairs={{0,4},{4,0},{8,12},{12,8},{16,20},{20,16},{24,28},{28,24},{1,5},{5... | collective-permute-start | bytes 196616 | tf_op jit(solution)/shard_map/ppermute | solution.py:77
  25.5 4.3 %collective-permute-start.15 = (f32[64,256]{1,0:T(8,128)S(1)}, f32[64,256]{1,0:T(8,128)S(1)}, u32[]{:S(2)}, u32[]{:S(2)}) collective-permute-start(f32[64,256]{1,0:T(8,128)S(1)} %get-tuple-element.70.refs_0_), channel_id=1, source_target_pairs={{0,4},{4,0},{8,12},{12,8},{16,20},{20,16},{24,28},{28,24},{1,5},{5... | collective-permute-start | bytes 196616 | tf_op jit(solution)/shard_map/ppermute | solution.py:77
  26.3 7.6 %collective-permute-start.13 = (f32[128,128]{1,0:T(8,128)S(1)}, f32[128,128]{1,0:T(8,128)S(1)}, u32[]{:S(2)}, u32[]{:S(2)}) collective-permute-start(f32[128,128]{1,0:T(8,128)S(1)} %pad_maximum_fusion.3), channel_id=1, source_target_pairs={{0,8},{4,12},{8,0},{12,4},{16,24},{20,28},{24,16},{28,20},{1,9},{5... | collective-permute-start | bytes 196616 | tf_op jit(solution)/shard_map/ppermute | solution.py:77
  30.0 4.0 %collective-permute-start.16 = (f32[64,128]{1,0:T(8,128)S(1)}, f32[64,128]{1,0:T(8,128)S(1)}, u32[]{:S(2)}, u32[]{:S(2)}) collective-permute-start(f32[64,128]{1,0:T(8,128)S(1)} %get-tuple-element.72), channel_id=1, source_target_pairs={{0,8},{4,12},{8,0},{12,4},{16,24},{20,28},{24,16},{28,20},{1,9},{5... | collective-permute-start | bytes 98312 | tf_op jit(solution)/shard_map/ppermute | solution.py:77
  31.6 4.4 %collective-permute-start.9 = (f32[576,128]{1,0:T(8,128)S(1)}, f32[576,128]{1,0:T(8,128)S(1)}, u32[]{:S(2)}, u32[]{:S(2)}) collective-permute-start(f32[576,128]{1,0:T(8,128)S(1)} %pad_maximum_fusion.own_ref), channel_id=1, source_target_pairs={{0,1},{1,0},{2,3},{3,2},{4,5},{5,4},{6,7},{7,6},{8,9},{9,8},{10,11... | collective-permute-start | bytes 884744 | tf_op jit(solution)/shard_map/ppermute | solution.py:77
  34.0 2.1 %collective-permute-start.14 = (f32[192,128]{1,0:T(8,128)S(1)}, f32[192,128]{1,0:T(8,128)S(1)}, u32[]{:S(2)}, u32[]{:S(2)}) collective-permute-start(f32[192,128]{1,0:T(8,128)S(1)} %pad_maximum_fusion.2.own_found_ref.refs_2_), channel_id=1, source_target_pairs={{0,1},{1,0},{2,3},{3,2},{4,5},{5,4},{6,7},{7,6},{8,9},{9,8},{10,11... | collective-permute-start | bytes 294920 | tf_op jit(solution)/shard_map/ppermute | solution.py:77
  34.1 3.5 %collective-permute-start.17 = (f32[128,128]{1,0:T(8,128)S(1)}, f32[128,128]{1,0:T(8,128)S(1)}, u32[]{:S(2)}, u32[]{:S(2)}) collective-permute-start(f32[128,128]{1,0:T(8,128)S(1)} %pad_maximum_fusion.4.refs_4_), channel_id=1, source_target_pairs={{0,1},{1,0},{2,3},{3,2},{4,5},{5,4},{6,7},{7,6},{8,9},{9,8},{10,11... | collective-permute-start | bytes 196616 | tf_op jit(solution)/shard_map/ppermute | solution.py:77

commit v4 on v3

--- a/solution.py
+++ b/solution.py
@@ -322,44 +322,62 @@
 
     def answer_body(*refs):
         factor_refs, basis_refs, out_refs = paired(refs[:-4]), refs[-4:-2], refs[-2:]
-        rows = {}
-        for f in reversed(range(count)):
-            if f + 1 < count:
-                stack = jnp.concatenate([rows[g] for g in range(f + 1, count)], axis=0)
-                row = -dot_parts(take(factor_refs[f], 0, stack.shape[0]), halves(stack))
-            else:
-                row = jnp.zeros((rank, coarse * rank), FLOAT)
-            if f >= head:
-                line = lax.broadcasted_iota(jnp.int32, row.shape, 0) + (f - head) * rank
-                row = row + jnp.where(line == lax.broadcasted_iota(jnp.int32, row.shape, 1), 1.0, 0.0)
-            rows[f] = row
-        gains = jnp.concatenate([rows[f] for f in range(count)], axis=0)
+        shape = (coarse * rank, coarse * rank)
+        line, column = (lax.broadcasted_iota(jnp.int32, shape, i) for i in range(2))
+        gains = jnp.where(line == column, 1.0, 0.0)
+        for f in reversed(range(head)):
+            row = -dot_parts(take(factor_refs[f], 0, gains.shape[0]), halves(gains))
+            gains = jnp.concatenate([row, gains], axis=0)
         store(out_refs, dot_parts([ref[...] for ref in basis_refs], halves(gains)))
 
     answer = call(
         answer_body,
         pair(rows_here, coarse * rank),
-        *flat(factors),
+        *flat(factors[:head]),
         *basis,
         flops=small * coarse * count * rows_here // rank,
     )
 
-    def base_body(scale_ref, queries_ref, own_ref, other_ref, own_found_ref, other_found_ref, core_ref, *refs):
-        factor_refs, basis_refs, scaled_refs = paired(refs[: 2 * head]), refs[2 * head : -7], refs[-7:-5]
-        out_ref, *gain_refs, stack_ref, gram_ref = refs[-5:]
+    def gain_body(own_ref, other_ref, own_found_ref, other_found_ref, core_ref, *refs):
+        out_refs, gram_ref = refs[:2], refs[2]
+        side = core_side()
+        sources = ((own_ref, own_found_ref, side), (other_ref, other_found_ref, 1 - side))
+        for late_ref, found_ref, place in sources:
+            gram_ref[at(place, half), (coarse - 1) * rank :] = found_ref[coarse * batch :]
+            for e in range(head, top):
+                start = columns // 2 + e * half
+                where = slice((e - head) * rank, (e - head + 1) * rank)
+                gram_ref[at(place, half), where] = late_ref[start : start + half]
+        gains = []
+        for e in range(head, count):
+            core = core_ref[e]
+            gram = gram_ref[:, (e - head) * rank : (e - head + 1) * rank]
+            gains.append(core + core.T - dot(dot(core.T, gram), core))
+        store(out_refs, lanes(gains))
+
+    gains = call(
+        gain_body,
+        pair(rank, coarse * rank),
+        *late_parts,
+        *found_parts[0],
+        cores,
+        flops=small * 2 * coarse,
+        scratch=[pltpu.VMEM((rank, coarse * rank), FLOAT)],
+    )
+
+    def base_body(scale_ref, queries_ref, own_ref, other_ref, core_ref, *refs):
+        factor_refs, basis_refs, scaled_refs = paired(refs[: 2 * head]), refs[2 * head : -5], refs[-5:-3]
+        out_ref, stack_ref, gram_ref = refs[-3:]
         pieces = [pl.ds(late_size + b * head * batch, head * batch) for b in range(batches)]
         scatter([(own_ref.at[piece], other_ref.at[piece]) for piece in pieces], head, stack_ref)
         side = core_side()
-        sources = ((own_ref, own_found_ref, side), (other_ref, other_found_ref, 1 - side))
-        for late_ref, found_ref, place in sources:
+        for late_ref, place in ((own_ref, side), (other_ref, 1 - side)):
             stack_ref[at(place, columns // 2), head * rank :] = late_ref[: columns // 2]
-            gram_ref[at(place, half), top * rank :] = found_ref[coarse * batch :]
-            for e in range(top):
+            for e in range(head):
                 start = columns // 2 + e * half
                 gram_ref[at(place, half), e * rank : (e + 1) * rank] = late_ref[start : start + half]
-        products = [dot(core_ref[e].T, gram_ref[:, e * rank : (e + 1) * rank]) for e in range(count)]
-        gains = [core_ref[e] + core_ref[e].T - dot(products[e], core_ref[e]) for e in range(1, count)]
-        store(gain_refs, lanes(gains[head - 1 :]))
+        products = [dot(core_ref[e].T, gram_ref[:, e * rank : (e + 1) * rank]) for e in range(head)]
+        gains = [core_ref[e] + core_ref[e].T - dot(products[e], core_ref[e]) for e in range(1, head)]
         moments = [stack_ref[:, e * rank : (e + 1) * rank] for e in range(head)]
         first = dot(moments[0], core_ref[0], 1)
         found = [dot(stack_ref[:, head * rank :], core_ref[0]) - dot(first, products[0], 1)]
@@ -372,29 +390,32 @@
         square = lanes([square] * (columns // rank))
         out_ref[...] = square * queries_ref[...] - dot_parts(left, halves(lanes([first, *found])), 1)
 
-    base, *gains = call(
+    (base,) = call(
         base_body,
-        [(rows_here, columns), *pair(rank, coarse * rank)],
+        [(rows_here, columns)],
         scale,
         queries,
         *late_parts,
-        *found_parts[0],
         cores,
         *flat(factors[:head]),
         *basis,
         *scaled,
         flops=small * 2 * (head + 1) * rows_here // rank,
-        scratch=[pltpu.VMEM((columns, (head + 1) * rank), FLOAT), pltpu.VMEM((rank, count * rank), FLOAT)],
+        scratch=[pltpu.VMEM((columns, (head + 1) * rank), FLOAT), pltpu.VMEM((rank, head * rank), FLOAT)],
     )
 
     def last_body(base_ref, high_ref, low_ref, *refs):
-        gain_refs, part_refs, (out_ref, stack_ref) = refs[:2], paired(refs[2:-2]), refs[-2:]
+        gain_refs, (out_ref, stack_ref) = refs[:2], refs[-2:]
+        part_refs, factor_refs = paired(refs[2 : 2 + 2 * batches]), paired(refs[2 + 2 * batches : -2])
         scatter(part_refs, coarse, stack_ref)
-        right = []
-        for e in range(coarse):
+        found = []
+        for e in reversed(range(coarse)):
             where = slice(e * rank, (e + 1) * rank)
-            right.append(dot_parts(halves(stack_ref[:, where]), [ref[:, where] for ref in gain_refs], 1))
-        out_ref[...] = base_ref[...] - dot_parts([high_ref[...], low_ref[...]], halves(lanes(right)), 1)
+            value = dot_parts(halves(stack_ref[:, where]), [ref[:, where] for ref in gain_refs], 1)
+            if found:
+                value = value - dot_parts(halves(lanes(found)), [ref[...] for ref in factor_refs[e]], 1)
+            found.insert(0, value)
+        out_ref[...] = base_ref[...] - dot_parts([high_ref[...], low_ref[...]], halves(lanes(found)), 1)
 
     (out,) = call(
         last_body,
@@ -403,6 +424,7 @@
         *answer,
         *gains,
         *flat(found_parts),
+        *flat(factors[head:]),
         flops=small * 2 * coarse * rows_here // rank,
         scratch=[pltpu.VMEM((columns, coarse * rank), FLOAT)],
     )

time: 39.2 us -> 39.5 us (level)
    pallas_call x12 -> x13, Pallas kernels: 9.62 us -> 9.99 us  [call(): pl.pallas_call(body, out_shape=outs, in_specs=[pl.BlockSpec(memory_space=...]
where the time goes in v4:
time: 39.5 us; the launch traced here: 39.4 us
  starting transfers between devices  14.7 us (37%)
  waiting for transfers between devices  14 us (35%)
  Pallas kernels  9.99 us (25%)
    ppermute x18, starting transfers between devices, swap(): lax.ppermute(array, axis, [(i, i ^ 1 << bit) for i in range(lax.axis_size...  14.7 us
    ppermute x18, waiting for transfers between devices, swap(): lax.ppermute(array, axis, [(i, i ^ 1 << bit) for i in range(lax.axis_size...  14 us
    pallas_call x13, Pallas kernels, call(): pl.pallas_call(body, out_shape=outs, in_specs=[pl.BlockSpec(memory_space=...  9.99 us
  transfers between devices with their start and end apart: 18, of which 8 were waited for; matrix products, arithmetic and copies ran while one was open for 1% of the time, Pallas kernels for 14%

profile of v4, /device:TPU:0, one launch (start us, length us, event | category | flops | bytes accessed | tf_op | source)
XLA Modules:
  0.0 39.4 jit_solution(15518527307978412284)
XLA Ops:
  0.0 2.1 %shard_map.64 = (f32[128,1024]{1,0:T(8,128)S(1)}, f32[4,128]{1,0:T(4,128)S(1)}, f32[512,128]{1,0:T(8,128)S(1)}, f32[3,512,128]{2,1,0:T(8,128)S(1)}, f32[512,256]{1,0:T(8,128)S(1)}, /*index=5*/f32[4,128,128]{2,1,0:T(8,128)S(1)}) custom-call(f32[4,128]{1,0:T(4,128)} %bitcast.1, f32[512,128]{1,0:T(8,128)} %refs_1_.1, f32[3,512,128]{2,1,0:T(8,128)} %refs_2_.1, ...), custom_call_target="tpu_custom_call" | custom-call | flops 402653184 | bytes 2557952 | tf_op jit(solution)/shard_map/pallas_call | solution.py:56
  2.1 0.8 %shard_map.65 = (f32[512,128]{1,0:T(8,128)S(1)}, bf16[512,128]{1,0:T(8,128)(2,1)S(1)}, bf16[512,128]{1,0:T(8,128)(2,1)S(1)}) custom-call(f32[4,128]{1,0:T(4,128)S(1)} %get-tuple-element.38.scale_ref, f32[512,256]{1,0:T(8,128)S(1)} %get-tuple-element.39.queries_ref, f32[512,128]{1,0:T(8,128)S(1)} %get-tuple-element.40.leaf_ref, ...), custom_call_target="tpu_custom_call" | custom-call | flops 201326592 | bytes 1574912 | tf_op jit(solution)/shard_map/pallas_call | solution.py:56
  2.9 0.6 %collective-permute-start = (f32[256,128]{1,0:T(8,128)S(1)}, f32[256,128]{1,0:T(8,128)S(1)}, u32[]{:S(2)}, u32[]{:S(2)}) collective-permute-start(f32[256,128]{1,0:T(8,128)S(1)} %slice.46), channel_id=1, source_target_pairs={{0,1},{1,0},{2,3},{3,2},{4,5},{5,4},{6,7},{7,6},{8,9},{9,8},{10,11... | collective-permute-start | bytes 393224 | tf_op jit(solution)/shard_map/ppermute | solution.py:77
  3.5 0.1 collective-permute-start.1
  3.6 0.8 %shard_map.66 = (f32[256,512]{1,0:T(8,128)S(1)}, bf16[512,512]{1,0:T(8,128)(2,1)S(1)}, bf16[512,512]{1,0:T(8,128)(2,1)S(1)}) custom-call(f32[4,128]{1,0:T(4,128)S(1)} %get-tuple-element.38.scale_ref, f32[512,256]{1,0:T(8,128)S(1)} %get-tuple-element.39.queries_ref, f32[512,128]{1,0:T(8,128)S(1)} %get-tuple-element.40.leaf_ref, ...), custom_call_target="tpu_custom_call" | custom-call | flops 402653184 | bytes 1574912 | tf_op jit(solution)/shard_map/pallas_call | solution.py:56
  4.4 0.6 %collective-permute-start.4 = (f32[128,512]{1,0:T(8,128)S(1)}, f32[128,512]{1,0:T(8,128)S(1)}, u32[]{:S(2)}, u32[]{:S(2)}) collective-permute-start(f32[128,512]{1,0:T(8,128)S(1)} %slice.54), channel_id=1, source_target_pairs={{0,1},{1,0},{2,3},{3,2},{4,5},{5,4},{6,7},{7,6},{8,9},{9,8},{10,11... | collective-permute-start | bytes 786440 | tf_op jit(solution)/shard_map/ppermute | solution.py:77
  4.9 0.0 collective-permute-done
  5.0 0.1 collective-permute-done.1
  5.2 2.7 %collective-permute-start.2 = (f32[64,384]{1,0:T(8,128)S(1)}, f32[64,384]{1,0:T(8,128)S(1)}, u32[]{:S(2)}, u32[]{:S(2)}) collective-permute-start(f32[64,384]{1,0:T(8,128)S(1)} %slice.60), channel_id=1, source_target_pairs={{0,4},{4,0},{8,12},{12,8},{16,20},{20,16},{24,28},{28,24},{1,5},{5... | collective-permute-start | bytes 294920 | tf_op jit(solution)/shard_map/ppermute | solution.py:77
  7.8 1.5 %collective-permute-start.6 = (f32[64,640]{1,0:T(8,128)S(1)}, f32[64,640]{1,0:T(8,128)S(1)}, u32[]{:S(2)}, u32[]{:S(2)}) collective-permute-start(f32[64,640]{1,0:T(8,128)S(1)} %slice.65), channel_id=1, source_target_pairs={{0,2},{1,3},{2,0},{3,1},{4,6},{5,7},{6,4},{7,5},{8,10},{9,11},{10,... | collective-permute-start | bytes 491528 | tf_op jit(solution)/shard_map/ppermute | solution.py:77
  9.4 0.0 collective-permute-done.4
  9.4 0.6 %collective-permute-start.5 = (f32[64,512]{1,0:T(8,128)S(1)}, f32[64,512]{1,0:T(8,128)S(1)}, u32[]{:S(2)}, u32[]{:S(2)}) collective-permute-start(f32[64,512]{1,0:T(8,128)S(1)} %get-tuple-element.71.refs_0_), channel_id=1, source_target_pairs={{0,2},{1,3},{2,0},{3,1},{4,6},{5,7},{6,4},{7,5},{8,10},{9,11},{10,... | collective-permute-start | bytes 393224 | tf_op jit(solution)/shard_map/ppermute | solution.py:77
  10.0 1.2 %collective-permute-done.2 = f32[64,384]{1,0:T(8,128)S(1)} collective-permute-done((f32[64,384]{1,0:T(8,128)S(1)}, f32[64,384]{1,0:T(8,128)S(1)}, u32[]{:S(2)}, u32[]{:S(2)}) %collective-permute-start.2) | collective-permute-done | bytes 98336 | tf_op jit(solution)/shard_map/ppermute | solution.py:77
  11.2 1.8 %collective-permute-start.11 = (f32[64,256]{1,0:T(8,128)S(1)}, f32[64,256]{1,0:T(8,128)S(1)}, u32[]{:S(2)}, u32[]{:S(2)}) collective-permute-start(f32[64,256]{1,0:T(8,128)S(1)} %constant_dynamic-update-slice_fusion), channel_id=1, source_target_pairs={{0,2},{1,3},{2,0},{3,1},{4,6},{5,7},{6,4},{7,5},{8,10},{9,11},{10,... | collective-permute-start | bytes 196616 | tf_op jit(solution)/shard_map/ppermute | solution.py:77
  13.1 0.3 collective-permute-start.3
  13.4 1.5 %collective-permute-done.6 = f32[64,640]{1,0:T(8,128)S(1)} collective-permute-done((f32[64,640]{1,0:T(8,128)S(1)}, f32[64,640]{1,0:T(8,128)S(1)}, u32[]{:S(2)}, u32[]{:S(2)}) %collective-permute-start.6) | collective-permute-done | bytes 163872 | tf_op jit(solution)/shard_map/ppermute | solution.py:77
  14.9 0.1 collective-permute-start.7
  15.0 4.1 %collective-permute-done.11 = f32[64,256]{1,0:T(8,128)S(1)} collective-permute-done((f32[64,256]{1,0:T(8,128)S(1)}, f32[64,256]{1,0:T(8,128)S(1)}, u32[]{:S(2)}, u32[]{:S(2)}) %collective-permute-start.11) | collective-permute-done | bytes 65568 | tf_op jit(solution)/shard_map/ppermute | solution.py:77
  19.2 0.1 collective-permute-start.12
  19.2 1.6 %collective-permute-start.8 = (f32[64,512]{1,0:T(8,128)S(1)}, f32[64,512]{1,0:T(8,128)S(1)}, u32[]{:S(2)}, u32[]{:S(2)}) collective-permute-start(f32[64,512]{1,0:T(8,128)S(1)} %get-tuple-element.72.refs_0_), channel_id=1, source_target_pairs={{0,2},{1,3},{2,0},{3,1},{4,6},{5,7},{6,4},{7,5},{8,10},{9,11},{10,... | collective-permute-start | bytes 393224 | tf_op jit(solution)/shard_map/ppermute | solution.py:77
  20.8 0.0 collective-permute-done.12.other_ref
  20.8 0.2 shard_map.72
  21.1 0.0 collective-permute-done.7.other_ref
  21.1 0.4 shard_map.67
  21.4 0.0 collective-permute-done.5.refs_1_
  21.5 0.4 shard_map.68
  21.8 0.6 %collective-permute-start.10 = (f32[64,256]{1,0:T(8,128)S(1)}, f32[64,256]{1,0:T(8,128)S(1)}, u32[]{:S(2)}, u32[]{:S(2)}) collective-permute-start(f32[64,256]{1,0:T(8,128)S(1)} %get-tuple-element.59.refs_0_), channel_id=1, source_target_pairs={{0,4},{4,0},{8,12},{12,8},{16,20},{20,16},{24,28},{28,24},{1,5},{5... | collective-permute-start | bytes 196616 | tf_op jit(solution)/shard_map/ppermute | solution.py:77
  22.4 0.0 collective-permute-done.3
  22.4 2.7 %collective-permute-done.8.refs_1_ = f32[64,512]{1,0:T(8,128)S(1)} collective-permute-done((f32[64,512]{1,0:T(8,128)S(1)}, f32[64,512]{1,0:T(8,128)S(1)}, u32[]{:S(2)}, u32[]{:S(2)}) %collective-permute-start.8) | collective-permute-done | bytes 131104 | tf_op jit(solution)/shard_map/ppermute | solution.py:77
  25.1 0.4 shard_map.69
  25.5 0.4 collective-permute-start.15
  25.9 0.3 collective-permute-done.10.refs_1_
  26.1 0.1 shard_map.73
  26.3 1.7 %collective-permute-start.13 = (f32[128,128]{1,0:T(8,128)S(1)}, f32[128,128]{1,0:T(8,128)S(1)}, u32[]{:S(2)}, u32[]{:S(2)}) collective-permute-start(f32[128,128]{1,0:T(8,128)S(1)} %pad_maximum_fusion.3), channel_id=1, source_target_pairs={{0,8},{4,12},{8,0},{12,4},{16,24},{20,28},{24,16},{28,20},{1,9},{5... | collective-permute-start | bytes 196616 | tf_op jit(solution)/shard_map/ppermute | solution.py:77
  28.0 1.9 %collective-permute-done.15.refs_1_ = f32[64,256]{1,0:T(8,128)S(1)} collective-permute-done((f32[64,256]{1,0:T(8,128)S(1)}, f32[64,256]{1,0:T(8,128)S(1)}, u32[]{:S(2)}, u32[]{:S(2)}) %collective-permute-start.15) | collective-permute-done | bytes 65568 | tf_op jit(solution)/shard_map/ppermute | solution.py:77
  29.8 0.1 shard_map.75
  30.0 1.6 %collective-permute-start.16 = (f32[64,128]{1,0:T(8,128)S(1)}, f32[64,128]{1,0:T(8,128)S(1)}, u32[]{:S(2)}, u32[]{:S(2)}) collective-permute-start(f32[64,128]{1,0:T(8,128)S(1)} %get-tuple-element.70), channel_id=1, source_target_pairs={{0,8},{4,12},{8,0},{12,4},{16,24},{20,28},{24,16},{28,20},{1,9},{5... | collective-permute-start | bytes 98312 | tf_op jit(solution)/shard_map/ppermute | solution.py:77
  31.6 0.1 collective-permute-start.9
  31.7 2.2 %collective-permute-done.16 = f32[64,128]{1,0:T(8,128)S(1)} collective-permute-done((f32[64,128]{1,0:T(8,128)S(1)}, f32[64,128]{1,0:T(8,128)S(1)}, u32[]{:S(2)}, u32[]{:S(2)}) %collective-permute-start.16) | collective-permute-done | bytes 32800 | tf_op jit(solution)/shard_map/ppermute | solution.py:77
  34.0 0.0 collective-permute-done.13
  34.0 0.1 collective-permute-start.14
  34.1 0.5 %collective-permute-start.17 = (f32[128,128]{1,0:T(8,128)S(1)}, f32[128,128]{1,0:T(8,128)S(1)}, u32[]{:S(2)}, u32[]{:S(2)}) collective-permute-start(f32[128,128]{1,0:T(8,128)S(1)} %pad_maximum_fusion.4.refs_4_), channel_id=1, source_target_pairs={{0,1},{1,0},{2,3},{3,2},{4,5},{5,4},{6,7},{7,6},{8,9},{9,8},{10,11... | collective-permute-start | bytes 196616 | tf_op jit(solution)/shard_map/ppermute | solution.py:77
  34.6 1.2 %shard_map.71 = (bf16[512,256]{1,0:T(8,128)(2,1)S(1)}, bf16[512,256]{1,0:T(8,128)(2,1)S(1)}) custom-call(bf16[128,384]{1,0:T(8,128)(2,1)S(1)} %get-tuple-element.47.refs_2_.refs_0_, bf16[128,384]{1,0:T(8,128)(2,1)S(1)} %get-tuple-element.48.refs_3_.refs_1_, bf16[128,256]{1,0:T(8,128)(2,1)S(1)} %get-tuple-element.49.refs_4_.refs_2_, ...), custom_call_target="tpu_custom_call" | custom-call | flops 402653184 | bytes 1376256 | tf_op jit(solution)/shard_map/pallas_call | solution.py:56
  35.8 0.0 collective-permute-done.14.other_found_ref.refs_3_
  35.8 0.0 collective-permute-done.9.other_ref
  35.8 0.5 %shard_map.74 = (bf16[128,256]{1,0:T(8,128)(2,1)S(1)}, bf16[128,256]{1,0:T(8,128)(2,1)S(1)}) custom-call(f32[576,128]{1,0:T(8,128)S(1)} %pad_maximum_fusion.own_ref, f32[576,128]{1,0:T(8,128)S(1)} %collective-permute-done.9.other_ref, f32[192,128]{1,0:T(8,128)S(1)} %pad_maximum_fusion.2.own_found_ref.refs_2_, ...), custom_call_target="tpu_custom_call" | custom-call | flops 50331648 | bytes 1048576 | tf_op jit(solution)/shard_map/pallas_call | solution.py:56
  36.3 1.4 %shard_map.70.base_ref = f32[512,256]{1,0:T(8,128)S(1)} custom-call(f32[4,128]{1,0:T(4,128)S(1)} %get-tuple-element.38.scale_ref, f32[512,256]{1,0:T(8,128)S(1)} %get-tuple-element.39.queries_ref, f32[576,128]{1,0:T(8,128)S(1)} %pad_maximum_fusion.own_ref, f32[576,128]{1,0:T(8,128)S(1)} %collective-permute-done.9.other_ref, ...), custom_call_target="tpu_custom_call" | custom-call | flops 301989888 | bytes 3016704 | tf_op jit(solution)/shard_map/pallas_call | solution.py:56
  37.7 0.0 collective-permute-done.17.refs_5_
  37.7 1.7 %shard_map.76 = f32[512,256]{1,0:T(8,128)} custom-call(f32[512,256]{1,0:T(8,128)S(1)} %shard_map.70.base_ref, bf16[512,256]{1,0:T(8,128)(2,1)S(1)} %get-tuple-element.57.high_ref, bf16[512,256]{1,0:T(8,128)(2,1)S(1)} %get-tuple-element.58.low_ref, bf16[128,256]{1,0:T(8,128)(2,1)S(1)} %get-tuple-element.66.refs_0_, ...), custom_call_target="tpu_custom_call" | custom-call | flops 201326592 | bytes 1572864 | tf_op jit(solution)/shard_map/pallas_call | solution.py:56
  (24 shorter events, 0.4 us)
Async XLA Ops:
  2.9 2.0 %collective-permute-start = (f32[256,128]{1,0:T(8,128)S(1)}, f32[256,128]{1,0:T(8,128)S(1)}, u32[]{:S(2)}, u32[]{:S(2)}) collective-permute-start(f32[256,128]{1,0:T(8,128)S(1)} %slice.46), channel_id=1, source_target_pairs={{0,1},{1,0},{2,3},{3,2},{4,5},{5,4},{6,7},{7,6},{8,9},{9,8},{10,11... | collective-permute-start | bytes 393224 | tf_op jit(solution)/shard_map/ppermute | solution.py:77
  3.5 1.6 %collective-permute-start.1 = (f32[64,1024]{1,0:T(8,128)S(1)}, f32[64,1024]{1,0:T(8,128)S(1)}, u32[]{:S(2)}, u32[]{:S(2)}) collective-permute-start(f32[64,1024]{1,0:T(8,128)S(1)} %slice.48), channel_id=1, source_target_pairs={{0,1},{1,0},{2,3},{3,2},{4,5},{5,4},{6,7},{7,6},{8,9},{9,8},{10,11... | collective-permute-start | bytes 786440 | tf_op jit(solution)/shard_map/ppermute | solution.py:77
  4.4 5.0 %collective-permute-start.4 = (f32[128,512]{1,0:T(8,128)S(1)}, f32[128,512]{1,0:T(8,128)S(1)}, u32[]{:S(2)}, u32[]{:S(2)}) collective-permute-start(f32[128,512]{1,0:T(8,128)S(1)} %slice.54), channel_id=1, source_target_pairs={{0,1},{1,0},{2,3},{3,2},{4,5},{5,4},{6,7},{7,6},{8,9},{9,8},{10,11... | collective-permute-start | bytes 786440 | tf_op jit(solution)/shard_map/ppermute | solution.py:77
  5.2 6.0 %collective-permute-start.2 = (f32[64,384]{1,0:T(8,128)S(1)}, f32[64,384]{1,0:T(8,128)S(1)}, u32[]{:S(2)}, u32[]{:S(2)}) collective-permute-start(f32[64,384]{1,0:T(8,128)S(1)} %slice.60), channel_id=1, source_target_pairs={{0,4},{4,0},{8,12},{12,8},{16,20},{20,16},{24,28},{28,24},{1,5},{5... | collective-permute-start | bytes 294920 | tf_op jit(solution)/shard_map/ppermute | solution.py:77
  7.8 7.1 %collective-permute-start.6 = (f32[64,640]{1,0:T(8,128)S(1)}, f32[64,640]{1,0:T(8,128)S(1)}, u32[]{:S(2)}, u32[]{:S(2)}) collective-permute-start(f32[64,640]{1,0:T(8,128)S(1)} %slice.65), channel_id=1, source_target_pairs={{0,2},{1,3},{2,0},{3,1},{4,6},{5,7},{6,4},{7,5},{8,10},{9,11},{10,... | collective-permute-start | bytes 491528 | tf_op jit(solution)/shard_map/ppermute | solution.py:77
  9.4 12.0 %collective-permute-start.5 = (f32[64,512]{1,0:T(8,128)S(1)}, f32[64,512]{1,0:T(8,128)S(1)}, u32[]{:S(2)}, u32[]{:S(2)}) collective-permute-start(f32[64,512]{1,0:T(8,128)S(1)} %get-tuple-element.71.refs_0_), channel_id=1, source_target_pairs={{0,2},{1,3},{2,0},{3,1},{4,6},{5,7},{6,4},{7,5},{8,10},{9,11},{10,... | collective-permute-start | bytes 393224 | tf_op jit(solution)/shard_map/ppermute | solution.py:77
  11.2 7.9 %collective-permute-start.11 = (f32[64,256]{1,0:T(8,128)S(1)}, f32[64,256]{1,0:T(8,128)S(1)}, u32[]{:S(2)}, u32[]{:S(2)}) collective-permute-start(f32[64,256]{1,0:T(8,128)S(1)} %constant_dynamic-update-slice_fusion), channel_id=1, source_target_pairs={{0,2},{1,3},{2,0},{3,1},{4,6},{5,7},{6,4},{7,5},{8,10},{9,11},{10,... | collective-permute-start | bytes 196616 | tf_op jit(solution)/shard_map/ppermute | solution.py:77
  13.1 9.3 %collective-permute-start.3 = (f32[320,128]{1,0:T(8,128)S(1)}, f32[320,128]{1,0:T(8,128)S(1)}, u32[]{:S(2)}, u32[]{:S(2)}) collective-permute-start(f32[320,128]{1,0:T(8,128)S(1)} %pad_maximum_fusion.1), channel_id=1, source_target_pairs={{0,2},{1,3},{2,0},{3,1},{4,6},{5,7},{6,4},{7,5},{8,10},{9,11},{10,... | collective-permute-start | bytes 491528 | tf_op jit(solution)/shard_map/ppermute | solution.py:77
  14.9 6.1 %collective-permute-start.7 = (f32[64,640]{1,0:T(8,128)S(1)}, f32[64,640]{1,0:T(8,128)S(1)}, u32[]{:S(2)}, u32[]{:S(2)}) collective-permute-start(f32[64,640]{1,0:T(8,128)S(1)} %slice_add_fusion.4.own_ref), channel_id=1, source_target_pairs={{0,1},{1,0},{2,3},{3,2},{4,5},{5,4},{6,7},{7,6},{8,9},{9,8},{10,11... | collective-permute-start | bytes 491528 | tf_op jit(solution)/shard_map/ppermute | solution.py:77
  19.2 1.7 %collective-permute-start.12 = (f32[64,128]{1,0:T(8,128)S(1)}, f32[64,128]{1,0:T(8,128)S(1)}, u32[]{:S(2)}, u32[]{:S(2)}) collective-permute-start(f32[64,128]{1,0:T(8,128)S(1)} %get-tuple-element.76.own_ref), channel_id=1, source_target_pairs={{0,1},{1,0},{2,3},{3,2},{4,5},{5,4},{6,7},{7,6},{8,9},{9,8},{10,11... | collective-permute-start | bytes 98312 | tf_op jit(solution)/shard_map/ppermute | solution.py:77
  19.2 5.9 %collective-permute-start.8 = (f32[64,512]{1,0:T(8,128)S(1)}, f32[64,512]{1,0:T(8,128)S(1)}, u32[]{:S(2)}, u32[]{:S(2)}) collective-permute-start(f32[64,512]{1,0:T(8,128)S(1)} %get-tuple-element.72.refs_0_), channel_id=1, source_target_pairs={{0,2},{1,3},{2,0},{3,1},{4,6},{5,7},{6,4},{7,5},{8,10},{9,11},{10,... | collective-permute-start | bytes 393224 | tf_op jit(solution)/shard_map/ppermute | solution.py:77
  21.8 4.3 %collective-permute-start.10 = (f32[64,256]{1,0:T(8,128)S(1)}, f32[64,256]{1,0:T(8,128)S(1)}, u32[]{:S(2)}, u32[]{:S(2)}) collective-permute-start(f32[64,256]{1,0:T(8,128)S(1)} %get-tuple-element.59.refs_0_), channel_id=1, source_target_pairs={{0,4},{4,0},{8,12},{12,8},{16,20},{20,16},{24,28},{28,24},{1,5},{5... | collective-permute-start | bytes 196616 | tf_op jit(solution)/shard_map/ppermute | solution.py:77
  25.5 4.3 %collective-permute-start.15 = (f32[64,256]{1,0:T(8,128)S(1)}, f32[64,256]{1,0:T(8,128)S(1)}, u32[]{:S(2)}, u32[]{:S(2)}) collective-permute-start(f32[64,256]{1,0:T(8,128)S(1)} %get-tuple-element.68.refs_0_), channel_id=1, source_target_pairs={{0,4},{4,0},{8,12},{12,8},{16,20},{20,16},{24,28},{28,24},{1,5},{5... | collective-permute-start | bytes 196616 | tf_op jit(solution)/shard_map/ppermute | solution.py:77
  26.3 7.6 %collective-permute-start.13 = (f32[128,128]{1,0:T(8,128)S(1)}, f32[128,128]{1,0:T(8,128)S(1)}, u32[]{:S(2)}, u32[]{:S(2)}) collective-permute-start(f32[128,128]{1,0:T(8,128)S(1)} %pad_maximum_fusion.3), channel_id=1, source_target_pairs={{0,8},{4,12},{8,0},{12,4},{16,24},{20,28},{24,16},{28,20},{1,9},{5... | collective-permute-start | bytes 196616 | tf_op jit(solution)/shard_map/ppermute | solution.py:77
  30.0 4.0 %collective-permute-start.16 = (f32[64,128]{1,0:T(8,128)S(1)}, f32[64,128]{1,0:T(8,128)S(1)}, u32[]{:S(2)}, u32[]{:S(2)}) collective-permute-start(f32[64,128]{1,0:T(8,128)S(1)} %get-tuple-element.70), channel_id=1, source_target_pairs={{0,8},{4,12},{8,0},{12,4},{16,24},{20,28},{24,16},{28,20},{1,9},{5... | collective-permute-start | bytes 98312 | tf_op jit(solution)/shard_map/ppermute | solution.py:77
  31.6 4.2 %collective-permute-start.9 = (f32[576,128]{1,0:T(8,128)S(1)}, f32[576,128]{1,0:T(8,128)S(1)}, u32[]{:S(2)}, u32[]{:S(2)}) collective-permute-start(f32[576,128]{1,0:T(8,128)S(1)} %pad_maximum_fusion.own_ref), channel_id=1, source_target_pairs={{0,1},{1,0},{2,3},{3,2},{4,5},{5,4},{6,7},{7,6},{8,9},{9,8},{10,11... | collective-permute-start | bytes 884744 | tf_op jit(solution)/shard_map/ppermute | solution.py:77
  34.0 1.8 %collective-permute-start.14 = (f32[192,128]{1,0:T(8,128)S(1)}, f32[192,128]{1,0:T(8,128)S(1)}, u32[]{:S(2)}, u32[]{:S(2)}) collective-permute-start(f32[192,128]{1,0:T(8,128)S(1)} %pad_maximum_fusion.2.own_found_ref.refs_2_), channel_id=1, source_target_pairs={{0,1},{1,0},{2,3},{3,2},{4,5},{5,4},{6,7},{7,6},{8,9},{9,8},{10,11... | collective-permute-start | bytes 294920 | tf_op jit(solution)/shard_map/ppermute | solution.py:77
  34.1 3.6 %collective-permute-start.17 = (f32[128,128]{1,0:T(8,128)S(1)}, f32[128,128]{1,0:T(8,128)S(1)}, u32[]{:S(2)}, u32[]{:S(2)}) collective-permute-start(f32[128,128]{1,0:T(8,128)S(1)} %pad_maximum_fusion.4.refs_4_), channel_id=1, source_target_pairs={{0,1},{1,0},{2,3},{3,2},{4,5},{5,4},{6,7},{7,6},{8,9},{9,8},{10,11... | collective-permute-start | bytes 196616 | tf_op jit(solution)/shard_map/ppermute | solution.py:77

commit v5 on v4

--- a/solution.py
+++ b/solution.py
@@ -116,6 +116,16 @@
     groups = [([e] if e >= head else []) + blocks[e] for e in range(count)]
     starts = [sum(len(b) for b in groups[:e]) * rank for e in range(count + 1)]
 
+    def store_blocks(out_ref, vectors, group):
+        parts = [None if v is None else halves(v) for v in vectors]
+        side = core_side()
+        for e in group:
+            right = [lanes([parts[f][i] for f in groups[e]]) for i in range(2)]
+            value = dot_parts(halves(vectors[e].T), right)
+            where = slice(starts[e] - starts[group[0]], starts[e + 1] - starts[group[0]])
+            for h in range(2):
+                out_ref[at(h ^ side, half), where] = value[h * half : (h + 1) * half]
+
     def gram_body(*refs):
         scale_hbm, leaf_hbm, level_hbm, queries_hbm, leaf_core_hbm, core_hbm = refs[:6]
         out_ref, scale_ref, leaf_ref, level_ref, queries_ref, core_ref, sems = refs[6:]
@@ -132,20 +142,14 @@
             copy.wait()
         vectors = [column_scale(scale_ref[...]) * leaf_ref[...]]
         vectors += [level_ref[levels - e] for e in range(1, count)]
-        parts = [halves(v) for v in vectors]
-        side = core_side()
-        for e in range(count):
-            right = [lanes([parts[f][i] for f in groups[e]]) for i in range(2)]
-            value = dot_parts(halves(vectors[e].T), right)
-            for h in range(2):
-                out_ref[at(h ^ side, half), starts[e] : starts[e + 1]] = value[h * half : (h + 1) * half]
+        store_blocks(out_ref, vectors, range(head))
         for copy in copies[2 + levels :]:
             copy.wait()
 
     gram, scale, leaf_basis, level_basis, queries, cores = call(
         gram_body,
         [
-            (rank, starts[count]),
+            (rank, starts[head]),
             *[array.shape for array in (scale, leaf_basis, level_basis, queries)],
             (count, rank, rank),
         ],
@@ -153,13 +157,35 @@
             pltpu.with_memory_space_constraint(array, pltpu.HBM)
             for array in (scale, leaf_basis, level_basis, queries, leaf_cores, level_cores)
         ],
-        flops=small * starts[count] // rank * rows_here // rank,
+        flops=small * starts[head] // rank * rows_here // rank,
         spaces=[pltpu.HBM] * 6,
         scratch=[pltpu.SemaphoreType.DMA((3 + levels + count,))],
     )
     gram_chip = gram[:half] + swap(gram[half:], "sub", 0)
-    early = add_all(partial_sums(gram_chip[:, : starts[head]], "sub", leaf_bits))
-    remaining, diagonal, coupling = gram_chip[:, starts[head] :], [], []
+    early = add_all(partial_sums(gram_chip, "sub", leaf_bits))
+
+    def moment_body(scale_ref, queries_ref, leaf_ref, level_ref, tail_ref, out_ref, *basis_refs):
+        vectors = [level_ref[levels - e] if e >= head else None for e in range(count)]
+        store_blocks(tail_ref, vectors, range(head, count))
+        spread = column_scale(scale_ref[...])
+        right = halves(lanes([leaf_ref[...]] + [spread * level_ref[levels - e] for e in range(1, count)]))
+        for basis_ref, part in zip(basis_refs, right):
+            basis_ref[...] = part
+        value = dot_parts(halves(queries_ref[...].T), right)
+        side = core_side()
+        for h in range(2):
+            out_ref[at(h ^ side, mine), :] = value[h * mine : (h + 1) * mine]
+
+    tail, value, *basis = call(
+        moment_body,
+        [(rank, starts[count] - starts[head]), (columns, count * rank), *pair(rows_here, count * rank)],
+        scale,
+        queries,
+        leaf_basis,
+        level_basis,
+        flops=small * count * 2 * rows_here // rank,
+    )
+    remaining, diagonal, coupling = tail[:half] + swap(tail[half:], "sub", 0), [], []
     for e in range(head, top):
         remaining = add_all(partial_sums(remaining, "rows", bits[e]))
         size = starts[e + 1] - starts[e]
@@ -171,25 +197,6 @@
     coupling = add_all(partial_sums(lanes([*coupling, remaining]), "sub", leaf_bits))
     top_block, coupling = coupling[:, -rank:], coupling[:, :-rank]
 
-    def moment_body(scale_ref, queries_ref, leaf_ref, level_ref, out_ref, *basis_refs):
-        spread = column_scale(scale_ref[...])
-        right = halves(lanes([leaf_ref[...]] + [spread * level_ref[levels - e] for e in range(1, count)]))
-        for basis_ref, part in zip(basis_refs, right):
-            basis_ref[...] = part
-        value = dot_parts(halves(queries_ref[...].T), right)
-        side = core_side()
-        for h in range(2):
-            out_ref[at(h ^ side, mine), :] = value[h * mine : (h + 1) * mine]
-
-    value, *basis = call(
-        moment_body,
-        [(columns, count * rank), *pair(rows_here, count * rank)],
-        scale,
-        queries,
-        leaf_basis,
-        level_basis,
-        flops=small * count * 2 * rows_here // rank,
-    )
     moment_chip = value[:mine] + swap(value[mine:], "sub", 0)
     moment_parts = [moment_chip[b * batch : (b + 1) * batch] for b in range(batches)]
     moment_parts = [partial_sums(moment_parts[b], "sub", leaf_bits) for b in range(batches)]

time: 39.5 us -> 39.5 us (level)
  starting transfers between devices: 14.7 us -> 18.3 us
  waiting for transfers between devices: 14 us -> 10.4 us
    ppermute x18 -> x19, waiting for transfers between devices: 14 us -> 10.4 us  [swap(): lax.ppermute(array, axis, [(i, i ^ 1 << bit) for i in range(lax.axis_size...]
    ppermute x18 -> x19, starting transfers between devices: 14.7 us -> 18.3 us  [swap(): lax.ppermute(array, axis, [(i, i ^ 1 << bit) for i in range(lax.axis_size...]
  transfers between devices with their start and end apart: 18 -> 19, of which waited for: 8 -> 5; matrix products, arithmetic and copies ran while one was open for 1% -> 1% of each run, Pallas kernels for 14% -> 14%
where the time goes in v5:
time: 39.5 us; the launch traced here: 39.3 us
  starting transfers between devices  18.3 us (46%)
  waiting for transfers between devices  10.4 us (26%)
  Pallas kernels  9.97 us (25%)
    ppermute x19, starting transfers between devices, swap(): lax.ppermute(array, axis, [(i, i ^ 1 << bit) for i in range(lax.axis_size...  18.3 us
    ppermute x19, waiting for transfers between devices, swap(): lax.ppermute(array, axis, [(i, i ^ 1 << bit) for i in range(lax.axis_size...  10.4 us
    pallas_call x13, Pallas kernels, call(): pl.pallas_call(body, out_shape=outs, in_specs=[pl.BlockSpec(memory_space=...  9.97 us
  transfers between devices with their start and end apart: 19, of which 5 were waited for; matrix products, arithmetic and copies ran while one was open for 1% of the time, Pallas kernels for 14%

profile of v5, /device:TPU:0, one launch (start us, length us, event | category | flops | bytes accessed | tf_op | source)
XLA Modules:
  0.0 39.3 jit_solution(14446446037374417745)
XLA Ops:
  0.0 1.9 %shard_map.64 = (f32[128,640]{1,0:T(8,128)S(1)}, f32[4,128]{1,0:T(4,128)S(1)}, f32[512,128]{1,0:T(8,128)S(1)}, f32[3,512,128]{2,1,0:T(8,128)S(1)}, f32[512,256]{1,0:T(8,128)S(1)}, /*index=5*/f32[4,128,128]{2,1,0:T(8,128)S(1)}) custom-call(f32[4,128]{1,0:T(4,128)} %bitcast.1, f32[512,128]{1,0:T(8,128)} %refs_1_.1, f32[3,512,128]{2,1,0:T(8,128)} %refs_2_.1, ...), custom_call_target="tpu_custom_call" | custom-call | flops 251658240 | bytes 2557952 | tf_op jit(solution)/shard_map/pallas_call | solution.py:56
  1.9 1.0 %shard_map.66 = (f32[128,384]{1,0:T(8,128)S(1)}, f32[256,512]{1,0:T(8,128)S(1)}, bf16[512,512]{1,0:T(8,128)(2,1)S(1)}, bf16[512,512]{1,0:T(8,128)(2,1)S(1)}) custom-call(f32[4,128]{1,0:T(4,128)S(1)} %get-tuple-element.39.scale_ref, f32[512,256]{1,0:T(8,128)S(1)} %get-tuple-element.40.queries_ref, f32[512,128]{1,0:T(8,128)S(1)} %get-tuple-element.41.leaf_ref, ...), custom_call_target="tpu_custom_call" | custom-call | flops 402653184 | bytes 1574912 | tf_op jit(solution)/shard_map/pallas_call | solution.py:56
  2.9 0.6 %collective-permute-start.1 = (f32[64,384]{1,0:T(8,128)S(1)}, f32[64,384]{1,0:T(8,128)S(1)}, u32[]{:S(2)}, u32[]{:S(2)}) collective-permute-start(f32[64,384]{1,0:T(8,128)S(1)} %slice.48), channel_id=1, source_target_pairs={{0,1},{1,0},{2,3},{3,2},{4,5},{5,4},{6,7},{7,6},{8,9},{9,8},{10,11... | collective-permute-start | bytes 294920 | tf_op jit(solution)/shard_map/ppermute | solution.py:77
  3.5 0.1 collective-permute-start.6
  3.6 0.7 %shard_map.65 = (f32[512,128]{1,0:T(8,128)S(1)}, bf16[512,128]{1,0:T(8,128)(2,1)S(1)}, bf16[512,128]{1,0:T(8,128)(2,1)S(1)}) custom-call(f32[4,128]{1,0:T(4,128)S(1)} %get-tuple-element.39.scale_ref, f32[512,256]{1,0:T(8,128)S(1)} %get-tuple-element.40.queries_ref, f32[512,128]{1,0:T(8,128)S(1)} %get-tuple-element.41.leaf_ref, ...), custom_call_target="tpu_custom_call" | custom-call | flops 201326592 | bytes 1574912 | tf_op jit(solution)/shard_map/pallas_call | solution.py:56
  4.3 0.6 %collective-permute-start = (f32[256,128]{1,0:T(8,128)S(1)}, f32[256,128]{1,0:T(8,128)S(1)}, u32[]{:S(2)}, u32[]{:S(2)}) collective-permute-start(f32[256,128]{1,0:T(8,128)S(1)} %slice.46), channel_id=1, source_target_pairs={{0,1},{1,0},{2,3},{3,2},{4,5},{5,4},{6,7},{7,6},{8,9},{9,8},{10,11... | collective-permute-start | bytes 393224 | tf_op jit(solution)/shard_map/ppermute | solution.py:77
  4.9 0.1 collective-permute-start.4
  5.0 0.0 collective-permute-done.1
  5.0 3.0 %collective-permute-start.2 = (f32[64,384]{1,0:T(8,128)S(1)}, f32[64,384]{1,0:T(8,128)S(1)}, u32[]{:S(2)}, u32[]{:S(2)}) collective-permute-start(f32[64,384]{1,0:T(8,128)S(1)} %slice_add_fusion.3), channel_id=1, source_target_pairs={{0,4},{4,0},{8,12},{12,8},{16,20},{20,16},{24,28},{28,24},{1,5},{5... | collective-permute-start | bytes 294920 | tf_op jit(solution)/shard_map/ppermute | solution.py:77
  8.1 0.0 collective-permute-done
  8.1 0.0 collective-permute-done.6
  8.1 1.6 %collective-permute-start.7 = (f32[64,640]{1,0:T(8,128)S(1)}, f32[64,640]{1,0:T(8,128)S(1)}, u32[]{:S(2)}, u32[]{:S(2)}) collective-permute-start(f32[64,640]{1,0:T(8,128)S(1)} %slice_add_fusion.1), channel_id=1, source_target_pairs={{0,2},{1,3},{2,0},{3,1},{4,6},{5,7},{6,4},{7,5},{8,10},{9,11},{10,... | collective-permute-start | bytes 491528 | tf_op jit(solution)/shard_map/ppermute | solution.py:77
  9.7 1.3 %collective-permute-done.2 = f32[64,384]{1,0:T(8,128)S(1)} collective-permute-done((f32[64,384]{1,0:T(8,128)S(1)}, f32[64,384]{1,0:T(8,128)S(1)}, u32[]{:S(2)}, u32[]{:S(2)}) %collective-permute-start.2) | collective-permute-done | bytes 98336 | tf_op jit(solution)/shard_map/ppermute | solution.py:77
  11.1 1.8 %collective-permute-start.12 = (f32[64,256]{1,0:T(8,128)S(1)}, f32[64,256]{1,0:T(8,128)S(1)}, u32[]{:S(2)}, u32[]{:S(2)}) collective-permute-start(f32[64,256]{1,0:T(8,128)S(1)} %constant_dynamic-update-slice_fusion), channel_id=1, source_target_pairs={{0,2},{1,3},{2,0},{3,1},{4,6},{5,7},{6,4},{7,5},{8,10},{9,11},{10,... | collective-permute-start | bytes 196616 | tf_op jit(solution)/shard_map/ppermute | solution.py:77
  13.0 0.3 collective-permute-start.3
  13.3 0.0 collective-permute-done.4
  13.4 1.8 %collective-permute-start.5 = (f32[64,512]{1,0:T(8,128)S(1)}, f32[64,512]{1,0:T(8,128)S(1)}, u32[]{:S(2)}, u32[]{:S(2)}) collective-permute-start(f32[64,512]{1,0:T(8,128)S(1)} %get-tuple-element.73.refs_0_), channel_id=1, source_target_pairs={{0,2},{1,3},{2,0},{3,1},{4,6},{5,7},{6,4},{7,5},{8,10},{9,11},{10,... | collective-permute-start | bytes 393224 | tf_op jit(solution)/shard_map/ppermute | solution.py:77
  15.2 1.1 %collective-permute-done.12 = f32[64,256]{1,0:T(8,128)S(1)} collective-permute-done((f32[64,256]{1,0:T(8,128)S(1)}, f32[64,256]{1,0:T(8,128)S(1)}, u32[]{:S(2)}, u32[]{:S(2)}) %collective-permute-start.12) | collective-permute-done | bytes 65568 | tf_op jit(solution)/shard_map/ppermute | solution.py:77
  16.3 0.0 collective-permute-done.7
  16.3 0.1 collective-permute-start.8
  16.4 0.5 %collective-permute-start.13 = (f32[64,128]{1,0:T(8,128)S(1)}, f32[64,128]{1,0:T(8,128)S(1)}, u32[]{:S(2)}, u32[]{:S(2)}) collective-permute-start(f32[64,128]{1,0:T(8,128)S(1)} %get-tuple-element.78.own_ref), channel_id=1, source_target_pairs={{0,1},{1,0},{2,3},{3,2},{4,5},{5,4},{6,7},{7,6},{8,9},{9,8},{10,11... | collective-permute-start | bytes 98312 | tf_op jit(solution)/shard_map/ppermute | solution.py:77
  16.9 1.6 %collective-permute-start.9 = (f32[64,512]{1,0:T(8,128)S(1)}, f32[64,512]{1,0:T(8,128)S(1)}, u32[]{:S(2)}, u32[]{:S(2)}) collective-permute-start(f32[64,512]{1,0:T(8,128)S(1)} %get-tuple-element.74.refs_0_), channel_id=1, source_target_pairs={{0,2},{1,3},{2,0},{3,1},{4,6},{5,7},{6,4},{7,5},{8,10},{9,11},{10,... | collective-permute-start | bytes 393224 | tf_op jit(solution)/shard_map/ppermute | solution.py:77
  18.5 0.0 collective-permute-done.13.other_ref
  18.5 0.2 shard_map.72
  18.8 0.0 collective-permute-done.8.other_ref
  18.8 0.4 shard_map.67
  19.2 3.7 %collective-permute-done.5.refs_1_ = f32[64,512]{1,0:T(8,128)S(1)} collective-permute-done((f32[64,512]{1,0:T(8,128)S(1)}, f32[64,512]{1,0:T(8,128)S(1)}, u32[]{:S(2)}, u32[]{:S(2)}) %collective-permute-start.5) | collective-permute-done | bytes 131104 | tf_op jit(solution)/shard_map/ppermute | solution.py:77
  22.9 0.4 shard_map.68
  23.3 1.6 %collective-permute-start.11 = (f32[64,256]{1,0:T(8,128)S(1)}, f32[64,256]{1,0:T(8,128)S(1)}, u32[]{:S(2)}, u32[]{:S(2)}) collective-permute-start(f32[64,256]{1,0:T(8,128)S(1)} %get-tuple-element.61.refs_0_), channel_id=1, source_target_pairs={{0,4},{4,0},{8,12},{12,8},{16,20},{20,16},{24,28},{28,24},{1,5},{5... | collective-permute-start | bytes 196616 | tf_op jit(solution)/shard_map/ppermute | solution.py:77
  24.8 0.0 collective-permute-done.3
  24.8 0.0 collective-permute-done.9.refs_1_
  24.9 0.4 shard_map.69
  25.2 1.0 %collective-permute-start.16 = (f32[64,256]{1,0:T(8,128)S(1)}, f32[64,256]{1,0:T(8,128)S(1)}, u32[]{:S(2)}, u32[]{:S(2)}) collective-permute-start(f32[64,256]{1,0:T(8,128)S(1)} %get-tuple-element.70.refs_0_), channel_id=1, source_target_pairs={{0,4},{4,0},{8,12},{12,8},{16,20},{20,16},{24,28},{28,24},{1,5},{5... | collective-permute-start | bytes 196616 | tf_op jit(solution)/shard_map/ppermute | solution.py:77
  26.2 1.7 %collective-permute-done.11.refs_1_ = f32[64,256]{1,0:T(8,128)S(1)} collective-permute-done((f32[64,256]{1,0:T(8,128)S(1)}, f32[64,256]{1,0:T(8,128)S(1)}, u32[]{:S(2)}, u32[]{:S(2)}) %collective-permute-start.11) | collective-permute-done | bytes 65568 | tf_op jit(solution)/shard_map/ppermute | solution.py:77
  28.0 0.1 shard_map.73
  28.1 1.6 %collective-permute-start.14 = (f32[128,128]{1,0:T(8,128)S(1)}, f32[128,128]{1,0:T(8,128)S(1)}, u32[]{:S(2)}, u32[]{:S(2)}) collective-permute-start(f32[128,128]{1,0:T(8,128)S(1)} %pad_maximum_fusion.3), channel_id=1, source_target_pairs={{0,8},{4,12},{8,0},{12,4},{16,24},{20,28},{24,16},{28,20},{1,9},{5... | collective-permute-start | bytes 196616 | tf_op jit(solution)/shard_map/ppermute | solution.py:77
  29.8 0.0 collective-permute-done.16.refs_1_
  29.8 0.1 shard_map.75
  29.9 1.4 %collective-permute-start.17 = (f32[64,128]{1,0:T(8,128)S(1)}, f32[64,128]{1,0:T(8,128)S(1)}, u32[]{:S(2)}, u32[]{:S(2)}) collective-permute-start(f32[64,128]{1,0:T(8,128)S(1)} %get-tuple-element.72), channel_id=1, source_target_pairs={{0,8},{4,12},{8,0},{12,4},{16,24},{20,28},{24,16},{28,20},{1,9},{5... | collective-permute-start | bytes 98312 | tf_op jit(solution)/shard_map/ppermute | solution.py:77
  31.4 0.1 collective-permute-start.10
  31.4 2.5 %collective-permute-done.17 = f32[64,128]{1,0:T(8,128)S(1)} collective-permute-done((f32[64,128]{1,0:T(8,128)S(1)}, f32[64,128]{1,0:T(8,128)S(1)}, u32[]{:S(2)}, u32[]{:S(2)}) %collective-permute-start.17) | collective-permute-done | bytes 32800 | tf_op jit(solution)/shard_map/ppermute | solution.py:77
  33.9 0.0 collective-permute-done.14
  34.0 0.1 collective-permute-start.15
  34.0 0.5 %collective-permute-start.18 = (f32[128,128]{1,0:T(8,128)S(1)}, f32[128,128]{1,0:T(8,128)S(1)}, u32[]{:S(2)}, u32[]{:S(2)}) collective-permute-start(f32[128,128]{1,0:T(8,128)S(1)} %pad_maximum_fusion.4.refs_4_), channel_id=1, source_target_pairs={{0,1},{1,0},{2,3},{3,2},{4,5},{5,4},{6,7},{7,6},{8,9},{9,8},{10,11... | collective-permute-start | bytes 196616 | tf_op jit(solution)/shard_map/ppermute | solution.py:77
  34.5 1.2 %shard_map.71 = (bf16[512,256]{1,0:T(8,128)(2,1)S(1)}, bf16[512,256]{1,0:T(8,128)(2,1)S(1)}) custom-call(bf16[128,384]{1,0:T(8,128)(2,1)S(1)} %get-tuple-element.49.refs_2_.refs_0_, bf16[128,384]{1,0:T(8,128)(2,1)S(1)} %get-tuple-element.50.refs_3_.refs_1_, bf16[128,256]{1,0:T(8,128)(2,1)S(1)} %get-tuple-element.51.refs_4_.refs_2_, ...), custom_call_target="tpu_custom_call" | custom-call | flops 402653184 | bytes 1376256 | tf_op jit(solution)/shard_map/pallas_call | solution.py:56
  35.8 0.0 collective-permute-done.15.other_found_ref.refs_3_
  35.8 0.0 collective-permute-done.10.other_ref
  35.8 0.5 %shard_map.74 = (bf16[128,256]{1,0:T(8,128)(2,1)S(1)}, bf16[128,256]{1,0:T(8,128)(2,1)S(1)}) custom-call(f32[576,128]{1,0:T(8,128)S(1)} %pad_maximum_fusion.own_ref, f32[576,128]{1,0:T(8,128)S(1)} %collective-permute-done.10.other_ref, f32[192,128]{1,0:T(8,128)S(1)} %pad_maximum_fusion.2.own_found_ref.refs_2_, ...), custom_call_target="tpu_custom_call" | custom-call | flops 50331648 | bytes 1048576 | tf_op jit(solution)/shard_map/pallas_call | solution.py:56
  36.3 1.4 %shard_map.70.base_ref = f32[512,256]{1,0:T(8,128)S(1)} custom-call(f32[4,128]{1,0:T(4,128)S(1)} %get-tuple-element.39.scale_ref, f32[512,256]{1,0:T(8,128)S(1)} %get-tuple-element.40.queries_ref, f32[576,128]{1,0:T(8,128)S(1)} %pad_maximum_fusion.own_ref, f32[576,128]{1,0:T(8,128)S(1)} %collective-permute-done.10.other_ref, ...), custom_call_target="tpu_custom_call" | custom-call | flops 301989888 | bytes 3016704 | tf_op jit(solution)/shard_map/pallas_call | solution.py:56
  37.7 0.0 collective-permute-done.18.refs_5_
  37.7 1.7 %shard_map.76 = f32[512,256]{1,0:T(8,128)} custom-call(f32[512,256]{1,0:T(8,128)S(1)} %shard_map.70.base_ref, bf16[512,256]{1,0:T(8,128)(2,1)S(1)} %get-tuple-element.59.high_ref, bf16[512,256]{1,0:T(8,128)(2,1)S(1)} %get-tuple-element.60.low_ref, bf16[128,256]{1,0:T(8,128)(2,1)S(1)} %get-tuple-element.68.refs_0_, ...), custom_call_target="tpu_custom_call" | custom-call | flops 201326592 | bytes 1572864 | tf_op jit(solution)/shard_map/pallas_call | solution.py:56
  (24 shorter events, 0.3 us)
Async XLA Ops:
  2.9 2.1 %collective-permute-start.1 = (f32[64,384]{1,0:T(8,128)S(1)}, f32[64,384]{1,0:T(8,128)S(1)}, u32[]{:S(2)}, u32[]{:S(2)}) collective-permute-start(f32[64,384]{1,0:T(8,128)S(1)} %slice.48), channel_id=1, source_target_pairs={{0,1},{1,0},{2,3},{3,2},{4,5},{5,4},{6,7},{7,6},{8,9},{9,8},{10,11... | collective-permute-start | bytes 294920 | tf_op jit(solution)/shard_map/ppermute | solution.py:77
  3.5 4.6 %collective-permute-start.6 = (f32[64,640]{1,0:T(8,128)S(1)}, f32[64,640]{1,0:T(8,128)S(1)}, u32[]{:S(2)}, u32[]{:S(2)}) collective-permute-start(f32[64,640]{1,0:T(8,128)S(1)} %slice.56), channel_id=1, source_target_pairs={{0,1},{1,0},{2,3},{3,2},{4,5},{5,4},{6,7},{7,6},{8,9},{9,8},{10,11... | collective-permute-start | bytes 491528 | tf_op jit(solution)/shard_map/ppermute | solution.py:77
  4.3 3.7 %collective-permute-start = (f32[256,128]{1,0:T(8,128)S(1)}, f32[256,128]{1,0:T(8,128)S(1)}, u32[]{:S(2)}, u32[]{:S(2)}) collective-permute-start(f32[256,128]{1,0:T(8,128)S(1)} %slice.46), channel_id=1, source_target_pairs={{0,1},{1,0},{2,3},{3,2},{4,5},{5,4},{6,7},{7,6},{8,9},{9,8},{10,11... | collective-permute-start | bytes 393224 | tf_op jit(solution)/shard_map/ppermute | solution.py:77
  4.9 8.4 %collective-permute-start.4 = (f32[128,512]{1,0:T(8,128)S(1)}, f32[128,512]{1,0:T(8,128)S(1)}, u32[]{:S(2)}, u32[]{:S(2)}) collective-permute-start(f32[128,512]{1,0:T(8,128)S(1)} %slice.53), channel_id=1, source_target_pairs={{0,1},{1,0},{2,3},{3,2},{4,5},{5,4},{6,7},{7,6},{8,9},{9,8},{10,11... | collective-permute-start | bytes 786440 | tf_op jit(solution)/shard_map/ppermute | solution.py:77
  5.0 6.0 %collective-permute-start.2 = (f32[64,384]{1,0:T(8,128)S(1)}, f32[64,384]{1,0:T(8,128)S(1)}, u32[]{:S(2)}, u32[]{:S(2)}) collective-permute-start(f32[64,384]{1,0:T(8,128)S(1)} %slice_add_fusion.3), channel_id=1, source_target_pairs={{0,4},{4,0},{8,12},{12,8},{16,20},{20,16},{24,28},{28,24},{1,5},{5... | collective-permute-start | bytes 294920 | tf_op jit(solution)/shard_map/ppermute | solution.py:77
  8.1 8.2 %collective-permute-start.7 = (f32[64,640]{1,0:T(8,128)S(1)}, f32[64,640]{1,0:T(8,128)S(1)}, u32[]{:S(2)}, u32[]{:S(2)}) collective-permute-start(f32[64,640]{1,0:T(8,128)S(1)} %slice_add_fusion.1), channel_id=1, source_target_pairs={{0,2},{1,3},{2,0},{3,1},{4,6},{5,7},{6,4},{7,5},{8,10},{9,11},{10,... | collective-permute-start | bytes 491528 | tf_op jit(solution)/shard_map/ppermute | solution.py:77
  11.1 5.2 %collective-permute-start.12 = (f32[64,256]{1,0:T(8,128)S(1)}, f32[64,256]{1,0:T(8,128)S(1)}, u32[]{:S(2)}, u32[]{:S(2)}) collective-permute-start(f32[64,256]{1,0:T(8,128)S(1)} %constant_dynamic-update-slice_fusion), channel_id=1, source_target_pairs={{0,2},{1,3},{2,0},{3,1},{4,6},{5,7},{6,4},{7,5},{8,10},{9,11},{10,... | collective-permute-start | bytes 196616 | tf_op jit(solution)/shard_map/ppermute | solution.py:77
  13.0 11.9 %collective-permute-start.3 = (f32[320,128]{1,0:T(8,128)S(1)}, f32[320,128]{1,0:T(8,128)S(1)}, u32[]{:S(2)}, u32[]{:S(2)}) collective-permute-start(f32[320,128]{1,0:T(8,128)S(1)} %pad_maximum_fusion.1), channel_id=1, source_target_pairs={{0,2},{1,3},{2,0},{3,1},{4,6},{5,7},{6,4},{7,5},{8,10},{9,11},{10,... | collective-permute-start | bytes 491528 | tf_op jit(solution)/shard_map/ppermute | solution.py:77
  13.4 9.6 %collective-permute-start.5 = (f32[64,512]{1,0:T(8,128)S(1)}, f32[64,512]{1,0:T(8,128)S(1)}, u32[]{:S(2)}, u32[]{:S(2)}) collective-permute-start(f32[64,512]{1,0:T(8,128)S(1)} %get-tuple-element.73.refs_0_), channel_id=1, source_target_pairs={{0,2},{1,3},{2,0},{3,1},{4,6},{5,7},{6,4},{7,5},{8,10},{9,11},{10,... | collective-permute-start | bytes 393224 | tf_op jit(solution)/shard_map/ppermute | solution.py:77
  16.3 2.5 %collective-permute-start.8 = (f32[64,640]{1,0:T(8,128)S(1)}, f32[64,640]{1,0:T(8,128)S(1)}, u32[]{:S(2)}, u32[]{:S(2)}) collective-permute-start(f32[64,640]{1,0:T(8,128)S(1)} %add.36.own_ref), channel_id=1, source_target_pairs={{0,1},{1,0},{2,3},{3,2},{4,5},{5,4},{6,7},{7,6},{8,9},{9,8},{10,11... | collective-permute-start | bytes 491528 | tf_op jit(solution)/shard_map/ppermute | solution.py:77
  16.4 2.1 %collective-permute-start.13 = (f32[64,128]{1,0:T(8,128)S(1)}, f32[64,128]{1,0:T(8,128)S(1)}, u32[]{:S(2)}, u32[]{:S(2)}) collective-permute-start(f32[64,128]{1,0:T(8,128)S(1)} %get-tuple-element.78.own_ref), channel_id=1, source_target_pairs={{0,1},{1,0},{2,3},{3,2},{4,5},{5,4},{6,7},{7,6},{8,9},{9,8},{10,11... | collective-permute-start | bytes 98312 | tf_op jit(solution)/shard_map/ppermute | solution.py:77
  16.9 7.9 %collective-permute-start.9 = (f32[64,512]{1,0:T(8,128)S(1)}, f32[64,512]{1,0:T(8,128)S(1)}, u32[]{:S(2)}, u32[]{:S(2)}) collective-permute-start(f32[64,512]{1,0:T(8,128)S(1)} %get-tuple-element.74.refs_0_), channel_id=1, source_target_pairs={{0,2},{1,3},{2,0},{3,1},{4,6},{5,7},{6,4},{7,5},{8,10},{9,11},{10,... | collective-permute-start | bytes 393224 | tf_op jit(solution)/shard_map/ppermute | solution.py:77
  23.3 4.7 %collective-permute-start.11 = (f32[64,256]{1,0:T(8,128)S(1)}, f32[64,256]{1,0:T(8,128)S(1)}, u32[]{:S(2)}, u32[]{:S(2)}) collective-permute-start(f32[64,256]{1,0:T(8,128)S(1)} %get-tuple-element.61.refs_0_), channel_id=1, source_target_pairs={{0,4},{4,0},{8,12},{12,8},{16,20},{20,16},{24,28},{28,24},{1,5},{5... | collective-permute-start | bytes 196616 | tf_op jit(solution)/shard_map/ppermute | solution.py:77
  25.2 4.6 %collective-permute-start.16 = (f32[64,256]{1,0:T(8,128)S(1)}, f32[64,256]{1,0:T(8,128)S(1)}, u32[]{:S(2)}, u32[]{:S(2)}) collective-permute-start(f32[64,256]{1,0:T(8,128)S(1)} %get-tuple-element.70.refs_0_), channel_id=1, source_target_pairs={{0,4},{4,0},{8,12},{12,8},{16,20},{20,16},{24,28},{28,24},{1,5},{5... | collective-permute-start | bytes 196616 | tf_op jit(solution)/shard_map/ppermute | solution.py:77
  28.1 5.8 %collective-permute-start.14 = (f32[128,128]{1,0:T(8,128)S(1)}, f32[128,128]{1,0:T(8,128)S(1)}, u32[]{:S(2)}, u32[]{:S(2)}) collective-permute-start(f32[128,128]{1,0:T(8,128)S(1)} %pad_maximum_fusion.3), channel_id=1, source_target_pairs={{0,8},{4,12},{8,0},{12,4},{16,24},{20,28},{24,16},{28,20},{1,9},{5... | collective-permute-start | bytes 196616 | tf_op jit(solution)/shard_map/ppermute | solution.py:77
  29.9 4.0 %collective-permute-start.17 = (f32[64,128]{1,0:T(8,128)S(1)}, f32[64,128]{1,0:T(8,128)S(1)}, u32[]{:S(2)}, u32[]{:S(2)}) collective-permute-start(f32[64,128]{1,0:T(8,128)S(1)} %get-tuple-element.72), channel_id=1, source_target_pairs={{0,8},{4,12},{8,0},{12,4},{16,24},{20,28},{24,16},{28,20},{1,9},{5... | collective-permute-start | bytes 98312 | tf_op jit(solution)/shard_map/ppermute | solution.py:77
  31.4 4.4 %collective-permute-start.10 = (f32[576,128]{1,0:T(8,128)S(1)}, f32[576,128]{1,0:T(8,128)S(1)}, u32[]{:S(2)}, u32[]{:S(2)}) collective-permute-start(f32[576,128]{1,0:T(8,128)S(1)} %pad_maximum_fusion.own_ref), channel_id=1, source_target_pairs={{0,1},{1,0},{2,3},{3,2},{4,5},{5,4},{6,7},{7,6},{8,9},{9,8},{10,11... | collective-permute-start | bytes 884744 | tf_op jit(solution)/shard_map/ppermute | solution.py:77
  34.0 1.8 %collective-permute-start.15 = (f32[192,128]{1,0:T(8,128)S(1)}, f32[192,128]{1,0:T(8,128)S(1)}, u32[]{:S(2)}, u32[]{:S(2)}) collective-permute-start(f32[192,128]{1,0:T(8,128)S(1)} %pad_maximum_fusion.2.own_found_ref.refs_2_), channel_id=1, source_target_pairs={{0,1},{1,0},{2,3},{3,2},{4,5},{5,4},{6,7},{7,6},{8,9},{9,8},{10,11... | collective-permute-start | bytes 294920 | tf_op jit(solution)/shard_map/ppermute | solution.py:77
  34.0 3.6 %collective-permute-start.18 = (f32[128,128]{1,0:T(8,128)S(1)}, f32[128,128]{1,0:T(8,128)S(1)}, u32[]{:S(2)}, u32[]{:S(2)}) collective-permute-start(f32[128,128]{1,0:T(8,128)S(1)} %pad_maximum_fusion.4.refs_4_), channel_id=1, source_target_pairs={{0,1},{1,0},{2,3},{3,2},{4,5},{5,4},{6,7},{7,6},{8,9},{9,8},{10,11... | collective-permute-start | bytes 196616 | tf_op jit(solution)/shard_map/ppermute | solution.py:77

commit v6 on v5

--- a/solution.py
+++ b/solution.py
@@ -108,8 +108,9 @@
     leaf_bits = range(1, sub.bit_length() - 1)
     mine = columns // 2
     half = rank // 2
-    batches = 2
-    batch = mine // batches
+    sizes = (3 * mine // 4, mine // 4)
+    batches = len(sizes)
+    offsets = [sum(sizes[:b]) for b in range(batches)]
     small = 2 * 3 * rank**3
 
     scale = row_scale.reshape(-1, rank)
@@ -198,7 +199,7 @@
     top_block, coupling = coupling[:, -rank:], coupling[:, :-rank]
 
     moment_chip = value[:mine] + swap(value[mine:], "sub", 0)
-    moment_parts = [moment_chip[b * batch : (b + 1) * batch] for b in range(batches)]
+    moment_parts = [moment_chip[offsets[b] : offsets[b] + sizes[b]] for b in range(batches)]
     moment_parts = [partial_sums(moment_parts[b], "sub", leaf_bits) for b in range(batches)]
 
     late_rows = columns // 2 + head * half
@@ -277,7 +278,7 @@
         rest = add_all([part[...] for part in part_refs])
         for e in range(head):
             own, rest = rest[:, :rank], rest[:, rank:]
-            own_ref[e * batch : (e + 1) * batch, :] = own
+            own_ref[e * own.shape[0] : (e + 1) * own.shape[0], :] = own
             rest = rest - dot_parts(halves(own), take(factor_refs[e], 0, rest.shape[1]))
         rest_ref[...] = rest
 
@@ -290,19 +291,18 @@
 
     def scatter(parts, number, stack_ref):
         side = core_side()
-        for b, part in enumerate(parts):
+        for part, size, offset in zip(parts, sizes, offsets):
             for ref, place in zip(part, (side, 1 - side)):
+                rows = pl.ds(pl.multiple_of(place * mine + offset, 8), size)
                 for e in range(number):
-                    stack_ref[at(place * batches + b, batch), e * rank : (e + 1) * rank] = ref[
-                        e * batch : (e + 1) * batch, :
-                    ]
+                    stack_ref[rows, e * rank : (e + 1) * rank] = ref[e * size : (e + 1) * size, :]
 
     factors += products(list(range(head, top)), coupling)
     head_moments, found_parts = [], []
-    for b in range(batches):
+    for b, size in enumerate(sizes):
         own, rest = call(
             functools.partial(head_body, len(moment_parts[b])),
-            [(head * batch, rank), (batch, coarse * rank)],
+            [(head * size, rank), (size, coarse * rank)],
             *moment_parts[b],
             *flat(factors[:head]),
             flops=small * sum(map(len, blocks[:head])) // batches,
@@ -313,7 +313,7 @@
             parts = partial_sums(rest, "rows", bits[e])
             own, rest = call(
                 functools.partial(step_body, len(parts)),
-                [(batch, rank), (batch, (top - e) * rank)],
+                [(size, rank), (size, (top - e) * rank)],
                 *parts,
                 *factors[e],
                 flops=small * (top - e) // batches,
@@ -350,7 +350,7 @@
         side = core_side()
         sources = ((own_ref, own_found_ref, side), (other_ref, other_found_ref, 1 - side))
         for late_ref, found_ref, place in sources:
-            gram_ref[at(place, half), (coarse - 1) * rank :] = found_ref[coarse * batch :]
+            gram_ref[at(place, half), (coarse - 1) * rank :] = found_ref[coarse * sizes[0] :]
             for e in range(head, top):
                 start = columns // 2 + e * half
                 where = slice((e - head) * rank, (e - head + 1) * rank)
@@ -375,7 +375,7 @@
     def base_body(scale_ref, queries_ref, own_ref, other_ref, core_ref, *refs):
         factor_refs, basis_refs, scaled_refs = paired(refs[: 2 * head]), refs[2 * head : -5], refs[-5:-3]
         out_ref, stack_ref, gram_ref = refs[-3:]
-        pieces = [pl.ds(late_size + b * head * batch, head * batch) for b in range(batches)]
+        pieces = [pl.ds(late_size + head * offset, head * size) for size, offset in zip(sizes, offsets)]
         scatter([(own_ref.at[piece], other_ref.at[piece]) for piece in pieces], head, stack_ref)
         side = core_side()
         for late_ref, place in ((own_ref, side), (other_ref, 1 - side)):

time: 39.5 us -> 39.1 us (0.990)
  starting transfers between devices: 18.3 us -> 17.1 us
  waiting for transfers between devices: 10.4 us -> 11.3 us
    ppermute x19, starting transfers between devices: 18.3 us -> 17.1 us  [swap(): lax.ppermute(array, axis, [(i, i ^ 1 << bit) for i in range(lax.axis_size...]
    ppermute x19, waiting for transfers between devices: 10.4 us -> 11.3 us  [swap(): lax.ppermute(array, axis, [(i, i ^ 1 << bit) for i in range(lax.axis_size...]
where the time goes in v6:
time: 39.1 us; the launch traced here: 39 us
  starting transfers between devices  17.1 us (44%)
  waiting for transfers between devices  11.3 us (29%)
  Pallas kernels  9.97 us (25%)
    ppermute x19, starting transfers between devices, swap(): lax.ppermute(array, axis, [(i, i ^ 1 << bit) for i in range(lax.axis_size...  17.1 us
    ppermute x19, waiting for transfers between devices, swap(): lax.ppermute(array, axis, [(i, i ^ 1 << bit) for i in range(lax.axis_size...  11.3 us
    pallas_call x13, Pallas kernels, call(): pl.pallas_call(body, out_shape=outs, in_specs=[pl.BlockSpec(memory_space=...  9.97 us
  transfers between devices with their start and end apart: 19, of which 5 were waited for; matrix products, arithmetic and copies ran while one was open for 1% of the time, Pallas kernels for 14%

profile of v6, /device:TPU:0, one launch (start us, length us, event | category | flops | bytes accessed | tf_op | source)
XLA Modules:
  0.0 39.0 jit_solution(12993752212393510094)
XLA Ops:
  0.0 1.9 %shard_map.64 = (f32[128,640]{1,0:T(8,128)S(1)}, f32[4,128]{1,0:T(4,128)S(1)}, f32[512,128]{1,0:T(8,128)S(1)}, f32[3,512,128]{2,1,0:T(8,128)S(1)}, f32[512,256]{1,0:T(8,128)S(1)}, /*index=5*/f32[4,128,128]{2,1,0:T(8,128)S(1)}) custom-call(f32[4,128]{1,0:T(4,128)} %bitcast.1, f32[512,128]{1,0:T(8,128)} %refs_1_.1, f32[3,512,128]{2,1,0:T(8,128)} %refs_2_.1, ...), custom_call_target="tpu_custom_call" | custom-call | flops 251658240 | bytes 2557952 | tf_op jit(solution)/shard_map/pallas_call | solution.py:56
  1.9 1.0 %shard_map.66 = (f32[128,384]{1,0:T(8,128)S(1)}, f32[256,512]{1,0:T(8,128)S(1)}, bf16[512,512]{1,0:T(8,128)(2,1)S(1)}, bf16[512,512]{1,0:T(8,128)(2,1)S(1)}) custom-call(f32[4,128]{1,0:T(4,128)S(1)} %get-tuple-element.39.scale_ref, f32[512,256]{1,0:T(8,128)S(1)} %get-tuple-element.40.queries_ref, f32[512,128]{1,0:T(8,128)S(1)} %get-tuple-element.41.leaf_ref, ...), custom_call_target="tpu_custom_call" | custom-call | flops 402653184 | bytes 1574912 | tf_op jit(solution)/shard_map/pallas_call | solution.py:56
  2.9 0.6 %collective-permute-start.1 = (f32[64,384]{1,0:T(8,128)S(1)}, f32[64,384]{1,0:T(8,128)S(1)}, u32[]{:S(2)}, u32[]{:S(2)}) collective-permute-start(f32[64,384]{1,0:T(8,128)S(1)} %slice.48), channel_id=1, source_target_pairs={{0,1},{1,0},{2,3},{3,2},{4,5},{5,4},{6,7},{7,6},{8,9},{9,8},{10,11... | collective-permute-start | bytes 294920 | tf_op jit(solution)/shard_map/ppermute | solution.py:77
  3.5 0.1 collective-permute-start.6
  3.6 0.7 %shard_map.65 = (f32[512,128]{1,0:T(8,128)S(1)}, bf16[512,128]{1,0:T(8,128)(2,1)S(1)}, bf16[512,128]{1,0:T(8,128)(2,1)S(1)}) custom-call(f32[4,128]{1,0:T(4,128)S(1)} %get-tuple-element.39.scale_ref, f32[512,256]{1,0:T(8,128)S(1)} %get-tuple-element.40.queries_ref, f32[512,128]{1,0:T(8,128)S(1)} %get-tuple-element.41.leaf_ref, ...), custom_call_target="tpu_custom_call" | custom-call | flops 201326592 | bytes 1574912 | tf_op jit(solution)/shard_map/pallas_call | solution.py:56
  4.3 0.6 %collective-permute-start = (f32[256,128]{1,0:T(8,128)S(1)}, f32[256,128]{1,0:T(8,128)S(1)}, u32[]{:S(2)}, u32[]{:S(2)}) collective-permute-start(f32[256,128]{1,0:T(8,128)S(1)} %slice.46), channel_id=1, source_target_pairs={{0,1},{1,0},{2,3},{3,2},{4,5},{5,4},{6,7},{7,6},{8,9},{9,8},{10,11... | collective-permute-start | bytes 393224 | tf_op jit(solution)/shard_map/ppermute | solution.py:77
  4.9 0.1 collective-permute-start.4
  5.0 0.0 collective-permute-done.1
  5.0 3.0 %collective-permute-start.2 = (f32[64,384]{1,0:T(8,128)S(1)}, f32[64,384]{1,0:T(8,128)S(1)}, u32[]{:S(2)}, u32[]{:S(2)}) collective-permute-start(f32[64,384]{1,0:T(8,128)S(1)} %slice_add_fusion.3), channel_id=1, source_target_pairs={{0,4},{4,0},{8,12},{12,8},{16,20},{20,16},{24,28},{28,24},{1,5},{5... | collective-permute-start | bytes 294920 | tf_op jit(solution)/shard_map/ppermute | solution.py:77
  8.1 0.0 collective-permute-done
  8.1 0.0 collective-permute-done.6
  8.1 1.6 %collective-permute-start.7 = (f32[64,640]{1,0:T(8,128)S(1)}, f32[64,640]{1,0:T(8,128)S(1)}, u32[]{:S(2)}, u32[]{:S(2)}) collective-permute-start(f32[64,640]{1,0:T(8,128)S(1)} %slice_add_fusion.1), channel_id=1, source_target_pairs={{0,2},{1,3},{2,0},{3,1},{4,6},{5,7},{6,4},{7,5},{8,10},{9,11},{10,... | collective-permute-start | bytes 491528 | tf_op jit(solution)/shard_map/ppermute | solution.py:77
  9.7 1.3 %collective-permute-done.2 = f32[64,384]{1,0:T(8,128)S(1)} collective-permute-done((f32[64,384]{1,0:T(8,128)S(1)}, f32[64,384]{1,0:T(8,128)S(1)}, u32[]{:S(2)}, u32[]{:S(2)}) %collective-permute-start.2) | collective-permute-done | bytes 98336 | tf_op jit(solution)/shard_map/ppermute | solution.py:77
  11.1 1.8 %collective-permute-start.12 = (f32[64,256]{1,0:T(8,128)S(1)}, f32[64,256]{1,0:T(8,128)S(1)}, u32[]{:S(2)}, u32[]{:S(2)}) collective-permute-start(f32[64,256]{1,0:T(8,128)S(1)} %constant_dynamic-update-slice_fusion), channel_id=1, source_target_pairs={{0,2},{1,3},{2,0},{3,1},{4,6},{5,7},{6,4},{7,5},{8,10},{9,11},{10,... | collective-permute-start | bytes 196616 | tf_op jit(solution)/shard_map/ppermute | solution.py:77
  13.0 0.3 collective-permute-start.3
  13.3 0.0 collective-permute-done.4
  13.3 1.8 %collective-permute-start.5 = (f32[96,512]{1,0:T(8,128)S(1)}, f32[96,512]{1,0:T(8,128)S(1)}, u32[]{:S(2)}, u32[]{:S(2)}) collective-permute-start(f32[96,512]{1,0:T(8,128)S(1)} %slice.63.refs_0_), channel_id=1, source_target_pairs={{0,2},{1,3},{2,0},{3,1},{4,6},{5,7},{6,4},{7,5},{8,10},{9,11},{10,... | collective-permute-start | bytes 589832 | tf_op jit(solution)/shard_map/ppermute | solution.py:77
  15.2 1.1 %collective-permute-done.12 = f32[64,256]{1,0:T(8,128)S(1)} collective-permute-done((f32[64,256]{1,0:T(8,128)S(1)}, f32[64,256]{1,0:T(8,128)S(1)}, u32[]{:S(2)}, u32[]{:S(2)}) %collective-permute-start.12) | collective-permute-done | bytes 65568 | tf_op jit(solution)/shard_map/ppermute | solution.py:77
  16.3 0.0 collective-permute-done.7
  16.3 0.1 collective-permute-start.8
  16.4 0.5 %collective-permute-start.13 = (f32[64,128]{1,0:T(8,128)S(1)}, f32[64,128]{1,0:T(8,128)S(1)}, u32[]{:S(2)}, u32[]{:S(2)}) collective-permute-start(f32[64,128]{1,0:T(8,128)S(1)} %get-tuple-element.76.own_ref), channel_id=1, source_target_pairs={{0,1},{1,0},{2,3},{3,2},{4,5},{5,4},{6,7},{7,6},{8,9},{9,8},{10,11... | collective-permute-start | bytes 98312 | tf_op jit(solution)/shard_map/ppermute | solution.py:77
  16.9 1.6 %collective-permute-start.9 = (f32[32,512]{1,0:T(8,128)S(1)}, f32[32,512]{1,0:T(8,128)S(1)}, u32[]{:S(2)}, u32[]{:S(2)}) collective-permute-start(f32[32,512]{1,0:T(8,128)S(1)} %slice.64.refs_0_), channel_id=1, source_target_pairs={{0,2},{1,3},{2,0},{3,1},{4,6},{5,7},{6,4},{7,5},{8,10},{9,11},{10,... | collective-permute-start | bytes 196616 | tf_op jit(solution)/shard_map/ppermute | solution.py:77
  18.5 0.0 collective-permute-done.13.other_ref
  18.5 0.2 shard_map.72
  18.8 0.0 collective-permute-done.8.other_ref
  18.8 0.4 shard_map.67
  19.2 4.7 %collective-permute-done.5.refs_1_ = f32[96,512]{1,0:T(8,128)S(1)} collective-permute-done((f32[96,512]{1,0:T(8,128)S(1)}, f32[96,512]{1,0:T(8,128)S(1)}, u32[]{:S(2)}, u32[]{:S(2)}) %collective-permute-start.5) | collective-permute-done | bytes 196640 | tf_op jit(solution)/shard_map/ppermute | solution.py:77
  23.9 0.4 shard_map.68
  24.3 1.3 %collective-permute-start.11 = (f32[96,256]{1,0:T(8,128)S(1)}, f32[96,256]{1,0:T(8,128)S(1)}, u32[]{:S(2)}, u32[]{:S(2)}) collective-permute-start(f32[96,256]{1,0:T(8,128)S(1)} %get-tuple-element.61.refs_0_), channel_id=1, source_target_pairs={{0,4},{4,0},{8,12},{12,8},{16,20},{20,16},{24,28},{28,24},{1,5},{5... | collective-permute-start | bytes 294920 | tf_op jit(solution)/shard_map/ppermute | solution.py:77
  25.6 0.0 collective-permute-done.3
  25.6 0.0 collective-permute-done.9.refs_1_
  25.6 0.3 shard_map.69
  25.9 0.8 %collective-permute-start.16 = (f32[32,256]{1,0:T(8,128)S(1)}, f32[32,256]{1,0:T(8,128)S(1)}, u32[]{:S(2)}, u32[]{:S(2)}) collective-permute-start(f32[32,256]{1,0:T(8,128)S(1)} %get-tuple-element.70.refs_0_), channel_id=1, source_target_pairs={{0,4},{4,0},{8,12},{12,8},{16,20},{20,16},{24,28},{28,24},{1,5},{5... | collective-permute-start | bytes 98312 | tf_op jit(solution)/shard_map/ppermute | solution.py:77
  26.7 2.2 %collective-permute-done.11.refs_1_ = f32[96,256]{1,0:T(8,128)S(1)} collective-permute-done((f32[96,256]{1,0:T(8,128)S(1)}, f32[96,256]{1,0:T(8,128)S(1)}, u32[]{:S(2)}, u32[]{:S(2)}) %collective-permute-start.11) | collective-permute-done | bytes 98336 | tf_op jit(solution)/shard_map/ppermute | solution.py:77
  28.9 0.1 shard_map.73
  29.1 1.6 %collective-permute-start.14 = (f32[160,128]{1,0:T(8,128)S(1)}, f32[160,128]{1,0:T(8,128)S(1)}, u32[]{:S(2)}, u32[]{:S(2)}) collective-permute-start(f32[160,128]{1,0:T(8,128)S(1)} %pad_maximum_fusion.3), channel_id=1, source_target_pairs={{0,8},{4,12},{8,0},{12,4},{16,24},{20,28},{24,16},{28,20},{1,9},{5... | collective-permute-start | bytes 245768 | tf_op jit(solution)/shard_map/ppermute | solution.py:77
  30.8 0.1 collective-permute-start.10
  30.9 0.0 collective-permute-done.16.refs_1_
  30.9 0.1 shard_map.75
  31.0 0.6 %collective-permute-start.17 = (f32[32,128]{1,0:T(8,128)S(1)}, f32[32,128]{1,0:T(8,128)S(1)}, u32[]{:S(2)}, u32[]{:S(2)}) collective-permute-start(f32[32,128]{1,0:T(8,128)S(1)} %get-tuple-element.72), channel_id=1, source_target_pairs={{0,8},{4,12},{8,0},{12,4},{16,24},{20,28},{24,16},{28,20},{1,9},{5... | collective-permute-start | bytes 49160 | tf_op jit(solution)/shard_map/ppermute | solution.py:77
  31.6 1.2 %shard_map.71 = (bf16[512,256]{1,0:T(8,128)(2,1)S(1)}, bf16[512,256]{1,0:T(8,128)(2,1)S(1)}) custom-call(bf16[128,384]{1,0:T(8,128)(2,1)S(1)} %get-tuple-element.49.refs_2_.refs_0_, bf16[128,384]{1,0:T(8,128)(2,1)S(1)} %get-tuple-element.50.refs_3_.refs_1_, bf16[128,256]{1,0:T(8,128)(2,1)S(1)} %get-tuple-element.51.refs_4_.refs_2_, ...), custom_call_target="tpu_custom_call" | custom-call | flops 402653184 | bytes 1376256 | tf_op jit(solution)/shard_map/pallas_call | solution.py:56
  32.8 1.9 %collective-permute-done.17 = f32[32,128]{1,0:T(8,128)S(1)} collective-permute-done((f32[32,128]{1,0:T(8,128)S(1)}, f32[32,128]{1,0:T(8,128)S(1)}, u32[]{:S(2)}, u32[]{:S(2)}) %collective-permute-start.17) | collective-permute-done | bytes 16416 | tf_op jit(solution)/shard_map/ppermute | solution.py:77
  34.8 0.0 collective-permute-done.14
  34.8 0.1 collective-permute-start.15
  34.9 0.5 %collective-permute-start.18 = (f32[64,128]{1,0:T(8,128)S(1)}, f32[64,128]{1,0:T(8,128)S(1)}, u32[]{:S(2)}, u32[]{:S(2)}) collective-permute-start(f32[64,128]{1,0:T(8,128)S(1)} %pad_maximum_fusion.4.refs_4_), channel_id=1, source_target_pairs={{0,1},{1,0},{2,3},{3,2},{4,5},{5,4},{6,7},{7,6},{8,9},{9,8},{10,11... | collective-permute-start | bytes 98312 | tf_op jit(solution)/shard_map/ppermute | solution.py:77
  35.4 0.0 collective-permute-done.10.other_ref
  35.4 1.4 %shard_map.70.base_ref = f32[512,256]{1,0:T(8,128)S(1)} custom-call(f32[4,128]{1,0:T(4,128)S(1)} %get-tuple-element.39.scale_ref, f32[512,256]{1,0:T(8,128)S(1)} %get-tuple-element.40.queries_ref, f32[576,128]{1,0:T(8,128)S(1)} %pad_maximum_fusion.own_ref, f32[576,128]{1,0:T(8,128)S(1)} %collective-permute-done.10.other_ref, ...), custom_call_target="tpu_custom_call" | custom-call | flops 301989888 | bytes 3016704 | tf_op jit(solution)/shard_map/pallas_call | solution.py:56
  36.8 0.0 collective-permute-done.15.other_found_ref.refs_3_
  36.8 0.5 %shard_map.74 = (bf16[128,256]{1,0:T(8,128)(2,1)S(1)}, bf16[128,256]{1,0:T(8,128)(2,1)S(1)}) custom-call(f32[576,128]{1,0:T(8,128)S(1)} %pad_maximum_fusion.own_ref, f32[576,128]{1,0:T(8,128)S(1)} %collective-permute-done.10.other_ref, f32[256,128]{1,0:T(8,128)S(1)} %pad_maximum_fusion.2.own_found_ref.refs_2_, ...), custom_call_target="tpu_custom_call" | custom-call | flops 50331648 | bytes 1114112 | tf_op jit(solution)/shard_map/pallas_call | solution.py:56
  37.3 0.0 collective-permute-done.18.refs_5_
  37.3 1.7 %shard_map.76 = f32[512,256]{1,0:T(8,128)} custom-call(f32[512,256]{1,0:T(8,128)S(1)} %shard_map.70.base_ref, bf16[512,256]{1,0:T(8,128)(2,1)S(1)} %get-tuple-element.59.high_ref, bf16[512,256]{1,0:T(8,128)(2,1)S(1)} %get-tuple-element.60.low_ref, bf16[128,256]{1,0:T(8,128)(2,1)S(1)} %get-tuple-element.68.refs_0_, ...), custom_call_target="tpu_custom_call" | custom-call | flops 201326592 | bytes 1572864 | tf_op jit(solution)/shard_map/pallas_call | solution.py:56
  (25 shorter events, 0.3 us)
Async XLA Ops:
  2.9 2.1 %collective-permute-start.1 = (f32[64,384]{1,0:T(8,128)S(1)}, f32[64,384]{1,0:T(8,128)S(1)}, u32[]{:S(2)}, u32[]{:S(2)}) collective-permute-start(f32[64,384]{1,0:T(8,128)S(1)} %slice.48), channel_id=1, source_target_pairs={{0,1},{1,0},{2,3},{3,2},{4,5},{5,4},{6,7},{7,6},{8,9},{9,8},{10,11... | collective-permute-start | bytes 294920 | tf_op jit(solution)/shard_map/ppermute | solution.py:77
  3.5 4.6 %collective-permute-start.6 = (f32[64,640]{1,0:T(8,128)S(1)}, f32[64,640]{1,0:T(8,128)S(1)}, u32[]{:S(2)}, u32[]{:S(2)}) collective-permute-start(f32[64,640]{1,0:T(8,128)S(1)} %slice.56), channel_id=1, source_target_pairs={{0,1},{1,0},{2,3},{3,2},{4,5},{5,4},{6,7},{7,6},{8,9},{9,8},{10,11... | collective-permute-start | bytes 491528 | tf_op jit(solution)/shard_map/ppermute | solution.py:77
  4.3 3.7 %collective-permute-start = (f32[256,128]{1,0:T(8,128)S(1)}, f32[256,128]{1,0:T(8,128)S(1)}, u32[]{:S(2)}, u32[]{:S(2)}) collective-permute-start(f32[256,128]{1,0:T(8,128)S(1)} %slice.46), channel_id=1, source_target_pairs={{0,1},{1,0},{2,3},{3,2},{4,5},{5,4},{6,7},{7,6},{8,9},{9,8},{10,11... | collective-permute-start | bytes 393224 | tf_op jit(solution)/shard_map/ppermute | solution.py:77
  4.9 8.4 %collective-permute-start.4 = (f32[128,512]{1,0:T(8,128)S(1)}, f32[128,512]{1,0:T(8,128)S(1)}, u32[]{:S(2)}, u32[]{:S(2)}) collective-permute-start(f32[128,512]{1,0:T(8,128)S(1)} %slice.53), channel_id=1, source_target_pairs={{0,1},{1,0},{2,3},{3,2},{4,5},{5,4},{6,7},{7,6},{8,9},{9,8},{10,11... | collective-permute-start | bytes 786440 | tf_op jit(solution)/shard_map/ppermute | solution.py:77
  5.0 6.0 %collective-permute-start.2 = (f32[64,384]{1,0:T(8,128)S(1)}, f32[64,384]{1,0:T(8,128)S(1)}, u32[]{:S(2)}, u32[]{:S(2)}) collective-permute-start(f32[64,384]{1,0:T(8,128)S(1)} %slice_add_fusion.3), channel_id=1, source_target_pairs={{0,4},{4,0},{8,12},{12,8},{16,20},{20,16},{24,28},{28,24},{1,5},{5... | collective-permute-start | bytes 294920 | tf_op jit(solution)/shard_map/ppermute | solution.py:77
  8.1 8.2 %collective-permute-start.7 = (f32[64,640]{1,0:T(8,128)S(1)}, f32[64,640]{1,0:T(8,128)S(1)}, u32[]{:S(2)}, u32[]{:S(2)}) collective-permute-start(f32[64,640]{1,0:T(8,128)S(1)} %slice_add_fusion.1), channel_id=1, source_target_pairs={{0,2},{1,3},{2,0},{3,1},{4,6},{5,7},{6,4},{7,5},{8,10},{9,11},{10,... | collective-permute-start | bytes 491528 | tf_op jit(solution)/shard_map/ppermute | solution.py:77
  11.1 5.2 %collective-permute-start.12 = (f32[64,256]{1,0:T(8,128)S(1)}, f32[64,256]{1,0:T(8,128)S(1)}, u32[]{:S(2)}, u32[]{:S(2)}) collective-permute-start(f32[64,256]{1,0:T(8,128)S(1)} %constant_dynamic-update-slice_fusion), channel_id=1, source_target_pairs={{0,2},{1,3},{2,0},{3,1},{4,6},{5,7},{6,4},{7,5},{8,10},{9,11},{10,... | collective-permute-start | bytes 196616 | tf_op jit(solution)/shard_map/ppermute | solution.py:77
  13.0 12.6 %collective-permute-start.3 = (f32[320,128]{1,0:T(8,128)S(1)}, f32[320,128]{1,0:T(8,128)S(1)}, u32[]{:S(2)}, u32[]{:S(2)}) collective-permute-start(f32[320,128]{1,0:T(8,128)S(1)} %pad_maximum_fusion.1), channel_id=1, source_target_pairs={{0,2},{1,3},{2,0},{3,1},{4,6},{5,7},{6,4},{7,5},{8,10},{9,11},{10,... | collective-permute-start | bytes 491528 | tf_op jit(solution)/shard_map/ppermute | solution.py:77
  13.3 10.5 %collective-permute-start.5 = (f32[96,512]{1,0:T(8,128)S(1)}, f32[96,512]{1,0:T(8,128)S(1)}, u32[]{:S(2)}, u32[]{:S(2)}) collective-permute-start(f32[96,512]{1,0:T(8,128)S(1)} %slice.63.refs_0_), channel_id=1, source_target_pairs={{0,2},{1,3},{2,0},{3,1},{4,6},{5,7},{6,4},{7,5},{8,10},{9,11},{10,... | collective-permute-start | bytes 589832 | tf_op jit(solution)/shard_map/ppermute | solution.py:77
  16.3 2.5 %collective-permute-start.8 = (f32[64,640]{1,0:T(8,128)S(1)}, f32[64,640]{1,0:T(8,128)S(1)}, u32[]{:S(2)}, u32[]{:S(2)}) collective-permute-start(f32[64,640]{1,0:T(8,128)S(1)} %add.36.own_ref), channel_id=1, source_target_pairs={{0,1},{1,0},{2,3},{3,2},{4,5},{5,4},{6,7},{7,6},{8,9},{9,8},{10,11... | collective-permute-start | bytes 491528 | tf_op jit(solution)/shard_map/ppermute | solution.py:77
  16.4 2.1 %collective-permute-start.13 = (f32[64,128]{1,0:T(8,128)S(1)}, f32[64,128]{1,0:T(8,128)S(1)}, u32[]{:S(2)}, u32[]{:S(2)}) collective-permute-start(f32[64,128]{1,0:T(8,128)S(1)} %get-tuple-element.76.own_ref), channel_id=1, source_target_pairs={{0,1},{1,0},{2,3},{3,2},{4,5},{5,4},{6,7},{7,6},{8,9},{9,8},{10,11... | collective-permute-start | bytes 98312 | tf_op jit(solution)/shard_map/ppermute | solution.py:77
  16.9 8.7 %collective-permute-start.9 = (f32[32,512]{1,0:T(8,128)S(1)}, f32[32,512]{1,0:T(8,128)S(1)}, u32[]{:S(2)}, u32[]{:S(2)}) collective-permute-start(f32[32,512]{1,0:T(8,128)S(1)} %slice.64.refs_0_), channel_id=1, source_target_pairs={{0,2},{1,3},{2,0},{3,1},{4,6},{5,7},{6,4},{7,5},{8,10},{9,11},{10,... | collective-permute-start | bytes 196616 | tf_op jit(solution)/shard_map/ppermute | solution.py:77
  24.3 4.7 %collective-permute-start.11 = (f32[96,256]{1,0:T(8,128)S(1)}, f32[96,256]{1,0:T(8,128)S(1)}, u32[]{:S(2)}, u32[]{:S(2)}) collective-permute-start(f32[96,256]{1,0:T(8,128)S(1)} %get-tuple-element.61.refs_0_), channel_id=1, source_target_pairs={{0,4},{4,0},{8,12},{12,8},{16,20},{20,16},{24,28},{28,24},{1,5},{5... | collective-permute-start | bytes 294920 | tf_op jit(solution)/shard_map/ppermute | solution.py:77
  25.9 4.9 %collective-permute-start.16 = (f32[32,256]{1,0:T(8,128)S(1)}, f32[32,256]{1,0:T(8,128)S(1)}, u32[]{:S(2)}, u32[]{:S(2)}) collective-permute-start(f32[32,256]{1,0:T(8,128)S(1)} %get-tuple-element.70.refs_0_), channel_id=1, source_target_pairs={{0,4},{4,0},{8,12},{12,8},{16,20},{20,16},{24,28},{28,24},{1,5},{5... | collective-permute-start | bytes 98312 | tf_op jit(solution)/shard_map/ppermute | solution.py:77
  29.1 5.7 %collective-permute-start.14 = (f32[160,128]{1,0:T(8,128)S(1)}, f32[160,128]{1,0:T(8,128)S(1)}, u32[]{:S(2)}, u32[]{:S(2)}) collective-permute-start(f32[160,128]{1,0:T(8,128)S(1)} %pad_maximum_fusion.3), channel_id=1, source_target_pairs={{0,8},{4,12},{8,0},{12,4},{16,24},{20,28},{24,16},{28,20},{1,9},{5... | collective-permute-start | bytes 245768 | tf_op jit(solution)/shard_map/ppermute | solution.py:77
  30.8 4.6 %collective-permute-start.10 = (f32[576,128]{1,0:T(8,128)S(1)}, f32[576,128]{1,0:T(8,128)S(1)}, u32[]{:S(2)}, u32[]{:S(2)}) collective-permute-start(f32[576,128]{1,0:T(8,128)S(1)} %pad_maximum_fusion.own_ref), channel_id=1, source_target_pairs={{0,1},{1,0},{2,3},{3,2},{4,5},{5,4},{6,7},{7,6},{8,9},{9,8},{10,11... | collective-permute-start | bytes 884744 | tf_op jit(solution)/shard_map/ppermute | solution.py:77
  31.0 3.8 %collective-permute-start.17 = (f32[32,128]{1,0:T(8,128)S(1)}, f32[32,128]{1,0:T(8,128)S(1)}, u32[]{:S(2)}, u32[]{:S(2)}) collective-permute-start(f32[32,128]{1,0:T(8,128)S(1)} %get-tuple-element.72), channel_id=1, source_target_pairs={{0,8},{4,12},{8,0},{12,4},{16,24},{20,28},{24,16},{28,20},{1,9},{5... | collective-permute-start | bytes 49160 | tf_op jit(solution)/shard_map/ppermute | solution.py:77
  34.8 2.0 %collective-permute-start.15 = (f32[256,128]{1,0:T(8,128)S(1)}, f32[256,128]{1,0:T(8,128)S(1)}, u32[]{:S(2)}, u32[]{:S(2)}) collective-permute-start(f32[256,128]{1,0:T(8,128)S(1)} %pad_maximum_fusion.2.own_found_ref.refs_2_), channel_id=1, source_target_pairs={{0,1},{1,0},{2,3},{3,2},{4,5},{5,4},{6,7},{7,6},{8,9},{9,8},{10,11... | collective-permute-start | bytes 393224 | tf_op jit(solution)/shard_map/ppermute | solution.py:77
  34.9 2.4 %collective-permute-start.18 = (f32[64,128]{1,0:T(8,128)S(1)}, f32[64,128]{1,0:T(8,128)S(1)}, u32[]{:S(2)}, u32[]{:S(2)}) collective-permute-start(f32[64,128]{1,0:T(8,128)S(1)} %pad_maximum_fusion.4.refs_4_), channel_id=1, source_target_pairs={{0,1},{1,0},{2,3},{3,2},{4,5},{5,4},{6,7},{7,6},{8,9},{9,8},{10,11... | collective-permute-start | bytes 98312 | tf_op jit(solution)/shard_map/ppermute | solution.py:77

commit v7 on v6

--- a/solution.py
+++ b/solution.py
@@ -108,7 +108,7 @@
     leaf_bits = range(1, sub.bit_length() - 1)
     mine = columns // 2
     half = rank // 2
-    sizes = (3 * mine // 4, mine // 4)
+    sizes = (5 * mine // 8, 3 * mine // 8)
     batches = len(sizes)
     offsets = [sum(sizes[:b]) for b in range(batches)]
     small = 2 * 3 * rank**3
@@ -137,10 +137,12 @@
         for e in range(1, count):
             targets.append((core_hbm.at[2 ** heights[e] - 2 + place // widths[e]], core_ref.at[e]))
         copies = [pltpu.make_async_copy(a, b, sems.at[i]) for i, (a, b) in enumerate(targets)]
-        for copy in copies:
+        for copy in copies[: 2 + levels]:
             copy.start()
         for copy in copies[: 2 + levels]:
             copy.wait()
+        for copy in copies[2 + levels :]:
+            copy.start()
         vectors = [column_scale(scale_ref[...]) * leaf_ref[...]]
         vectors += [level_ref[levels - e] for e in range(1, count)]
         store_blocks(out_ref, vectors, range(head))
@@ -346,7 +348,7 @@
     )
 
     def gain_body(own_ref, other_ref, own_found_ref, other_found_ref, core_ref, *refs):
-        out_refs, gram_ref = refs[:2], refs[2]
+        factor_refs, out_refs, gram_ref = paired(refs[:-3]), refs[-3:-1], refs[-1]
         side = core_side()
         sources = ((own_ref, own_found_ref, side), (other_ref, other_found_ref, 1 - side))
         for late_ref, found_ref, place in sources:
@@ -355,19 +357,25 @@
                 start = columns // 2 + e * half
                 where = slice((e - head) * rank, (e - head + 1) * rank)
                 gram_ref[at(place, half), where] = late_ref[start : start + half]
-        gains = []
-        for e in range(head, count):
+        gains = None
+        for e in reversed(range(head, count)):
             core = core_ref[e]
             gram = gram_ref[:, (e - head) * rank : (e - head + 1) * rank]
-            gains.append(core + core.T - dot(dot(core.T, gram), core))
-        store(out_refs, lanes(gains))
+            row = core + core.T - dot(dot(core.T, gram), core)
+            if gains is not None:
+                row = lanes([row, -dot_parts([ref[...] for ref in factor_refs[e - head]], halves(gains))])
+                gains = lanes([jnp.zeros((gains.shape[0], rank), FLOAT), gains])
+                row = jnp.concatenate([row, gains], axis=0)
+            gains = row
+        store(out_refs, gains)
 
     gains = call(
         gain_body,
-        pair(rank, coarse * rank),
+        pair(coarse * rank, coarse * rank),
         *late_parts,
         *found_parts[0],
         cores,
+        *flat(factors[head:]),
         flops=small * 2 * coarse,
         scratch=[pltpu.VMEM((rank, coarse * rank), FLOAT)],
     )
@@ -412,17 +420,10 @@
     )
 
     def last_body(base_ref, high_ref, low_ref, *refs):
-        gain_refs, (out_ref, stack_ref) = refs[:2], refs[-2:]
-        part_refs, factor_refs = paired(refs[2 : 2 + 2 * batches]), paired(refs[2 + 2 * batches : -2])
+        gain_refs, part_refs, (out_ref, stack_ref) = refs[:2], paired(refs[2:-2]), refs[-2:]
         scatter(part_refs, coarse, stack_ref)
-        found = []
-        for e in reversed(range(coarse)):
-            where = slice(e * rank, (e + 1) * rank)
-            value = dot_parts(halves(stack_ref[:, where]), [ref[:, where] for ref in gain_refs], 1)
-            if found:
-                value = value - dot_parts(halves(lanes(found)), [ref[...] for ref in factor_refs[e]], 1)
-            found.insert(0, value)
-        out_ref[...] = base_ref[...] - dot_parts([high_ref[...], low_ref[...]], halves(lanes(found)), 1)
+        found = dot_parts(halves(stack_ref[...]), [ref[...] for ref in gain_refs], 1)
+        out_ref[...] = base_ref[...] - dot_parts([high_ref[...], low_ref[...]], halves(found), 1)
 
     (out,) = call(
         last_body,
@@ -431,7 +432,6 @@
         *answer,
         *gains,
         *flat(found_parts),
-        *flat(factors[head:]),
         flops=small * 2 * coarse * rows_here // rank,
         scratch=[pltpu.VMEM((columns, coarse * rank), FLOAT)],
     )

time: 39.1 us -> 40.3 us (1.031)
  Pallas kernels: 9.97 us -> 10.7 us
    pallas_call x13, Pallas kernels: 9.97 us -> 10.7 us  [call(): pl.pallas_call(body, out_shape=outs, in_specs=[pl.BlockSpec(memory_space=...]
    ppermute x19, starting transfers between devices: 17.1 us -> 17.5 us  [swap(): lax.ppermute(array, axis, [(i, i ^ 1 << bit) for i in range(lax.axis_size...]
  transfers between devices with their start and end apart: 19 -> 19, of which waited for: 5 -> 8; matrix products, arithmetic and copies ran while one was open for 1% -> 1% of each run, Pallas kernels for 14% -> 14%
where the time goes in v7:
time: 40.3 us; the launch traced here: 40.2 us
  starting transfers between devices  17.5 us (43%)
  waiting for transfers between devices  11.3 us (28%)
  Pallas kernels  10.7 us (27%)
    ppermute x19, starting transfers between devices, swap(): lax.ppermute(array, axis, [(i, i ^ 1 << bit) for i in range(lax.axis_size...  17.5 us
    ppermute x19, waiting for transfers between devices, swap(): lax.ppermute(array, axis, [(i, i ^ 1 << bit) for i in range(lax.axis_size...  11.3 us
    pallas_call x13, Pallas kernels, call(): pl.pallas_call(body, out_shape=outs, in_specs=[pl.BlockSpec(memory_space=...  10.7 us
  transfers between devices with their start and end apart: 19, of which 8 were waited for; matrix products, arithmetic and copies ran while one was open for 1% of the time, Pallas kernels for 14%

profile of v7, /device:TPU:0, one launch (start us, length us, event | category | flops | bytes accessed | tf_op | source)
XLA Modules:
  0.0 40.2 jit_solution(11996828003672947426)
XLA Ops:
  0.0 2.6 %shard_map.64 = (f32[128,640]{1,0:T(8,128)S(1)}, f32[4,128]{1,0:T(4,128)S(1)}, f32[512,128]{1,0:T(8,128)S(1)}, f32[3,512,128]{2,1,0:T(8,128)S(1)}, f32[512,256]{1,0:T(8,128)S(1)}, /*index=5*/f32[4,128,128]{2,1,0:T(8,128)S(1)}) custom-call(f32[4,128]{1,0:T(4,128)} %bitcast.1, f32[512,128]{1,0:T(8,128)} %refs_1_.1, f32[3,512,128]{2,1,0:T(8,128)} %refs_2_.1, ...), custom_call_target="tpu_custom_call" | custom-call | flops 251658240 | bytes 2557952 | tf_op jit(solution)/shard_map/pallas_call | solution.py:56
  2.6 1.0 %shard_map.66 = (f32[128,384]{1,0:T(8,128)S(1)}, f32[256,512]{1,0:T(8,128)S(1)}, bf16[512,512]{1,0:T(8,128)(2,1)S(1)}, bf16[512,512]{1,0:T(8,128)(2,1)S(1)}) custom-call(f32[4,128]{1,0:T(4,128)S(1)} %get-tuple-element.39.scale_ref, f32[512,256]{1,0:T(8,128)S(1)} %get-tuple-element.40.queries_ref, f32[512,128]{1,0:T(8,128)S(1)} %get-tuple-element.41.leaf_ref, ...), custom_call_target="tpu_custom_call" | custom-call | flops 402653184 | bytes 1574912 | tf_op jit(solution)/shard_map/pallas_call | solution.py:56
  3.6 0.6 %collective-permute-start.1 = (f32[64,384]{1,0:T(8,128)S(1)}, f32[64,384]{1,0:T(8,128)S(1)}, u32[]{:S(2)}, u32[]{:S(2)}) collective-permute-start(f32[64,384]{1,0:T(8,128)S(1)} %slice.48), channel_id=1, source_target_pairs={{0,1},{1,0},{2,3},{3,2},{4,5},{5,4},{6,7},{7,6},{8,9},{9,8},{10,11... | collective-permute-start | bytes 294920 | tf_op jit(solution)/shard_map/ppermute | solution.py:77
  4.1 0.1 collective-permute-start.6
  4.2 0.7 %shard_map.65 = (f32[512,128]{1,0:T(8,128)S(1)}, bf16[512,128]{1,0:T(8,128)(2,1)S(1)}, bf16[512,128]{1,0:T(8,128)(2,1)S(1)}) custom-call(f32[4,128]{1,0:T(4,128)S(1)} %get-tuple-element.39.scale_ref, f32[512,256]{1,0:T(8,128)S(1)} %get-tuple-element.40.queries_ref, f32[512,128]{1,0:T(8,128)S(1)} %get-tuple-element.41.leaf_ref, ...), custom_call_target="tpu_custom_call" | custom-call | flops 201326592 | bytes 1574912 | tf_op jit(solution)/shard_map/pallas_call | solution.py:56
  5.0 0.6 %collective-permute-start = (f32[256,128]{1,0:T(8,128)S(1)}, f32[256,128]{1,0:T(8,128)S(1)}, u32[]{:S(2)}, u32[]{:S(2)}) collective-permute-start(f32[256,128]{1,0:T(8,128)S(1)} %slice.46), channel_id=1, source_target_pairs={{0,1},{1,0},{2,3},{3,2},{4,5},{5,4},{6,7},{7,6},{8,9},{9,8},{10,11... | collective-permute-start | bytes 393224 | tf_op jit(solution)/shard_map/ppermute | solution.py:77
  5.6 0.1 collective-permute-start.4
  5.7 0.0 collective-permute-done.1
  5.7 3.0 %collective-permute-start.2 = (f32[64,384]{1,0:T(8,128)S(1)}, f32[64,384]{1,0:T(8,128)S(1)}, u32[]{:S(2)}, u32[]{:S(2)}) collective-permute-start(f32[64,384]{1,0:T(8,128)S(1)} %slice_add_fusion.3), channel_id=1, source_target_pairs={{0,4},{4,0},{8,12},{12,8},{16,20},{20,16},{24,28},{28,24},{1,5},{5... | collective-permute-start | bytes 294920 | tf_op jit(solution)/shard_map/ppermute | solution.py:77
  8.7 0.0 collective-permute-done
  8.7 0.0 collective-permute-done.6
  8.8 1.6 %collective-permute-start.7 = (f32[64,640]{1,0:T(8,128)S(1)}, f32[64,640]{1,0:T(8,128)S(1)}, u32[]{:S(2)}, u32[]{:S(2)}) collective-permute-start(f32[64,640]{1,0:T(8,128)S(1)} %slice_add_fusion.1), channel_id=1, source_target_pairs={{0,2},{1,3},{2,0},{3,1},{4,6},{5,7},{6,4},{7,5},{8,10},{9,11},{10,... | collective-permute-start | bytes 491528 | tf_op jit(solution)/shard_map/ppermute | solution.py:77
  10.4 1.3 %collective-permute-done.2 = f32[64,384]{1,0:T(8,128)S(1)} collective-permute-done((f32[64,384]{1,0:T(8,128)S(1)}, f32[64,384]{1,0:T(8,128)S(1)}, u32[]{:S(2)}, u32[]{:S(2)}) %collective-permute-start.2) | collective-permute-done | bytes 98336 | tf_op jit(solution)/shard_map/ppermute | solution.py:77
  11.8 1.8 %collective-permute-start.12 = (f32[64,256]{1,0:T(8,128)S(1)}, f32[64,256]{1,0:T(8,128)S(1)}, u32[]{:S(2)}, u32[]{:S(2)}) collective-permute-start(f32[64,256]{1,0:T(8,128)S(1)} %constant_dynamic-update-slice_fusion), channel_id=1, source_target_pairs={{0,2},{1,3},{2,0},{3,1},{4,6},{5,7},{6,4},{7,5},{8,10},{9,11},{10,... | collective-permute-start | bytes 196616 | tf_op jit(solution)/shard_map/ppermute | solution.py:77
  13.6 0.3 collective-permute-start.3
  13.9 0.0 collective-permute-done.4
  14.0 1.8 %collective-permute-start.9 = (f32[48,512]{1,0:T(8,128)S(1)}, f32[48,512]{1,0:T(8,128)S(1)}, u32[]{:S(2)}, u32[]{:S(2)}) collective-permute-start(f32[48,512]{1,0:T(8,128)S(1)} %slice.64.refs_0_), channel_id=1, source_target_pairs={{0,2},{1,3},{2,0},{3,1},{4,6},{5,7},{6,4},{7,5},{8,10},{9,11},{10,... | collective-permute-start | bytes 294920 | tf_op jit(solution)/shard_map/ppermute | solution.py:77
  15.9 0.3 collective-permute-start.5
  16.1 0.8 %collective-permute-done.12 = f32[64,256]{1,0:T(8,128)S(1)} collective-permute-done((f32[64,256]{1,0:T(8,128)S(1)}, f32[64,256]{1,0:T(8,128)S(1)}, u32[]{:S(2)}, u32[]{:S(2)}) %collective-permute-start.12) | collective-permute-done | bytes 65568 | tf_op jit(solution)/shard_map/ppermute | solution.py:77
  16.9 0.0 collective-permute-done.7
  17.0 0.1 collective-permute-start.8
  17.1 0.5 %collective-permute-start.13 = (f32[64,128]{1,0:T(8,128)S(1)}, f32[64,128]{1,0:T(8,128)S(1)}, u32[]{:S(2)}, u32[]{:S(2)}) collective-permute-start(f32[64,128]{1,0:T(8,128)S(1)} %get-tuple-element.76.own_ref), channel_id=1, source_target_pairs={{0,1},{1,0},{2,3},{3,2},{4,5},{5,4},{6,7},{7,6},{8,9},{9,8},{10,11... | collective-permute-start | bytes 98312 | tf_op jit(solution)/shard_map/ppermute | solution.py:77
  17.6 0.9 %collective-permute-done.13.other_ref = f32[64,128]{1,0:T(8,128)S(1)} collective-permute-done((f32[64,128]{1,0:T(8,128)S(1)}, f32[64,128]{1,0:T(8,128)S(1)}, u32[]{:S(2)}, u32[]{:S(2)}) %collective-permute-start.13) | collective-permute-done | bytes 32800 | tf_op jit(solution)/shard_map/ppermute | solution.py:77
  18.5 0.2 shard_map.72
  18.7 0.0 collective-permute-done.8.other_ref
  18.7 0.4 shard_map.67
  19.1 3.7 %collective-permute-done.9.refs_1_ = f32[48,512]{1,0:T(8,128)S(1)} collective-permute-done((f32[48,512]{1,0:T(8,128)S(1)}, f32[48,512]{1,0:T(8,128)S(1)}, u32[]{:S(2)}, u32[]{:S(2)}) %collective-permute-start.9) | collective-permute-done | bytes 98336 | tf_op jit(solution)/shard_map/ppermute | solution.py:77
  22.9 0.3 shard_map.69
  23.2 1.6 %collective-permute-start.16 = (f32[48,256]{1,0:T(8,128)S(1)}, f32[48,256]{1,0:T(8,128)S(1)}, u32[]{:S(2)}, u32[]{:S(2)}) collective-permute-start(f32[48,256]{1,0:T(8,128)S(1)} %get-tuple-element.70.refs_0_), channel_id=1, source_target_pairs={{0,4},{4,0},{8,12},{12,8},{16,20},{20,16},{24,28},{28,24},{1,5},{5... | collective-permute-start | bytes 147464 | tf_op jit(solution)/shard_map/ppermute | solution.py:77
  24.7 0.5 %collective-permute-done.5.refs_1_ = f32[80,512]{1,0:T(8,128)S(1)} collective-permute-done((f32[80,512]{1,0:T(8,128)S(1)}, f32[80,512]{1,0:T(8,128)S(1)}, u32[]{:S(2)}, u32[]{:S(2)}) %collective-permute-start.5) | collective-permute-done | bytes 163872 | tf_op jit(solution)/shard_map/ppermute | solution.py:77
  25.2 0.3 shard_map.68
  25.6 1.3 %collective-permute-start.11 = (f32[80,256]{1,0:T(8,128)S(1)}, f32[80,256]{1,0:T(8,128)S(1)}, u32[]{:S(2)}, u32[]{:S(2)}) collective-permute-start(f32[80,256]{1,0:T(8,128)S(1)} %get-tuple-element.61.refs_0_), channel_id=1, source_target_pairs={{0,4},{4,0},{8,12},{12,8},{16,20},{20,16},{24,28},{28,24},{1,5},{5... | collective-permute-start | bytes 245768 | tf_op jit(solution)/shard_map/ppermute | solution.py:77
  26.9 0.0 collective-permute-done.3
  26.9 0.5 %collective-permute-done.16.refs_1_ = f32[48,256]{1,0:T(8,128)S(1)} collective-permute-done((f32[48,256]{1,0:T(8,128)S(1)}, f32[48,256]{1,0:T(8,128)S(1)}, u32[]{:S(2)}, u32[]{:S(2)}) %collective-permute-start.16) | collective-permute-done | bytes 49184 | tf_op jit(solution)/shard_map/ppermute | solution.py:77
  27.5 0.1 shard_map.75
  27.6 1.7 %collective-permute-start.17 = (f32[48,128]{1,0:T(8,128)S(1)}, f32[48,128]{1,0:T(8,128)S(1)}, u32[]{:S(2)}, u32[]{:S(2)}) collective-permute-start(f32[48,128]{1,0:T(8,128)S(1)} %get-tuple-element.72), channel_id=1, source_target_pairs={{0,8},{4,12},{8,0},{12,4},{16,24},{20,28},{24,16},{28,20},{1,9},{5... | collective-permute-start | bytes 73736 | tf_op jit(solution)/shard_map/ppermute | solution.py:77
  29.3 0.8 %collective-permute-done.11.refs_1_ = f32[80,256]{1,0:T(8,128)S(1)} collective-permute-done((f32[80,256]{1,0:T(8,128)S(1)}, f32[80,256]{1,0:T(8,128)S(1)}, u32[]{:S(2)}, u32[]{:S(2)}) %collective-permute-start.11) | collective-permute-done | bytes 81952 | tf_op jit(solution)/shard_map/ppermute | solution.py:77
  30.1 0.2 shard_map.73
  30.3 1.6 %collective-permute-start.14 = (f32[144,128]{1,0:T(8,128)S(1)}, f32[144,128]{1,0:T(8,128)S(1)}, u32[]{:S(2)}, u32[]{:S(2)}) collective-permute-start(f32[144,128]{1,0:T(8,128)S(1)} %pad_maximum_fusion.3), channel_id=1, source_target_pairs={{0,8},{4,12},{8,0},{12,4},{16,24},{20,28},{24,16},{28,20},{1,9},{5... | collective-permute-start | bytes 221192 | tf_op jit(solution)/shard_map/ppermute | solution.py:77
  32.0 0.1 collective-permute-start.10
  32.0 0.0 collective-permute-done.17
  32.1 2.6 %collective-permute-done.14 = f32[144,128]{1,0:T(8,128)S(1)} collective-permute-done((f32[144,128]{1,0:T(8,128)S(1)}, f32[144,128]{1,0:T(8,128)S(1)}, u32[]{:S(2)}, u32[]{:S(2)}) %collective-permute-start.14) | collective-permute-done | bytes 73760 | tf_op jit(solution)/shard_map/ppermute | solution.py:77
  34.7 0.1 collective-permute-start.15
  34.8 0.5 %collective-permute-start.18 = (f32[96,128]{1,0:T(8,128)S(1)}, f32[96,128]{1,0:T(8,128)S(1)}, u32[]{:S(2)}, u32[]{:S(2)}) collective-permute-start(f32[96,128]{1,0:T(8,128)S(1)} %pad_maximum_fusion.4.refs_4_), channel_id=1, source_target_pairs={{0,1},{1,0},{2,3},{3,2},{4,5},{5,4},{6,7},{7,6},{8,9},{9,8},{10,11... | collective-permute-start | bytes 147464 | tf_op jit(solution)/shard_map/ppermute | solution.py:77
  35.3 1.2 %shard_map.71 = (bf16[512,256]{1,0:T(8,128)(2,1)S(1)}, bf16[512,256]{1,0:T(8,128)(2,1)S(1)}) custom-call(bf16[128,384]{1,0:T(8,128)(2,1)S(1)} %get-tuple-element.49.refs_2_.refs_0_, bf16[128,384]{1,0:T(8,128)(2,1)S(1)} %get-tuple-element.50.refs_3_.refs_1_, bf16[128,256]{1,0:T(8,128)(2,1)S(1)} %get-tuple-element.51.refs_4_.refs_2_, ...), custom_call_target="tpu_custom_call" | custom-call | flops 402653184 | bytes 1376256 | tf_op jit(solution)/shard_map/pallas_call | solution.py:56
  36.5 0.0 collective-permute-done.15.other_found_ref.refs_3_
  36.6 0.0 collective-permute-done.10.other_ref
  36.6 0.6 %shard_map.74 = (bf16[256,256]{1,0:T(8,128)(2,1)S(1)}, bf16[256,256]{1,0:T(8,128)(2,1)S(1)}) custom-call(f32[576,128]{1,0:T(8,128)S(1)} %pad_maximum_fusion.own_ref, f32[576,128]{1,0:T(8,128)S(1)} %collective-permute-done.10.other_ref, f32[224,128]{1,0:T(8,128)S(1)} %pad_maximum_fusion.2.own_found_ref.refs_2_, ...), custom_call_target="tpu_custom_call" | custom-call | flops 50331648 | bytes 1146880 | tf_op jit(solution)/shard_map/pallas_call | solution.py:56
  37.1 1.4 %shard_map.70.base_ref = f32[512,256]{1,0:T(8,128)S(1)} custom-call(f32[4,128]{1,0:T(4,128)S(1)} %get-tuple-element.39.scale_ref, f32[512,256]{1,0:T(8,128)S(1)} %get-tuple-element.40.queries_ref, f32[576,128]{1,0:T(8,128)S(1)} %pad_maximum_fusion.own_ref, f32[576,128]{1,0:T(8,128)S(1)} %collective-permute-done.10.other_ref, ...), custom_call_target="tpu_custom_call" | custom-call | flops 301989888 | bytes 3016704 | tf_op jit(solution)/shard_map/pallas_call | solution.py:56
  38.6 0.0 collective-permute-done.18.refs_5_
  38.6 1.6 %shard_map.76 = f32[512,256]{1,0:T(8,128)} custom-call(f32[512,256]{1,0:T(8,128)S(1)} %shard_map.70.base_ref, bf16[512,256]{1,0:T(8,128)(2,1)S(1)} %get-tuple-element.59.high_ref, bf16[512,256]{1,0:T(8,128)(2,1)S(1)} %get-tuple-element.60.low_ref, bf16[256,256]{1,0:T(8,128)(2,1)S(1)} %get-tuple-element.68.refs_0_, ...), custom_call_target="tpu_custom_call" | custom-call | flops 201326592 | bytes 1638400 | tf_op jit(solution)/shard_map/pallas_call | solution.py:56
  (25 shorter events, 0.3 us)
Async XLA Ops:
  3.6 2.1 %collective-permute-start.1 = (f32[64,384]{1,0:T(8,128)S(1)}, f32[64,384]{1,0:T(8,128)S(1)}, u32[]{:S(2)}, u32[]{:S(2)}) collective-permute-start(f32[64,384]{1,0:T(8,128)S(1)} %slice.48), channel_id=1, source_target_pairs={{0,1},{1,0},{2,3},{3,2},{4,5},{5,4},{6,7},{7,6},{8,9},{9,8},{10,11... | collective-permute-start | bytes 294920 | tf_op jit(solution)/shard_map/ppermute | solution.py:77
  4.1 4.6 %collective-permute-start.6 = (f32[64,640]{1,0:T(8,128)S(1)}, f32[64,640]{1,0:T(8,128)S(1)}, u32[]{:S(2)}, u32[]{:S(2)}) collective-permute-start(f32[64,640]{1,0:T(8,128)S(1)} %slice.56), channel_id=1, source_target_pairs={{0,1},{1,0},{2,3},{3,2},{4,5},{5,4},{6,7},{7,6},{8,9},{9,8},{10,11... | collective-permute-start | bytes 491528 | tf_op jit(solution)/shard_map/ppermute | solution.py:77
  5.0 3.7 %collective-permute-start = (f32[256,128]{1,0:T(8,128)S(1)}, f32[256,128]{1,0:T(8,128)S(1)}, u32[]{:S(2)}, u32[]{:S(2)}) collective-permute-start(f32[256,128]{1,0:T(8,128)S(1)} %slice.46), channel_id=1, source_target_pairs={{0,1},{1,0},{2,3},{3,2},{4,5},{5,4},{6,7},{7,6},{8,9},{9,8},{10,11... | collective-permute-start | bytes 393224 | tf_op jit(solution)/shard_map/ppermute | solution.py:77
  5.6 8.4 %collective-permute-start.4 = (f32[128,512]{1,0:T(8,128)S(1)}, f32[128,512]{1,0:T(8,128)S(1)}, u32[]{:S(2)}, u32[]{:S(2)}) collective-permute-start(f32[128,512]{1,0:T(8,128)S(1)} %slice.53), channel_id=1, source_target_pairs={{0,1},{1,0},{2,3},{3,2},{4,5},{5,4},{6,7},{7,6},{8,9},{9,8},{10,11... | collective-permute-start | bytes 786440 | tf_op jit(solution)/shard_map/ppermute | solution.py:77
  5.7 6.0 %collective-permute-start.2 = (f32[64,384]{1,0:T(8,128)S(1)}, f32[64,384]{1,0:T(8,128)S(1)}, u32[]{:S(2)}, u32[]{:S(2)}) collective-permute-start(f32[64,384]{1,0:T(8,128)S(1)} %slice_add_fusion.3), channel_id=1, source_target_pairs={{0,4},{4,0},{8,12},{12,8},{16,20},{20,16},{24,28},{28,24},{1,5},{5... | collective-permute-start | bytes 294920 | tf_op jit(solution)/shard_map/ppermute | solution.py:77
  8.8 8.2 %collective-permute-start.7 = (f32[64,640]{1,0:T(8,128)S(1)}, f32[64,640]{1,0:T(8,128)S(1)}, u32[]{:S(2)}, u32[]{:S(2)}) collective-permute-start(f32[64,640]{1,0:T(8,128)S(1)} %slice_add_fusion.1), channel_id=1, source_target_pairs={{0,2},{1,3},{2,0},{3,1},{4,6},{5,7},{6,4},{7,5},{8,10},{9,11},{10,... | collective-permute-start | bytes 491528 | tf_op jit(solution)/shard_map/ppermute | solution.py:77
  11.8 5.2 %collective-permute-start.12 = (f32[64,256]{1,0:T(8,128)S(1)}, f32[64,256]{1,0:T(8,128)S(1)}, u32[]{:S(2)}, u32[]{:S(2)}) collective-permute-start(f32[64,256]{1,0:T(8,128)S(1)} %constant_dynamic-update-slice_fusion), channel_id=1, source_target_pairs={{0,2},{1,3},{2,0},{3,1},{4,6},{5,7},{6,4},{7,5},{8,10},{9,11},{10,... | collective-permute-start | bytes 196616 | tf_op jit(solution)/shard_map/ppermute | solution.py:77
  13.6 13.3 %collective-permute-start.3 = (f32[320,128]{1,0:T(8,128)S(1)}, f32[320,128]{1,0:T(8,128)S(1)}, u32[]{:S(2)}, u32[]{:S(2)}) collective-permute-start(f32[320,128]{1,0:T(8,128)S(1)} %pad_maximum_fusion.1), channel_id=1, source_target_pairs={{0,2},{1,3},{2,0},{3,1},{4,6},{5,7},{6,4},{7,5},{8,10},{9,11},{10,... | collective-permute-start | bytes 491528 | tf_op jit(solution)/shard_map/ppermute | solution.py:77
  14.0 8.8 %collective-permute-start.9 = (f32[48,512]{1,0:T(8,128)S(1)}, f32[48,512]{1,0:T(8,128)S(1)}, u32[]{:S(2)}, u32[]{:S(2)}) collective-permute-start(f32[48,512]{1,0:T(8,128)S(1)} %slice.64.refs_0_), channel_id=1, source_target_pairs={{0,2},{1,3},{2,0},{3,1},{4,6},{5,7},{6,4},{7,5},{8,10},{9,11},{10,... | collective-permute-start | bytes 294920 | tf_op jit(solution)/shard_map/ppermute | solution.py:77
  15.9 9.4 %collective-permute-start.5 = (f32[80,512]{1,0:T(8,128)S(1)}, f32[80,512]{1,0:T(8,128)S(1)}, u32[]{:S(2)}, u32[]{:S(2)}) collective-permute-start(f32[80,512]{1,0:T(8,128)S(1)} %slice.63.refs_0_), channel_id=1, source_target_pairs={{0,2},{1,3},{2,0},{3,1},{4,6},{5,7},{6,4},{7,5},{8,10},{9,11},{10,... | collective-permute-start | bytes 491528 | tf_op jit(solution)/shard_map/ppermute | solution.py:77
  17.0 1.8 %collective-permute-start.8 = (f32[64,640]{1,0:T(8,128)S(1)}, f32[64,640]{1,0:T(8,128)S(1)}, u32[]{:S(2)}, u32[]{:S(2)}) collective-permute-start(f32[64,640]{1,0:T(8,128)S(1)} %add.36.own_ref), channel_id=1, source_target_pairs={{0,1},{1,0},{2,3},{3,2},{4,5},{5,4},{6,7},{7,6},{8,9},{9,8},{10,11... | collective-permute-start | bytes 491528 | tf_op jit(solution)/shard_map/ppermute | solution.py:77
  17.1 1.4 %collective-permute-start.13 = (f32[64,128]{1,0:T(8,128)S(1)}, f32[64,128]{1,0:T(8,128)S(1)}, u32[]{:S(2)}, u32[]{:S(2)}) collective-permute-start(f32[64,128]{1,0:T(8,128)S(1)} %get-tuple-element.76.own_ref), channel_id=1, source_target_pairs={{0,1},{1,0},{2,3},{3,2},{4,5},{5,4},{6,7},{7,6},{8,9},{9,8},{10,11... | collective-permute-start | bytes 98312 | tf_op jit(solution)/shard_map/ppermute | solution.py:77
  23.2 4.3 %collective-permute-start.16 = (f32[48,256]{1,0:T(8,128)S(1)}, f32[48,256]{1,0:T(8,128)S(1)}, u32[]{:S(2)}, u32[]{:S(2)}) collective-permute-start(f32[48,256]{1,0:T(8,128)S(1)} %get-tuple-element.70.refs_0_), channel_id=1, source_target_pairs={{0,4},{4,0},{8,12},{12,8},{16,20},{20,16},{24,28},{28,24},{1,5},{5... | collective-permute-start | bytes 147464 | tf_op jit(solution)/shard_map/ppermute | solution.py:77
  25.6 4.5 %collective-permute-start.11 = (f32[80,256]{1,0:T(8,128)S(1)}, f32[80,256]{1,0:T(8,128)S(1)}, u32[]{:S(2)}, u32[]{:S(2)}) collective-permute-start(f32[80,256]{1,0:T(8,128)S(1)} %get-tuple-element.61.refs_0_), channel_id=1, source_target_pairs={{0,4},{4,0},{8,12},{12,8},{16,20},{20,16},{24,28},{28,24},{1,5},{5... | collective-permute-start | bytes 245768 | tf_op jit(solution)/shard_map/ppermute | solution.py:77
  27.6 4.4 %collective-permute-start.17 = (f32[48,128]{1,0:T(8,128)S(1)}, f32[48,128]{1,0:T(8,128)S(1)}, u32[]{:S(2)}, u32[]{:S(2)}) collective-permute-start(f32[48,128]{1,0:T(8,128)S(1)} %get-tuple-element.72), channel_id=1, source_target_pairs={{0,8},{4,12},{8,0},{12,4},{16,24},{20,28},{24,16},{28,20},{1,9},{5... | collective-permute-start | bytes 73736 | tf_op jit(solution)/shard_map/ppermute | solution.py:77
  30.3 4.4 %collective-permute-start.14 = (f32[144,128]{1,0:T(8,128)S(1)}, f32[144,128]{1,0:T(8,128)S(1)}, u32[]{:S(2)}, u32[]{:S(2)}) collective-permute-start(f32[144,128]{1,0:T(8,128)S(1)} %pad_maximum_fusion.3), channel_id=1, source_target_pairs={{0,8},{4,12},{8,0},{12,4},{16,24},{20,28},{24,16},{28,20},{1,9},{5... | collective-permute-start | bytes 221192 | tf_op jit(solution)/shard_map/ppermute | solution.py:77
  32.0 4.6 %collective-permute-start.10 = (f32[576,128]{1,0:T(8,128)S(1)}, f32[576,128]{1,0:T(8,128)S(1)}, u32[]{:S(2)}, u32[]{:S(2)}) collective-permute-start(f32[576,128]{1,0:T(8,128)S(1)} %pad_maximum_fusion.own_ref), channel_id=1, source_target_pairs={{0,1},{1,0},{2,3},{3,2},{4,5},{5,4},{6,7},{7,6},{8,9},{9,8},{10,11... | collective-permute-start | bytes 884744 | tf_op jit(solution)/shard_map/ppermute | solution.py:77
  34.7 1.8 %collective-permute-start.15 = (f32[224,128]{1,0:T(8,128)S(1)}, f32[224,128]{1,0:T(8,128)S(1)}, u32[]{:S(2)}, u32[]{:S(2)}) collective-permute-start(f32[224,128]{1,0:T(8,128)S(1)} %pad_maximum_fusion.2.own_found_ref.refs_2_), channel_id=1, source_target_pairs={{0,1},{1,0},{2,3},{3,2},{4,5},{5,4},{6,7},{7,6},{8,9},{9,8},{10,11... | collective-permute-start | bytes 344072 | tf_op jit(solution)/shard_map/ppermute | solution.py:77
  34.8 3.7 %collective-permute-start.18 = (f32[96,128]{1,0:T(8,128)S(1)}, f32[96,128]{1,0:T(8,128)S(1)}, u32[]{:S(2)}, u32[]{:S(2)}) collective-permute-start(f32[96,128]{1,0:T(8,128)S(1)} %pad_maximum_fusion.4.refs_4_), channel_id=1, source_target_pairs={{0,1},{1,0},{2,3},{3,2},{4,5},{5,4},{6,7},{7,6},{8,9},{9,8},{10,11... | collective-permute-start | bytes 147464 | tf_op jit(solution)/shard_map/ppermute | solution.py:77
